TPU v7x, 512 devices: a whole 4x8x8 slice. The times are simulated.
512 devices in a mesh: grp: 16 (over y, core), dev: 32 (over x, z).
Axes of the slice: x: 4, y: 8, z: 8, core: 2. Of those that a mesh axis runs over, the one named last changes fastest.
Arguments:
- pixels: bfloat16 [256, 2048, 256], P('grp', 'dev'), may hold values from -16 to 16
- offsets: float32 [256, 2048], P('grp', 'dev'), may hold values from -1 to 1
- first_weights: bfloat16 [3, 256, 256], replicated, may hold values from -0.21875 to 0.21875
- second_weights: bfloat16 [3, 256, 256], replicated, may hold values from -0.21875 to 0.21875
- cotangent: bfloat16 [128, 1024, 256], P('grp', 'dev'), may hold values from -24 to 24
Outputs:
- grad_pixels: bfloat16 [256, 2048, 256], P('grp', 'dev')
- grad_first: float32 [3, 256, 256], replicated
- grad_second: float32 [3, 256, 256], replicated
- level_out: bfloat16 [128, 1024, 256], P('grp', 'dev')
All inputs are finite; a program needn't handle non-finite values.
Results may differ from a plain program's by a relative error of at most 0.01.
Values may be sent and summed in bfloat16 or wider, within the bound.
No kernel may reach another device: no remote copies, remote signals or barrier semaphores. Data moves between devices by JAX's collectives and lax.ppermute only.
A program may use at most 64 MiB of HBM per device.

v0:
```python
import jax
import jax.numpy as jnp
from jax import lax
from jax.sharding import Mesh
from jax.sharding import PartitionSpec as P

GRP = ("grp_0", "grp_1")
DEV = ("dev_0", "dev_1")


NEIGHBOUR_STEPS = (
    (-1, 0, 1.0),
    (1, 0, 1.0),
    (0, -1, 1.0),
    (0, 1, 1.0),
    (-1, -1, 0.5),
    (-1, 1, 0.5),
    (1, -1, 0.5),
    (1, 1, 0.5),
)


def with_halo(block, sides, width):
    for axis, dim in sides:
        count = lax.axis_size(axis)
        forward = [(i, i + 1) for i in range(count - 1)]
        backward = [(target, source) for source, target in forward]
        low = lax.ppermute(
            lax.slice_in_dim(block, block.shape[dim] - width, None, axis=dim), axis, forward
        )
        high = lax.ppermute(lax.slice_in_dim(block, 0, width, axis=dim), axis, backward)
        block = jnp.concatenate([low, block, high], axis=dim)
    return block


def padded_to(lines, size):
    spare = -lines.shape[0] % size
    if not spare:
        return lines
    return jnp.concatenate([lines, jnp.zeros((spare, *lines.shape[1:]), lines.dtype)])


def sent_to_all(value, axis):
    copies = jnp.broadcast_to(value, (lax.axis_size(axis), *value.shape))
    return lax.all_to_all(copies, axis, split_axis=0, concat_axis=0, tiled=True)


def laid_out(tiles, dim):
    tiles = jnp.moveaxis(tiles, 0, dim)
    dims = tiles.shape
    return tiles.reshape(*dims[:dim], dims[dim] * dims[dim + 1], *dims[dim + 2 :])


def gathered_by_axis(value, axes, dim):
    far, near = axes
    first = sent_to_all(value, far)
    tiles = jnp.swapaxes(sent_to_all(first, near), 0, 1)
    return laid_out(tiles.reshape(-1, *value.shape), dim)


def split_up(value, dim, size):
    before, after = (value.shape[:dim], value.shape[dim + 1 :])
    return jnp.moveaxis(value.reshape(*before, size, -1, *after), dim, 0)


def sum_at_owner(value, axis, dim):
    size = lax.axis_size(axis)
    tiles = lax.all_to_all(split_up(value, dim, size), axis, 0, 0, tiled=True)
    return jnp.sum(tiles, axis=0)


def summed_rows(value, axes, dim):
    far, near = axes
    own = sum_at_owner(split_up(value, dim, lax.axis_size(far)), near, dim + 1)
    return jnp.sum(lax.all_to_all(own, far, 0, 0, tiled=True), axis=0)


def total_of(value, axes):
    padded = padded_to(value, lax.axis_size(axes[0]) * lax.axis_size(axes[1]))
    whole = gathered_by_axis(summed_rows(padded, axes, 0), axes, 0)
    return lax.slice_in_dim(whole, 0, len(value)).reshape(value.shape)


def packed_total(arrays, axis):
    ends = [0]
    for a in arrays:
        ends.append(ends[-1] + a.size)
    running = total_of(jnp.concatenate([a.ravel() for a in arrays]), axis)
    return tuple((running[b:e].reshape(a.shape) for a, b, e in zip(arrays, ends, ends[1:])))


def trim(tensor, have_ext, want_ext):
    margin_cut = have_ext - want_ext
    if margin_cut == 0:
        return tensor
    return tensor[
        margin_cut : tensor.shape[0] - margin_cut, margin_cut : tensor.shape[1] - margin_cut
    ]


def graph_parts(offsets, inside, have_ext):
    height = offsets.shape[0] - 2
    breadth = offsets.shape[1] - 2
    centre = offsets[1:-1, 1:-1]
    centre_in = inside[1:-1, 1:-1]
    weights = []
    degree = jnp.zeros(centre.shape, jnp.float32)
    for row_step, col_step, coupling in NEIGHBOUR_STEPS:
        neighbour = offsets[
            1 + row_step : 1 + row_step + height, 1 + col_step : 1 + col_step + breadth
        ]
        present = inside[
            1 + row_step : 1 + row_step + height, 1 + col_step : 1 + col_step + breadth
        ]
        weight = (
            coupling * present * jnp.exp(-(centre - neighbour) * (centre - neighbour)) * centre_in
        )
        weights.append(weight)
        degree = degree + weight
    inverse_root = lax.rsqrt(degree + 1.0 - centre_in) * centre_in
    return (weights, inverse_root, have_ext - 1)


def apply_operator(extended, extent, graph_data):
    weights, inverse_root, have_ext = graph_data
    root_ext = trim(inverse_root, have_ext, extent)
    scaled = root_ext[:, :, None] * extended.astype(jnp.float32)
    height = scaled.shape[0] - 2
    breadth = scaled.shape[1] - 2
    summed = jnp.zeros((height, breadth, scaled.shape[2]), jnp.float32)
    for (row_step, col_step, coupling), weight in zip(NEIGHBOUR_STEPS, weights):
        summed = (
            summed
            + trim(weight, have_ext, extent - 1)[:, :, None]
            * scaled[1 + row_step : 1 + row_step + height, 1 + col_step : 1 + col_step + breadth, :]
        )
    return -root_ext[1:-1, 1:-1, None] * summed


def deep_rim(values):
    return with_halo(values, ((GRP, 0), (DEV, 1)), 2)


def forward_terms(values, graph_data):
    first_wide = apply_operator(deep_rim(values), 2, graph_data).astype(jnp.bfloat16)
    second = (2.0 * apply_operator(first_wide, 1, graph_data) - values.astype(jnp.float32)).astype(
        jnp.bfloat16
    )
    first_term = first_wide[1:-1, 1:-1]
    return jnp.concatenate([values, first_term, second], axis=-1)


def project_back(inputs, weights, order_index):
    flattened = inputs.reshape(-1, inputs.shape[-1])
    result = jnp.dot(flattened, weights[order_index].T, preferred_element_type=jnp.float32)
    return result.reshape(inputs.shape[:-1] + (weights.shape[2],))


def backward_terms(cotangent, weights, graph_data):
    widened = deep_rim(cotangent)
    top_term = project_back(widened, weights, 2).astype(jnp.bfloat16)
    middle = (
        project_back(widened[1:-1, 1:-1], weights, 1)
        + 2.0 * apply_operator(top_term, 2, graph_data)
    ).astype(jnp.bfloat16)
    return (
        project_back(cotangent, weights, 0)
        - top_term[2:-2, 2:-2].astype(jnp.float32)
        + apply_operator(middle, 1, graph_data)
    )


def shards(pixels, offsets, first_weights, second_weights, cotangent):
    shard_rows, shard_cols, channels = pixels.shape
    groups = lax.axis_size(GRP)
    members = lax.axis_size(DEV)
    features = first_weights.shape[0] * channels
    row_ids = lax.axis_index(GRP) * shard_rows - 6 + lax.iota(jnp.int32, shard_rows + 12)
    col_ids = lax.axis_index(DEV) * shard_cols - 6 + lax.iota(jnp.int32, shard_cols + 12)
    row_in = (row_ids >= 0) & (row_ids < shard_rows * groups)
    col_in = (col_ids >= 0) & (col_ids < shard_cols * members)
    inside = (row_in[:, None] & col_in[None, :]).astype(jnp.float32)
    offset_wide = with_halo(offsets, ((GRP, 0), (DEV, 1)), 6)
    fine_graph = graph_parts(offset_wide, inside, 6)
    pooled_offsets = offset_wide.reshape(shard_rows // 2 + 6, 2, shard_cols // 2 + 6, 2).mean(
        axis=(1, 3)
    )
    pooled_graph = graph_parts(pooled_offsets, inside[0::2, 0::2], 3)
    fine_terms = forward_terms(pixels, fine_graph)
    activation = jnp.dot(
        fine_terms.reshape(-1, features),
        first_weights.reshape(features, channels),
        preferred_element_type=jnp.float32,
    ).reshape(shard_rows, shard_cols, channels)
    hidden = jax.nn.silu(activation)
    pooled = (
        hidden.reshape(shard_rows // 2, 2, shard_cols // 2, 2, channels)
        .mean(axis=(1, 3))
        .astype(jnp.bfloat16)
    )
    pooled_terms = forward_terms(pooled, pooled_graph)
    level_out = (
        jnp.dot(
            pooled_terms.reshape(-1, features),
            second_weights.reshape(features, channels),
            preferred_element_type=jnp.float32,
        )
        .astype(jnp.bfloat16)
        .reshape(shard_rows // 2, shard_cols // 2, channels)
    )
    second_sum = jnp.dot(
        pooled_terms.reshape(-1, features).T,
        cotangent.reshape(-1, channels),
        preferred_element_type=jnp.float32,
    ).reshape(second_weights.shape)
    pooled_grad = backward_terms(cotangent, second_weights, pooled_graph)
    spread = jnp.broadcast_to(
        (0.25 * pooled_grad)[:, None, :, None, :],
        (shard_rows // 2, 2, shard_cols // 2, 2, channels),
    ).reshape(shard_rows, shard_cols, channels)
    sigmoid = jax.nn.sigmoid(activation)
    slope_term = sigmoid * (1.0 + activation * (1.0 - sigmoid))
    act_grad = (spread * slope_term).astype(jnp.bfloat16)
    first_sum = jnp.dot(
        fine_terms.reshape(-1, features).T,
        act_grad.reshape(-1, channels),
        preferred_element_type=jnp.float32,
    ).reshape(first_weights.shape)
    grad_pixels = backward_terms(act_grad, first_weights, fine_graph).astype(jnp.bfloat16)
    clip_level = 2.0 * channels
    first_total, second_total = packed_total(
        (first_sum, second_sum), (("grp_0", "grp_1"), ("dev_0", "dev_1"))
    )
    square_sum = jnp.sum(first_total * first_total) + jnp.sum(second_total * second_total)
    factor = jnp.minimum(1.0, clip_level * lax.rsqrt(square_sum + 1e-06))
    first_out = first_total * factor
    second_out = second_total * factor
    return (grad_pixels, first_out, second_out, level_out)


def solution(mesh):
    finer = Mesh(mesh.devices.reshape(8, 2, 4, 8), ("grp_0", "grp_1", "dev_0", "dev_1"))
    in_specs = (P(GRP, DEV, None), P(GRP, DEV), P(), P(), P(GRP, DEV, None))
    out_specs = (P(GRP, DEV, None), P(), P(), P(GRP, DEV, None))
    return jax.shard_map(
        shards, mesh=finer, in_specs=in_specs, out_specs=out_specs, check_vma=False
    )
```

profile of v0, /device:TPU:1, one launch (start us, length us, event | category | flops | bytes accessed | tf_op | source)
XLA Modules:
  0.0 219.4 jit_solution(6652790231110055705)
XLA Ops:
  0.6 0.7 fusion.212
  1.3 4.7 %collective-permute-start.4 = (f32[6,64]{1,0:T(8,128)S(1)}, f32[6,64]{1,0:T(8,128)S(1)}, u32[]{:S(2)}, u32[]{:S(2)}) collective-permute-start(f32[6,64]{1,0:T(8,128)S(1)} %get-tuple-element.54), channel_id=1, source_target_pairs={{0,32},{32,64},{64,96},{96,128},{128,160},{160,192},{192,224},{224... | collective-permute-start | bytes 4616 | tf_op jit(solution)/shard_map/ppermute | solution.py:28
  6.1 5.5 %collective-permute-start.5 = (f32[6,64]{1,0:T(8,128)S(1)}, f32[6,64]{1,0:T(8,128)S(1)}, u32[]{:S(2)}, u32[]{:S(2)}) collective-permute-start(f32[6,64]{1,0:T(8,128)S(1)} %get-tuple-element.55), channel_id=1, source_target_pairs={{32,0},{64,32},{96,64},{128,96},{160,128},{192,160},{224,192},{256... | collective-permute-start | bytes 4616 | tf_op jit(solution)/shard_map/ppermute | solution.py:31
  11.5 0.8 fusion.209
  12.3 1.9 collective-permute-start.1
  14.2 3.6 %collective-permute-start = (bf16[2,32,256]{2,1,0:T(8,128)(2,1)S(1)}, bf16[2,32,256]{2,1,0:T(8,128)(2,1)S(1)}, u32[]{:S(2)}, u32[]{:S(2)}) collective-permute-start(bf16[2,32,256]{2,1,0:T(8,128)(2,1)S(1)} %get-tuple-element.47), channel_id=1, source_target_pairs={{0,32},{32,64},{64,96},{96,128},{128,160},{160,192},{192,224},{224... | collective-permute-start | bytes 98312 | tf_op jit(solution)/shard_map/ppermute | solution.py:28
  17.9 0.9 fusion.206
  18.8 1.9 collective-permute-start.9
  20.7 0.7 pad_maximum_fusion.7
  21.5 1.3 collective-permute-start.6
  22.8 1.3 collective-permute-start.7
  24.4 3.6 %collective-permute-start.8 = (bf16[2,64,256]{2,1,0:T(8,128)(2,1)S(1)}, bf16[2,64,256]{2,1,0:T(8,128)(2,1)S(1)}, u32[]{:S(2)}, u32[]{:S(2)}) collective-permute-start(bf16[2,64,256]{2,1,0:T(8,128)(2,1)S(1)} %get-tuple-element.39), channel_id=1, source_target_pairs={{0,32},{32,64},{64,96},{96,128},{128,160},{160,192},{192,224},{224... | collective-permute-start | bytes 196616 | tf_op jit(solution)/shard_map/ppermute | solution.py:28
  28.0 0.8 pad_maximum_fusion.8
  29.2 0.7 slice_negate_fusion.3
  30.2 0.7 slice_negate_fusion
  31.0 4.3 %collective-permute-start.2 = (bf16[12,2,256]{2,1,0:T(2,128)(2,1)S(1)}, bf16[12,2,256]{2,1,0:T(2,128)(2,1)S(1)}, u32[]{:S(2)}, u32[]{:S(2)}) collective-permute-start(bf16[12,2,256]{2,1,0:T(2,128)(2,1)S(1)} %get-tuple-element.42), channel_id=1, source_target_pairs={{0,1},{1,2},{2,3},{3,4},{4,5},{5,6},{6,7},{7,8},{8,9},{9,10},{10,1... | collective-permute-start | bytes 36872 | tf_op jit(solution)/shard_map/ppermute | solution.py:28
  35.2 1.3 collective-permute-start.3
  36.6 0.7 slice.833
  37.4 0.7 slice.831
  38.1 0.7 slice.835
  38.9 0.7 slice.837
  39.6 0.7 slice.839
  40.3 0.7 slice.841
  41.1 0.7 slice.843
  41.8 0.7 slice.845
  44.2 0.6 fusion.23
  45.3 4.7 %collective-permute-start.10 = (bf16[20,2,256]{2,1,0:T(2,128)(2,1)S(1)}, bf16[20,2,256]{2,1,0:T(2,128)(2,1)S(1)}, u32[]{:S(2)}, u32[]{:S(2)}) collective-permute-start(bf16[20,2,256]{2,1,0:T(2,128)(2,1)S(1)} %get-tuple-element.34), channel_id=1, source_target_pairs={{0,1},{1,2},{2,3},{3,4},{4,5},{5,6},{6,7},{7,8},{8,9},{9,10},{10,1... | collective-permute-start | bytes 61448 | tf_op jit(solution)/shard_map/ppermute | solution.py:28
  50.0 1.3 collective-permute-start.11
  52.2 0.7 reshape.141
  53.0 3.5 %collective-permute-done.11 = bf16[20,2,256]{2,1,0:T(2,128)(2,1)S(1)} collective-permute-done((bf16[20,2,256]{2,1,0:T(2,128)(2,1)S(1)}, bf16[20,2,256]{2,1,0:T(2,128)(2,1)S(1)}, u32[]{:S(2)}, u32[]{:S(2)}) %collective-permute-start.11) | collective-permute-done | bytes 20512 | tf_op jit(solution)/shard_map/ppermute | solution.py:31
  57.0 2.3 %convert_multiply_fusion.2 = (f32[18,66,256]{2,1,0:T(8,128)S(1)}, bf16[18,66,256]{2,1,0:T(8,128)(2,1)S(1)}) fusion(f32[18,66]{1,0:T(8,128)S(1)} %copy-done.33, f32[20,68,256]{2,1,0:T(8,128)S(1)} %convert_multiply_fusion.1, f32[18,66]{1,0:T(8,128)S(1)} %slice.827, f32[18,66]{1,0:T(8,128)S(1)} %slice.825, f32[18,66]{1,0:T(8,128)S(1)} %slice.823, ...), kind=kLoop, calls=%fused_computation.43 | loop fusion | flops 5778432 | bytes 11604384 | tf_op jit(solution)/shard_map/mul | solution.py:127
  59.6 1.6 fusion.38
  61.3 2.2 fusion.45
  63.5 0.6 reshape.143
  64.1 0.7 reduce_sum.55
  64.9 5.8 %collective-permute-start.16 = (bf16[2,32,256]{2,1,0:T(8,128)(2,1)S(1)}, bf16[2,32,256]{2,1,0:T(8,128)(2,1)S(1)}, u32[]{:S(2)}, u32[]{:S(2)}) collective-permute-start(bf16[2,32,256]{2,1,0:T(8,128)(2,1)S(1)} %get-tuple-element.44), channel_id=1, source_target_pairs={{0,32},{32,64},{64,96},{96,128},{128,160},{160,192},{192,224},{224... | collective-permute-start | bytes 98312 | tf_op jit(solution)/shard_map/ppermute | solution.py:28
  70.7 1.9 collective-permute-start.17
  72.6 3.3 %collective-permute-done.17 = bf16[2,32,256]{2,1,0:T(8,128)(2,1)S(1)} collective-permute-done((bf16[2,32,256]{2,1,0:T(8,128)(2,1)S(1)}, bf16[2,32,256]{2,1,0:T(8,128)(2,1)S(1)}, u32[]{:S(2)}, u32[]{:S(2)}) %collective-permute-start.17) | collective-permute-done | bytes 32800 | tf_op jit(solution)/shard_map/ppermute | solution.py:31
  75.9 0.6 pad_maximum_fusion.11
  76.6 4.2 %collective-permute-start.18 = (bf16[12,2,256]{2,1,0:T(2,128)(2,1)}, bf16[12,2,256]{2,1,0:T(2,128)(2,1)}, u32[]{:S(2)}, u32[]{:S(2)}) collective-permute-start(bf16[12,2,256]{2,1,0:T(2,128)(2,1)} %get-tuple-element.40), channel_id=1, source_target_pairs={{0,1},{1,2},{2,3},{3,4},{4,5},{5,6},{6,7},{7,8},{8,9},{9,10},{10,1... | collective-permute-start | bytes 36872 | tf_op jit(solution)/shard_map/ppermute | solution.py:28
  80.8 1.5 collective-permute-start.19
  82.3 0.6 convolution_bitcast_fusion
  83.3 0.5 copy.11
  83.7 1.8 collective-permute-done.19
  85.5 0.9 convert_multiply_fusion.3
  86.6 0.8 convert_multiply_fusion.5
  89.5 50.9 %all_to_all.28 = f32[32,16,768]{2,1,0:T(8,128)S(1)} all-to-all(f32[32,16,768]{2,1,0:T(8,128)S(1)} %maximum_bitcast_fusion), channel_id=1, replica_groups=mesh['grp_0'=8,'grp_1'=2,'dev_0'=4,'dev_1'=8] {'dev_0','dev_1'}, dimensions={0} | all-to-all | bytes 3145728 | tf_op jit(solution)/shard_map/all_to_all | solution.py:68
  140.6 15.9 %all_to_all.29 = f32[16,1,768]{2,1,0:T(1,128)S(1)} all-to-all(f32[16,1,768]{2,1,0:T(1,128)S(1)} %all_to_all.19), channel_id=1, replica_groups=mesh['grp_0'=8,'grp_1'=2,'dev_0'=4,'dev_1'=8] {'grp_0','grp_1'}, dimensions={0} | all-to-all | bytes 98304 | tf_op jit(solution)/shard_map/all_to_all | solution.py:75
  156.5 10.3 %all_to_all.30 = f32[16,1,768]{2,1,0:T(1,128)S(1)} all-to-all(f32[16,1,768]{2,1,0:T(1,128)S(1)} %broadcast_in_dim.7), channel_id=1, replica_groups=mesh['grp_0'=8,'grp_1'=2,'dev_0'=4,'dev_1'=8] {'grp_0','grp_1'}, dimensions={0} | all-to-all | bytes 98304 | tf_op jit(solution)/shard_map/all_to_all | solution.py:45
  166.8 1.3 broadcast_in_dim.8
  168.1 5.5 %all-to-all-start.3 = ((f32[32,16,768]{2,1,0:T(8,128)}), f32[32,16,768]{2,1,0:T(8,128)S(1)}, u32[]{:S(2)}, u32[]{:S(2)}) async-start(f32[32,16,768]{2,1,0:T(8,128)} %broadcast_in_dim.8), calls=%async_computation.3 | async-start | bytes 3145728 | tf_op jit(solution)/shard_map/all_to_all | solution.py:45
  173.6 2.8 %collective-permute-start.12 = (bf16[2,64,256]{2,1,0:T(8,128)(2,1)S(1)}, bf16[2,64,256]{2,1,0:T(8,128)(2,1)S(1)}, u32[]{:S(2)}, u32[]{:S(2)}) collective-permute-start(bf16[2,64,256]{2,1,0:T(8,128)(2,1)S(1)} %get-tuple-element.36), channel_id=1, source_target_pairs={{0,32},{32,64},{64,96},{96,128},{128,160},{160,192},{192,224},{224... | collective-permute-start | bytes 196616 | tf_op jit(solution)/shard_map/ppermute | solution.py:28
  176.4 1.9 collective-permute-start.13
  178.4 3.6 %collective-permute-done.13 = bf16[2,64,256]{2,1,0:T(8,128)(2,1)S(1)} collective-permute-done((bf16[2,64,256]{2,1,0:T(8,128)(2,1)S(1)}, bf16[2,64,256]{2,1,0:T(8,128)(2,1)S(1)}, u32[]{:S(2)}, u32[]{:S(2)}) %collective-permute-start.13) | collective-permute-done | bytes 65568 | tf_op jit(solution)/shard_map/ppermute | solution.py:31
  182.1 3.7 %collective-permute-start.14 = (bf16[20,2,256]{2,1,0:T(2,128)(2,1)S(1)}, bf16[20,2,256]{2,1,0:T(2,128)(2,1)S(1)}, u32[]{:S(2)}, u32[]{:S(2)}) collective-permute-start(bf16[20,2,256]{2,1,0:T(2,128)(2,1)S(1)} %get-tuple-element.32), channel_id=1, source_target_pairs={{0,1},{1,2},{2,3},{3,4},{4,5},{5,6},{6,7},{7,8},{8,9},{9,10},{10,1... | collective-permute-start | bytes 61448 | tf_op jit(solution)/shard_map/ppermute | solution.py:28
  185.8 1.3 collective-permute-start.15
  187.1 0.9 convolution_convert_fusion.2
  188.1 17.0 %collective-permute-done.14 = bf16[20,2,256]{2,1,0:T(2,128)(2,1)S(1)} collective-permute-done((bf16[20,2,256]{2,1,0:T(2,128)(2,1)S(1)}, bf16[20,2,256]{2,1,0:T(2,128)(2,1)S(1)}, u32[]{:S(2)}, u32[]{:S(2)}) %collective-permute-start.14) | collective-permute-done | bytes 20512 | tf_op jit(solution)/shard_map/ppermute | solution.py:28
  205.1 4.2 %collective-permute-done.15 = bf16[20,2,256]{2,1,0:T(2,128)(2,1)S(1)} collective-permute-done((bf16[20,2,256]{2,1,0:T(2,128)(2,1)S(1)}, bf16[20,2,256]{2,1,0:T(2,128)(2,1)S(1)}, u32[]{:S(2)}, u32[]{:S(2)}) %collective-permute-start.15) | collective-permute-done | bytes 20512 | tf_op jit(solution)/shard_map/ppermute | solution.py:31
  209.9 1.8 fusion.2
  211.9 2.6 %fusion.27 = bf16[16,64,256]{2,1,0:T(8,128)(2,1)} fusion(f32[18,66,256]{2,1,0:T(8,128)S(1)} %fusion.2, bf16[20,68,256]{2,1,0:T(8,128)(2,1)S(1)} %get-tuple-element.59, f32[16,64]{1,0:T(8,128)S(1)} %copy-done.70, f32[16,64]{1,0:T(8,128)S(1)} %copy-done.68, f32[16,64]{1,0:T(8,128)S(1)} %copy-done.66, f32[16,64]{1,0:T(8,128)S(1)} %copy-done.64, ...), kind=kOutput, calls=%fused_computation.56 | convolution fusion | flops 139460608 | bytes 10166272 | tf_op jit(solution)/shard_map/dot_general | solution.py:155
  214.5 0.8 multiply_reduce_fusion
  217.0 1.0 mul.1015
  218.3 1.0 mul.1013
  (268 shorter events, 8.9 us)
Async XLA Ops:
  1.3 29.6 %copy-start.7 = (bf16[8,32,256]{2,1,0:T(8,128)(2,1)S(1)}, bf16[8,32,256]{2,1,0:T(8,128)(2,1)}, u32[]{:S(2)}) copy-start(bf16[8,32,256]{2,1,0:T(8,128)(2,1)} %param.9) | copy-start | bytes 393220
  1.3 19.4 %collective-permute-start.4 = (f32[6,64]{1,0:T(8,128)S(1)}, f32[6,64]{1,0:T(8,128)S(1)}, u32[]{:S(2)}, u32[]{:S(2)}) collective-permute-start(f32[6,64]{1,0:T(8,128)S(1)} %get-tuple-element.54), channel_id=1, source_target_pairs={{0,32},{32,64},{64,96},{96,128},{128,160},{160,192},{192,224},{224... | collective-permute-start | bytes 4616 | tf_op jit(solution)/shard_map/ppermute | solution.py:28
  6.1 14.7 %collective-permute-start.5 = (f32[6,64]{1,0:T(8,128)S(1)}, f32[6,64]{1,0:T(8,128)S(1)}, u32[]{:S(2)}, u32[]{:S(2)}) collective-permute-start(f32[6,64]{1,0:T(8,128)S(1)} %get-tuple-element.55), channel_id=1, source_target_pairs={{32,0},{64,32},{96,64},{128,96},{160,128},{192,160},{224,192},{256... | collective-permute-start | bytes 4616 | tf_op jit(solution)/shard_map/ppermute | solution.py:31
  12.3 18.6 %collective-permute-start.1 = (bf16[2,32,256]{2,1,0:T(8,128)(2,1)S(1)}, bf16[2,32,256]{2,1,0:T(8,128)(2,1)S(1)}, u32[]{:S(2)}, u32[]{:S(2)}) collective-permute-start(bf16[2,32,256]{2,1,0:T(8,128)(2,1)S(1)} %get-tuple-element.46), channel_id=1, source_target_pairs={{32,0},{64,32},{96,64},{128,96},{160,128},{192,160},{224,192},{256... | collective-permute-start | bytes 98312 | tf_op jit(solution)/shard_map/ppermute | solution.py:31
  14.2 16.7 %collective-permute-start = (bf16[2,32,256]{2,1,0:T(8,128)(2,1)S(1)}, bf16[2,32,256]{2,1,0:T(8,128)(2,1)S(1)}, u32[]{:S(2)}, u32[]{:S(2)}) collective-permute-start(bf16[2,32,256]{2,1,0:T(8,128)(2,1)S(1)} %get-tuple-element.47), channel_id=1, source_target_pairs={{0,32},{32,64},{64,96},{96,128},{128,160},{160,192},{192,224},{224... | collective-permute-start | bytes 98312 | tf_op jit(solution)/shard_map/ppermute | solution.py:28
  18.8 26.5 %collective-permute-start.9 = (bf16[2,64,256]{2,1,0:T(8,128)(2,1)S(1)}, bf16[2,64,256]{2,1,0:T(8,128)(2,1)S(1)}, u32[]{:S(2)}, u32[]{:S(2)}) collective-permute-start(bf16[2,64,256]{2,1,0:T(8,128)(2,1)S(1)} %get-tuple-element.38), channel_id=1, source_target_pairs={{32,0},{64,32},{96,64},{128,96},{160,128},{192,160},{224,192},{256... | collective-permute-start | bytes 196616 | tf_op jit(solution)/shard_map/ppermute | solution.py:31
  21.5 2.8 %collective-permute-start.6 = (f32[28,6]{1,0:T(8,128)S(1)}, f32[28,6]{1,0:T(8,128)S(1)}, u32[]{:S(2)}, u32[]{:S(2)}) collective-permute-start(f32[28,6]{1,0:T(8,128)S(1)} %get-tuple-element.50), channel_id=1, source_target_pairs={{0,1},{1,2},{2,3},{3,4},{4,5},{5,6},{6,7},{7,8},{8,9},{9,10},{10,1... | collective-permute-start | bytes 2024 | tf_op jit(solution)/shard_map/ppermute | solution.py:28
  22.8 5.2 %collective-permute-start.7 = (f32[28,6]{1,0:T(8,128)S(1)}, f32[28,6]{1,0:T(8,128)S(1)}, u32[]{:S(2)}, u32[]{:S(2)}) collective-permute-start(f32[28,6]{1,0:T(8,128)S(1)} %get-tuple-element.51), channel_id=1, source_target_pairs={{1,0},{2,1},{3,2},{4,3},{5,4},{6,5},{7,6},{8,7},{9,8},{10,9},{11,1... | collective-permute-start | bytes 2024 | tf_op jit(solution)/shard_map/ppermute | solution.py:31
  24.4 20.6 %collective-permute-start.8 = (bf16[2,64,256]{2,1,0:T(8,128)(2,1)S(1)}, bf16[2,64,256]{2,1,0:T(8,128)(2,1)S(1)}, u32[]{:S(2)}, u32[]{:S(2)}) collective-permute-start(bf16[2,64,256]{2,1,0:T(8,128)(2,1)S(1)} %get-tuple-element.39), channel_id=1, source_target_pairs={{0,32},{32,64},{64,96},{96,128},{128,160},{160,192},{192,224},{224... | collective-permute-start | bytes 196616 | tf_op jit(solution)/shard_map/ppermute | solution.py:28
  28.9 14.9 %copy-start.1 = (bf16[3,256,256]{2,1,0:T(8,128)(2,1)S(1)}, bf16[3,256,256]{2,1,0:T(8,128)(2,1)}, u32[]{:S(2)}) copy-start(bf16[3,256,256]{2,1,0:T(8,128)(2,1)} %param.8) | copy-start | bytes 1179652
  30.2 14.6 %copy-start.35 = (f32[10,34]{1,0:T(8,128)}, f32[10,34]{1,0:T(8,128)S(1)}, u32[]{:S(2)}) copy-start(f32[10,34]{1,0:T(8,128)S(1)} %get-tuple-element.53) | copy-start | bytes 4084
  31.0 12.9 %collective-permute-start.2 = (bf16[12,2,256]{2,1,0:T(2,128)(2,1)S(1)}, bf16[12,2,256]{2,1,0:T(2,128)(2,1)S(1)}, u32[]{:S(2)}, u32[]{:S(2)}) collective-permute-start(bf16[12,2,256]{2,1,0:T(2,128)(2,1)S(1)} %get-tuple-element.42), channel_id=1, source_target_pairs={{0,1},{1,2},{2,3},{3,4},{4,5},{5,6},{6,7},{7,8},{8,9},{9,10},{10,1... | collective-permute-start | bytes 36872 | tf_op jit(solution)/shard_map/ppermute | solution.py:28
  35.2 8.6 %collective-permute-start.3 = (bf16[12,2,256]{2,1,0:T(2,128)(2,1)S(1)}, bf16[12,2,256]{2,1,0:T(2,128)(2,1)S(1)}, u32[]{:S(2)}, u32[]{:S(2)}) collective-permute-start(bf16[12,2,256]{2,1,0:T(2,128)(2,1)S(1)} %get-tuple-element.43), channel_id=1, source_target_pairs={{1,0},{2,1},{3,2},{4,3},{5,4},{6,5},{7,6},{8,7},{9,8},{10,9},{11,1... | collective-permute-start | bytes 36872 | tf_op jit(solution)/shard_map/ppermute | solution.py:31
  36.6 14.7 %copy-start.71 = (f32[8,32]{1,0:T(8,128)}, f32[8,32]{1,0:T(8,128)S(1)}, u32[]{:S(2)}) copy-start(f32[8,32]{1,0:T(8,128)S(1)} %slice_negate_fusion.1) | copy-start | bytes 3076
  37.4 19.5 %copy-start.13 = (f32[18,66]{1,0:T(8,128)}, f32[18,66]{1,0:T(8,128)S(1)}, u32[]{:S(2)}) copy-start(f32[18,66]{1,0:T(8,128)S(1)} %slice.815) | copy-start | bytes 14260
  38.1 18.8 %copy-start.15 = (f32[18,66]{1,0:T(8,128)}, f32[18,66]{1,0:T(8,128)S(1)}, u32[]{:S(2)}) copy-start(f32[18,66]{1,0:T(8,128)S(1)} %slice.810) | copy-start | bytes 14260
  38.9 18.0 %copy-start.17 = (f32[18,66]{1,0:T(8,128)}, f32[18,66]{1,0:T(8,128)S(1)}, u32[]{:S(2)}) copy-start(f32[18,66]{1,0:T(8,128)S(1)} %slice.817) | copy-start | bytes 14260
  39.6 17.3 %copy-start.19 = (f32[18,66]{1,0:T(8,128)}, f32[18,66]{1,0:T(8,128)S(1)}, u32[]{:S(2)}) copy-start(f32[18,66]{1,0:T(8,128)S(1)} %slice.819) | copy-start | bytes 14260
  40.3 16.6 %copy-start.21 = (f32[18,66]{1,0:T(8,128)}, f32[18,66]{1,0:T(8,128)S(1)}, u32[]{:S(2)}) copy-start(f32[18,66]{1,0:T(8,128)S(1)} %slice.821) | copy-start | bytes 14260
  41.1 15.8 %copy-start.23 = (f32[18,66]{1,0:T(8,128)}, f32[18,66]{1,0:T(8,128)S(1)}, u32[]{:S(2)}) copy-start(f32[18,66]{1,0:T(8,128)S(1)} %slice.823) | copy-start | bytes 14260
  41.8 15.1 %copy-start.25 = (f32[18,66]{1,0:T(8,128)}, f32[18,66]{1,0:T(8,128)S(1)}, u32[]{:S(2)}) copy-start(f32[18,66]{1,0:T(8,128)S(1)} %slice.825) | copy-start | bytes 14260
  42.6 14.4 %copy-start.27 = (f32[18,66]{1,0:T(8,128)}, f32[18,66]{1,0:T(8,128)S(1)}, u32[]{:S(2)}) copy-start(f32[18,66]{1,0:T(8,128)S(1)} %slice.827) | copy-start | bytes 14260
  42.6 13.8 %copy-start.29 = (f32[20,68]{1,0:T(8,128)}, f32[20,68]{1,0:T(8,128)S(1)}, u32[]{:S(2)}) copy-start(f32[20,68]{1,0:T(8,128)S(1)} %slice.811) | copy-start | bytes 16324
  42.7 8.6 %copy-start.73 = (f32[8,32]{1,0:T(8,128)}, f32[8,32]{1,0:T(8,128)S(1)}, u32[]{:S(2)}) copy-start(f32[8,32]{1,0:T(8,128)S(1)} %slice.777) | copy-start | bytes 3076
  42.9 8.4 %copy-start.75 = (f32[8,32]{1,0:T(8,128)}, f32[8,32]{1,0:T(8,128)S(1)}, u32[]{:S(2)}) copy-start(f32[8,32]{1,0:T(8,128)S(1)} %slice.758) | copy-start | bytes 3076
  43.0 8.3 %copy-start.77 = (f32[8,32]{1,0:T(8,128)}, f32[8,32]{1,0:T(8,128)S(1)}, u32[]{:S(2)}) copy-start(f32[8,32]{1,0:T(8,128)S(1)} %slice.779) | copy-start | bytes 3076
  43.2 8.2 %copy-start.79 = (f32[8,32]{1,0:T(8,128)}, f32[8,32]{1,0:T(8,128)S(1)}, u32[]{:S(2)}) copy-start(f32[8,32]{1,0:T(8,128)S(1)} %slice.781) | copy-start | bytes 3076
  43.3 8.0 %copy-start.81 = (f32[8,32]{1,0:T(8,128)}, f32[8,32]{1,0:T(8,128)S(1)}, u32[]{:S(2)}) copy-start(f32[8,32]{1,0:T(8,128)S(1)} %slice.783) | copy-start | bytes 3076
  43.5 7.9 %copy-start.83 = (f32[8,32]{1,0:T(8,128)}, f32[8,32]{1,0:T(8,128)S(1)}, u32[]{:S(2)}) copy-start(f32[8,32]{1,0:T(8,128)S(1)} %slice.785) | copy-start | bytes 3076
  43.6 7.7 %copy-start.85 = (f32[8,32]{1,0:T(8,128)}, f32[8,32]{1,0:T(8,128)S(1)}, u32[]{:S(2)}) copy-start(f32[8,32]{1,0:T(8,128)S(1)} %slice.787) | copy-start | bytes 3076
  43.8 7.6 %copy-start.87 = (f32[8,32]{1,0:T(8,128)}, f32[8,32]{1,0:T(8,128)S(1)}, u32[]{:S(2)}) copy-start(f32[8,32]{1,0:T(8,128)S(1)} %slice.789) | copy-start | bytes 3076
  45.3 7.7 %collective-permute-start.10 = (bf16[20,2,256]{2,1,0:T(2,128)(2,1)S(1)}, bf16[20,2,256]{2,1,0:T(2,128)(2,1)S(1)}, u32[]{:S(2)}, u32[]{:S(2)}) collective-permute-start(bf16[20,2,256]{2,1,0:T(2,128)(2,1)S(1)} %get-tuple-element.34), channel_id=1, source_target_pairs={{0,1},{1,2},{2,3},{3,4},{4,5},{5,6},{6,7},{7,8},{8,9},{9,10},{10,1... | collective-permute-start | bytes 61448 | tf_op jit(solution)/shard_map/ppermute | solution.py:28
  50.0 6.5 %collective-permute-start.11 = (bf16[20,2,256]{2,1,0:T(2,128)(2,1)S(1)}, bf16[20,2,256]{2,1,0:T(2,128)(2,1)S(1)}, u32[]{:S(2)}, u32[]{:S(2)}) collective-permute-start(bf16[20,2,256]{2,1,0:T(2,128)(2,1)S(1)} %get-tuple-element.35), channel_id=1, source_target_pairs={{1,0},{2,1},{3,2},{4,3},{5,4},{6,5},{7,6},{8,7},{9,8},{10,9},{11,1... | collective-permute-start | bytes 61448 | tf_op jit(solution)/shard_map/ppermute | solution.py:31
  52.9 4.0 %copy-start.31 = (f32[18,66]{1,0:T(8,128)S(1)}, f32[18,66]{1,0:T(8,128)}, u32[]{:S(2)}) copy-start(f32[18,66]{1,0:T(8,128)} %get-tuple-element.48) | copy-start | bytes 14260
  53.0 4.0 %copy-start.33 = (f32[18,66]{1,0:T(8,128)S(1)}, f32[18,66]{1,0:T(8,128)}, u32[]{:S(2)}) copy-start(f32[18,66]{1,0:T(8,128)} %get-tuple-element.49) | copy-start | bytes 14260
  64.1 18.2 %copy-start.4 = (bf16[16,64,256]{2,1,0:T(8,128)(2,1)S(1)}, bf16[16,64,256]{2,1,0:T(8,128)(2,1)}, u32[]{:S(2)}) copy-start(bf16[16,64,256]{2,1,0:T(8,128)(2,1)} %copy-done.3) | copy-start | bytes 1572868
  64.1 18.2 %copy-start.6 = (bf16[16,64,256]{2,1,0:T(8,128)(2,1)S(1)}, bf16[16,64,256]{2,1,0:T(8,128)(2,1)}, u32[]{:S(2)}) copy-start(bf16[16,64,256]{2,1,0:T(8,128)(2,1)} %copy-done.5) | copy-start | bytes 1572868
  64.9 7.7 %collective-permute-start.16 = (bf16[2,32,256]{2,1,0:T(8,128)(2,1)S(1)}, bf16[2,32,256]{2,1,0:T(8,128)(2,1)S(1)}, u32[]{:S(2)}, u32[]{:S(2)}) collective-permute-start(bf16[2,32,256]{2,1,0:T(8,128)(2,1)S(1)} %get-tuple-element.44), channel_id=1, source_target_pairs={{0,32},{32,64},{64,96},{96,128},{128,160},{160,192},{192,224},{224... | collective-permute-start | bytes 98312 | tf_op jit(solution)/shard_map/ppermute | solution.py:28
  70.7 5.2 %collective-permute-start.17 = (bf16[2,32,256]{2,1,0:T(8,128)(2,1)S(1)}, bf16[2,32,256]{2,1,0:T(8,128)(2,1)S(1)}, u32[]{:S(2)}, u32[]{:S(2)}) collective-permute-start(bf16[2,32,256]{2,1,0:T(8,128)(2,1)S(1)} %get-tuple-element.45), channel_id=1, source_target_pairs={{32,0},{64,32},{96,64},{128,96},{160,128},{192,160},{224,192},{256... | collective-permute-start | bytes 98312 | tf_op jit(solution)/shard_map/ppermute | solution.py:31
  72.6 9.6 %copy-start.9 = (bf16[2,32,256]{2,1,0:T(8,128)(2,1)}, bf16[2,32,256]{2,1,0:T(8,128)(2,1)S(1)}, u32[]{:S(2)}) copy-start(bf16[2,32,256]{2,1,0:T(8,128)(2,1)S(1)} %collective-permute-done.16) | copy-start | bytes 98308
  75.9 6.3 %copy-start.11 = (bf16[2,32,256]{2,1,0:T(8,128)(2,1)}, bf16[2,32,256]{2,1,0:T(8,128)(2,1)S(1)}, u32[]{:S(2)}) copy-start(bf16[2,32,256]{2,1,0:T(8,128)(2,1)S(1)} %collective-permute-done.17) | copy-start | bytes 98308
  76.6 7.2 %collective-permute-start.18 = (bf16[12,2,256]{2,1,0:T(2,128)(2,1)}, bf16[12,2,256]{2,1,0:T(2,128)(2,1)}, u32[]{:S(2)}, u32[]{:S(2)}) collective-permute-start(bf16[12,2,256]{2,1,0:T(2,128)(2,1)} %get-tuple-element.40), channel_id=1, source_target_pairs={{0,1},{1,2},{2,3},{3,4},{4,5},{5,6},{6,7},{7,8},{8,9},{9,10},{10,1... | collective-permute-start | bytes 36872 | tf_op jit(solution)/shard_map/ppermute | solution.py:28
  80.8 4.7 %collective-permute-start.19 = (bf16[12,2,256]{2,1,0:T(2,128)(2,1)}, bf16[12,2,256]{2,1,0:T(2,128)(2,1)}, u32[]{:S(2)}, u32[]{:S(2)}) collective-permute-start(bf16[12,2,256]{2,1,0:T(2,128)(2,1)} %get-tuple-element.41), channel_id=1, source_target_pairs={{1,0},{2,1},{3,2},{4,3},{5,4},{6,5},{7,6},{8,7},{9,8},{10,9},{11,1... | collective-permute-start | bytes 36872 | tf_op jit(solution)/shard_map/ppermute | solution.py:31
  83.2 3.2 %copy-start.36 = (f32[10,34]{1,0:T(8,128)S(1)}, f32[10,34]{1,0:T(8,128)}, u32[]{:S(2)}) copy-start(f32[10,34]{1,0:T(8,128)} %copy-done.35) | copy-start | bytes 4084
  83.2 3.2 %copy-start.38 = (f32[10,34]{1,0:T(8,128)S(1)}, f32[10,34]{1,0:T(8,128)}, u32[]{:S(2)}) copy-start(f32[10,34]{1,0:T(8,128)} %copy-done.37) | copy-start | bytes 4084
  83.2 3.2 %copy-start.40 = (f32[10,34]{1,0:T(8,128)S(1)}, f32[10,34]{1,0:T(8,128)}, u32[]{:S(2)}) copy-start(f32[10,34]{1,0:T(8,128)} %copy-done.39) | copy-start | bytes 4084
  168.1 46.4 %all-to-all-start.3 = ((f32[32,16,768]{2,1,0:T(8,128)}), f32[32,16,768]{2,1,0:T(8,128)S(1)}, u32[]{:S(2)}, u32[]{:S(2)}) async-start(f32[32,16,768]{2,1,0:T(8,128)} %broadcast_in_dim.8), calls=%async_computation.3 | async-start | bytes 3145728 | tf_op jit(solution)/shard_map/all_to_all | solution.py:45
  173.5 13.5 %copy-start.2 = (bf16[3,256,256]{2,1,0:T(8,128)(2,1)S(1)}, bf16[3,256,256]{2,1,0:T(8,128)(2,1)}, u32[]{:S(2)}) copy-start(bf16[3,256,256]{2,1,0:T(8,128)(2,1)} %param.8) | copy-start | bytes 1179652
  173.6 35.8 %copy-start.30 = (f32[20,68]{1,0:T(8,128)S(1)}, f32[20,68]{1,0:T(8,128)}, u32[]{:S(2)}) copy-start(f32[20,68]{1,0:T(8,128)} %copy-done.29) | copy-start | bytes 16324
  173.6 35.7 %copy-start.90 = (bf16[3,256,256]{2,1,0:T(8,128)(2,1)S(1)}, bf16[3,256,256]{2,1,0:T(8,128)(2,1)}, u32[]{:S(2)}) copy-start(bf16[3,256,256]{2,1,0:T(8,128)(2,1)} %param.7) | copy-start | bytes 1179652
  173.6 4.8 %collective-permute-start.12 = (bf16[2,64,256]{2,1,0:T(8,128)(2,1)S(1)}, bf16[2,64,256]{2,1,0:T(8,128)(2,1)S(1)}, u32[]{:S(2)}, u32[]{:S(2)}) collective-permute-start(bf16[2,64,256]{2,1,0:T(8,128)(2,1)S(1)} %get-tuple-element.36), channel_id=1, source_target_pairs={{0,32},{32,64},{64,96},{96,128},{128,160},{160,192},{192,224},{224... | collective-permute-start | bytes 196616 | tf_op jit(solution)/shard_map/ppermute | solution.py:28
  176.4 5.6 %collective-permute-start.13 = (bf16[2,64,256]{2,1,0:T(8,128)(2,1)S(1)}, bf16[2,64,256]{2,1,0:T(8,128)(2,1)S(1)}, u32[]{:S(2)}, u32[]{:S(2)}) collective-permute-start(bf16[2,64,256]{2,1,0:T(8,128)(2,1)S(1)} %get-tuple-element.37), channel_id=1, source_target_pairs={{32,0},{64,32},{96,64},{128,96},{160,128},{192,160},{224,192},{256... | collective-permute-start | bytes 196616 | tf_op jit(solution)/shard_map/ppermute | solution.py:31
  182.1 23.1 %collective-permute-start.14 = (bf16[20,2,256]{2,1,0:T(2,128)(2,1)S(1)}, bf16[20,2,256]{2,1,0:T(2,128)(2,1)S(1)}, u32[]{:S(2)}, u32[]{:S(2)}) collective-permute-start(bf16[20,2,256]{2,1,0:T(2,128)(2,1)S(1)} %get-tuple-element.32), channel_id=1, source_target_pairs={{0,1},{1,2},{2,3},{3,4},{4,5},{5,6},{6,7},{7,8},{8,9},{9,10},{10,1... | collective-permute-start | bytes 61448 | tf_op jit(solution)/shard_map/ppermute | solution.py:28
  185.8 23.5 %collective-permute-start.15 = (bf16[20,2,256]{2,1,0:T(2,128)(2,1)S(1)}, bf16[20,2,256]{2,1,0:T(2,128)(2,1)S(1)}, u32[]{:S(2)}, u32[]{:S(2)}) collective-permute-start(bf16[20,2,256]{2,1,0:T(2,128)(2,1)S(1)} %get-tuple-element.33), channel_id=1, source_target_pairs={{1,0},{2,1},{3,2},{4,3},{5,4},{6,5},{7,6},{8,7},{9,8},{10,9},{11,1... | collective-permute-start | bytes 61448 | tf_op jit(solution)/shard_map/ppermute | solution.py:31
  188.0 21.7 %copy-start.14 = (f32[18,66]{1,0:T(8,128)S(1)}, f32[18,66]{1,0:T(8,128)}, u32[]{:S(2)}) copy-start(f32[18,66]{1,0:T(8,128)} %copy-done.13) | copy-start | bytes 14260
  188.0 21.7 %copy-start.16 = (f32[18,66]{1,0:T(8,128)S(1)}, f32[18,66]{1,0:T(8,128)}, u32[]{:S(2)}) copy-start(f32[18,66]{1,0:T(8,128)} %copy-done.15) | copy-start | bytes 14260
  188.0 21.8 %copy-start.18 = (f32[18,66]{1,0:T(8,128)S(1)}, f32[18,66]{1,0:T(8,128)}, u32[]{:S(2)}) copy-start(f32[18,66]{1,0:T(8,128)} %copy-done.17) | copy-start | bytes 14260
  188.0 21.8 %copy-start.20 = (f32[18,66]{1,0:T(8,128)S(1)}, f32[18,66]{1,0:T(8,128)}, u32[]{:S(2)}) copy-start(f32[18,66]{1,0:T(8,128)} %copy-done.19) | copy-start | bytes 14260
  188.0 21.8 %copy-start.22 = (f32[18,66]{1,0:T(8,128)S(1)}, f32[18,66]{1,0:T(8,128)}, u32[]{:S(2)}) copy-start(f32[18,66]{1,0:T(8,128)} %copy-done.21) | copy-start | bytes 14260
  188.0 21.8 %copy-start.24 = (f32[18,66]{1,0:T(8,128)S(1)}, f32[18,66]{1,0:T(8,128)}, u32[]{:S(2)}) copy-start(f32[18,66]{1,0:T(8,128)} %copy-done.23) | copy-start | bytes 14260
  188.0 21.8 %copy-start.26 = (f32[18,66]{1,0:T(8,128)S(1)}, f32[18,66]{1,0:T(8,128)}, u32[]{:S(2)}) copy-start(f32[18,66]{1,0:T(8,128)} %copy-done.25) | copy-start | bytes 14260
  188.0 21.8 %copy-start.28 = (f32[18,66]{1,0:T(8,128)S(1)}, f32[18,66]{1,0:T(8,128)}, u32[]{:S(2)}) copy-start(f32[18,66]{1,0:T(8,128)} %copy-done.27) | copy-start | bytes 14260
  188.1 21.8 %copy-start.32 = (f32[18,66]{1,0:T(8,128)S(1)}, f32[18,66]{1,0:T(8,128)}, u32[]{:S(2)}) copy-start(f32[18,66]{1,0:T(8,128)} %get-tuple-element.48) | copy-start | bytes 14260
  188.1 21.8 %copy-start.34 = (f32[18,66]{1,0:T(8,128)S(1)}, f32[18,66]{1,0:T(8,128)}, u32[]{:S(2)}) copy-start(f32[18,66]{1,0:T(8,128)} %get-tuple-element.49) | copy-start | bytes 14260
  (48 other events, 92.8 us)
where the time goes:
time: 222 us; the launch traced here: 219 us
  blocking collectives  77.1 us (35%)
  starting transfers between devices  63.9 us (29%)
  waiting for transfers between devices  33.4 us (15%)
  local copies, waits for them, and re-layouts  18.5 us (8%)
  other arithmetic  12.4 us (6%)
  matrix products  10.2 us (5%)
  between operations  3.76 us (2%)
    all_to_all x1, blocking collectives, sum_at_owner(): tiles = lax.all_to_all(split_up(value, dim, size), axis, 0, 0, tiled=True)  50.9 us
    ppermute x10, starting transfers between devices, with_halo(): lax.ppermute(lax.slice_in_dim(block, block.shape[dim] - width, None, axis...  38.7 us
    ppermute x10, starting transfers between devices, with_halo(): lax.ppermute(lax.slice_in_dim(block, 0, width, axis=dim), axis, backward)  19.8 us
    ppermute x10, waiting for transfers between devices, with_halo(): lax.ppermute(lax.slice_in_dim(block, block.shape[dim] - width, None, axis...  17.1 us
    ppermute x10, waiting for transfers between devices, with_halo(): lax.ppermute(lax.slice_in_dim(block, 0, width, axis=dim), axis, backward)  16.4 us
    all_to_all x1, blocking collectives, summed_rows(): return jnp.sum(lax.all_to_all(own, far, 0, 0, tiled=True), axis=0)  15.9 us
    all_to_all x1, blocking collectives, sent_to_all(): return lax.all_to_all(copies, axis, split_axis=0, concat_axis=0, tiled=True)  10.3 us
    slice x33, local copies, waits for them, and re-layouts, trim(): tensor[margin_cut:tensor.shape[0] - margin_cut, margin_cut:tensor.shape[1...  7.15 us
  transfers between devices with their start and end apart: 21, of which 6 were waited for; matrix products, arithmetic and copies ran while one was open for 10% of the time, Pallas kernels for 0%

commit v1 on v0

v1 whole, which is shorter than its diff:
```python
import functools

import jax
import jax.numpy as jnp
from jax import lax
from jax.experimental import pallas as pl
from jax.experimental.pallas import tpu as pltpu
from jax.sharding import Mesh
from jax.sharding import PartitionSpec as P

GRP = ("grp_0", "grp_1")
DEV = ("dev_0", "dev_1")
EVERY = GRP + DEV
BF = jnp.bfloat16
F32 = jnp.float32

R, C, F = 16, 64, 256
PR, PC = R // 2, C // 2
HR, HC = 6, 8
ER, EC = R + 2 * HR, C + 2 * HC
QR, QC = PR + 6, PC + 8
OR = R + 16

SIDES = ((-1, 0), (1, 0), (0, -1), (0, 1), (-1, -1), (-1, 1), (1, -1), (1, 1))
STEPS = (
    (-1, 0, 1.0),
    (1, 0, 1.0),
    (0, -1, 1.0),
    (0, 1, 1.0),
    (-1, -1, 0.5),
    (-1, 1, 0.5),
    (1, -1, 0.5),
    (1, 1, 0.5),
)


def mm(a, b):
    return lax.dot_general(a, b, (((1,), (0,)), ((), ())), preferred_element_type=F32)


def mm_nt(a, b):
    return lax.dot_general(a, b, (((1,), (1,)), ((), ())), preferred_element_type=F32)


def mm_tn(a, b):
    return lax.dot_general(a, b, (((0,), (0,)), ((), ())), preferred_element_type=F32)


def px_rows(di):
    return {-1: (0, HR), 1: (R - HR, HR), 0: (0, R)}[di]


def ct_rows(di):
    return {-1: (0, 3), 1: (PR - 3, 3), 0: (0, PR)}[di]


def off_rows(di):
    return {-1: (0, 8), 1: (R - 8, 8), 0: (0, R)}[di]


def message_parts(di, dj):
    px = px_rows(di)[1] * (HC if dj else C)
    ct = ct_rows(di)[1] * (8 if dj else PC)
    ct += -ct % 16
    off = 48 if di == 0 else 32
    return px, px + ct, px + ct + off


def rolled(x, shift, axis):
    return pltpu.roll(x, shift % x.shape[axis], axis)


def pack_kernel(px_ref, ct_ref, off_ref, *rest):
    outs, wide = rest[:8], rest[8]
    wide[...] = jnp.zeros_like(wide)
    wide[:, 0:C] = off_ref[...]
    lane = lax.broadcasted_iota(jnp.int32, (R, 128), 1)
    for (di, dj), out in zip(SIDES, outs):
        ct_at, off_at, _ = message_parts(di, dj)
        first, count = px_rows(di)
        if dj == 0:
            out[0 : count * C, :] = px_ref[first * C : (first + count) * C, :]
        else:
            start = 0 if dj < 0 else C - 16
            half = slice(0, 8) if dj < 0 else slice(8, 16)
            for r in range(0, count, 2):
                tiles = []
                for k in (0, 1):
                    at = (first + r + k) * C + start
                    tiles.append(px_ref[at : at + 16, :].astype(F32)[half])
                out[r * 8 : r * 8 + 16, :] = jnp.concatenate(tiles, 0).astype(BF)
        first, count = ct_rows(di)
        if dj == 0:
            out[ct_at : ct_at + count * PC, :] = ct_ref[first * PC : (first + count) * PC, :]
        else:
            start = 0 if dj < 0 else PC - 16
            half = slice(0, 8) if dj < 0 else slice(8, 16)
            for r in range(0, count, 2):
                tiles = []
                for k in (0, 1):
                    if r + k < count:
                        at = (first + r + k) * PC + start
                        tiles.append(ct_ref[at : at + 16, :].astype(F32)[half])
                    else:
                        tiles.append(jnp.zeros((8, F), F32))
                at = ct_at + r * 8
                out[at : at + 16, :] = jnp.concatenate(tiles, 0).astype(BF)
        first, count = off_rows(di)
        part = wide[first : first + count, :]
        lanes = lane[0:count]
        if dj < 0:
            part = jnp.where(lanes < HC, part, 0.0)
        elif dj > 0:
            part = jnp.where(lanes < HC, rolled(part, HC - C, 1), 0.0)
        high = part.astype(BF).astype(F32)
        left = part - high
        middle = left.astype(BF).astype(F32)
        low = left - middle
        if di == 0:
            packed = jnp.concatenate([high, middle, low], 0)
        else:
            packed = jnp.concatenate([high, middle, low, jnp.zeros_like(low)], 0)
        packed = jnp.concatenate([packed, jnp.zeros_like(packed)], 1)
        out[off_at : off_at + packed.shape[0], :] = packed.astype(BF)


def packed_messages(pixels, cotangent, offsets):
    shapes = [jax.ShapeDtypeStruct((message_parts(*side)[2], F), BF) for side in SIDES]
    return pl.pallas_call(
        pack_kernel,
        out_shape=shapes,
        scratch_shapes=[pltpu.VMEM((R, 128), F32)],
        name="pack",
    )(pixels, cotangent, offsets)


def exchanged(messages):
    rows = lax.axis_size(GRP)
    cols = lax.axis_size(DEV)
    got = []
    for di, dj in SIDES:
        pairs = []
        for i in range(rows):
            for j in range(cols):
                if 0 <= i + di < rows and 0 <= j + dj < cols:
                    pairs.append(((i + di) * cols + j + dj, i * cols + j))
        got.append(lax.ppermute(messages[SIDES.index((-di, -dj))], EVERY, pairs))
    return got


def inverse_roots(h, inside):
    degree = jnp.zeros_like(h)
    for row_step, col_step, coupling in STEPS:
        other = rolled(rolled(h, -row_step, 0), -col_step, 1)
        present = rolled(rolled(inside, -row_step, 0), -col_step, 1)
        degree = degree + coupling * present * jnp.exp(-(h - other) * (h - other))
    return lax.rsqrt(degree + 1.0 - inside) * inside


def couplings(row_gap, col_gap):
    near = jnp.abs(col_gap)
    side = jnp.where(near == 0, 1.0, jnp.where(near == 1, 0.5, 0.0))
    own = jnp.where(near == 1, 1.0, 0.0)
    return jnp.where(row_gap == 0, own, jnp.where(jnp.abs(row_gap) == 1, side, 0.0))


def fine_windows(x):
    lane = lax.broadcasted_iota(jnp.int32, x.shape, 1)
    over = rolled(x, EC, 1)
    low = jnp.where(lane < EC, rolled(x, 1, 0), over)
    high = jnp.where(lane < 2 * EC - 128, over, rolled(rolled(x, -1, 0), 2 * EC - 128, 1))
    return jnp.concatenate([low, high], 1)


def pooled_windows(x):
    lane = lax.broadcasted_iota(jnp.int32, x.shape, 1)
    rows = [rolled(rolled(x, 1 - j, 0), QC * j, 1) for j in range(6)]
    low = jnp.where(
        lane < QC,
        rows[0],
        jnp.where(lane < 2 * QC, rows[1], jnp.where(lane < 3 * QC, rows[2], rows[3])),
    )
    high = jnp.where(
        lane < 4 * QC - 128,
        rows[3],
        jnp.where(
            lane < 5 * QC - 128, rows[4], jnp.where(lane < 6 * QC - 128, rows[5], 0.0)
        ),
    )
    return jnp.concatenate([low, high], 1)


def transposed(x):
    if x.shape[0] < 128:
        x = jnp.concatenate([x, jnp.zeros((128 - x.shape[0], 128), F32)], 0)
    return x.T


def main_kernel(px_ref, ct_ref, off_ref, w1_ref, w2_ref, *rest):
    got = dict(zip(SIDES, rest[:8]))
    level_ref, sums_ref, table_ref, grad_ref = rest[8:12]
    (h_ref, hw_ref, sw_ref, pxe_ref, f1_ref, f2_ref, f1c_ref, f2c_ref, slope_ref, hid_ref,
     poolf_ref, p1f_ref, p2f_ref, ctf_ref, ptab_ref, pb_ref, p1b_ref, ctb_ref, topb_ref,
     midf_ref, midb_ref, pgf_ref, sp_ref, agc_ref, low_ref) = rest[12:]

    row0 = (lax.axis_index("grp_0") * 2 + lax.axis_index("grp_1")) * R
    col0 = (lax.axis_index("dev_0") * lax.axis_size("dev_1") + lax.axis_index("dev_1")) * C
    rows_all = lax.axis_size("grp_0") * lax.axis_size("grp_1") * R
    cols_all = lax.axis_size("dev_0") * lax.axis_size("dev_1") * C

    h_ref[...] = jnp.zeros_like(h_ref)
    h_ref[8 : 8 + R, 0:C] = off_ref[...]

    def offsets_of(side):
        ref = got[side]
        _, at, end = message_parts(*side)
        all_parts = ref[at:end, 0:128].astype(F32)
        n = R if side[0] == 0 else 8
        return all_parts[0:n] + all_parts[n : 2 * n] + all_parts[2 * n : 3 * n]

    for di, at, n in ((-1, 0, 8), (0, 8, R), (1, 8 + R, 8)):
        middle = h_ref[at : at + n, :] if di == 0 else offsets_of((di, 0))
        h_ref[at : at + n, :] = (
            offsets_of((di, -1)) + rolled(middle, HC, 1) + rolled(offsets_of((di, 1)), HC + C, 1)
        )
    h = h_ref[...]
    q = lax.broadcasted_iota(jnp.int32, (OR, 128), 0)
    c = lax.broadcasted_iota(jnp.int32, (OR, 128), 1)
    row_id = row0 - 8 + q
    col_id = col0 - HC + c
    inside = (
        (row_id >= 0) & (row_id < rows_all) & (col_id >= 0) & (col_id < cols_all) & (c < EC)
    ).astype(F32)
    s = inverse_roots(h, inside)

    pick_r = lax.broadcasted_iota(jnp.int32, (OR // 2, OR), 1) // 2
    pick_r = jnp.where(pick_r == lax.broadcasted_iota(jnp.int32, (OR // 2, OR), 0), 0.5, 0.0)
    pick_c = lax.broadcasted_iota(jnp.int32, (128, 128), 0) // 2
    pick_c = jnp.where(pick_c == lax.broadcasted_iota(jnp.int32, (128, 128), 1), 0.5, 0.0)
    ph = jnp.dot(pick_r, h, precision=lax.Precision.HIGHEST, preferred_element_type=F32)
    ph = jnp.dot(ph, pick_c, precision=lax.Precision.HIGHEST, preferred_element_type=F32)
    pq = lax.broadcasted_iota(jnp.int32, (OR // 2, 128), 0)
    pc = lax.broadcasted_iota(jnp.int32, (OR // 2, 128), 1)
    prow = row0 // 2 - 4 + pq
    pcol = col0 // 2 - 4 + pc
    pinside = (
        (prow >= 0) & (prow < rows_all // 2) & (pcol >= 0) & (pcol < cols_all // 2) & (pc < QC)
    ).astype(F32)
    ps = inverse_roots(ph, pinside)

    hw_ref[0:OR, :] = fine_windows(h)
    sw_ref[0:OR, :] = fine_windows(s)
    hw_ref[OR : OR + OR // 2, :] = pooled_windows(ph)
    sw_ref[OR : OR + OR // 2, :] = pooled_windows(ps)
    ht, st = transposed(h), transposed(s)
    pht, pst = transposed(ph), transposed(ps)
    k = lax.broadcasted_iota(jnp.int32, (EC, 256), 1)
    i = lax.broadcasted_iota(jnp.int32, (EC, 256), 0)
    block = (k >= EC).astype(jnp.int32) + (k >= 2 * EC).astype(jnp.int32)
    link = -couplings(block - 1, k - block * EC - i)
    for r in range(1, ER - 1):
        at = r + 2
        gap = ht[0:EC, at : at + 1] - hw_ref[at : at + 1, :]
        scale = st[0:EC, at : at + 1] * sw_ref[at : at + 1, :]
        table = link * jnp.exp(-gap * gap) * scale
        table_ref[(r - 1) * EC : r * EC, :] = table.astype(BF)
    k = lax.broadcasted_iota(jnp.int32, (QC, 256), 1)
    i = lax.broadcasted_iota(jnp.int32, (QC, 256), 0)
    block = sum((k >= QC * j).astype(jnp.int32) for j in range(1, 6))
    plinks = [-couplings(block - 1 - j, k - block * QC - i) for j in range(4)]
    for b in range(3):
        at = 2 + 4 * b
        for j in (0, 2):
            both = []
            for jj in (j, j + 1):
                col = at + jj
                gap = pht[0:QC, col : col + 1] - hw_ref[OR + at : OR + at + 1, :]
                scale = pst[0:QC, col : col + 1] * sw_ref[OR + at : OR + at + 1, :]
                both.append(plinks[jj] * jnp.exp(-gap * gap) * scale)
            ptab_ref[b * 160 + j * QC : b * 160 + (j + 2) * QC, :] = jnp.concatenate(both, 0).astype(BF)

    for di, at, n in ((-1, 0, HR), (0, HR, R), (1, HR + R, HR)):
        lefts, rights = got[(di, -1)], got[(di, 1)]
        middles = px_ref if di == 0 else got[(di, 0)]
        for r in range(0, n, 2):
            left = lefts[r * 8 : r * 8 + 16, :].astype(F32)
            right = rights[r * 8 : r * 8 + 16, :].astype(F32)
            middle = middles[r * C : (r + 2) * C, :].astype(F32)
            lines = [left[0:8], middle[0:C], right[0:8], left[8:16], middle[C:], right[8:16]]
            row = (at + r) * EC
            pxe_ref[row : row + 2 * EC, :] = jnp.concatenate(lines, 0).astype(BF)

    for di, at, n in ((-1, 0, 3), (0, 3, PR), (1, 3 + PR, 3)):
        lefts, rights = got[(di, -1)], got[(di, 1)]
        side_at = message_parts(di, 1)[0]
        middles = ct_ref if di == 0 else got[(di, 0)]
        mid_at = 0 if di == 0 else message_parts(di, 0)[0]
        for r in range(0, n, 2):
            left = lefts[side_at + r * 8 : side_at + r * 8 + 16, :].astype(F32)
            right = rights[side_at + r * 8 : side_at + r * 8 + 16, :].astype(F32)
            for kk in range(min(2, n - r)):
                base = (at + r + kk) * QC
                ctf_ref[base : base + 4, :] = left[kk * 8 + 4 : kk * 8 + 8]
                from_at = mid_at + (r + kk) * PC
                ctf_ref[base + 4 : base + 4 + PC, :] = middles[from_at : from_at + PC, :].astype(F32)
                ctf_ref[base + 4 + PC : base + QC, :] = right[kk * 8 : kk * 8 + 4]
    ctb_ref[...] = ctf_ref[...].astype(BF)

    def table_of(r):
        return table_ref[(r - 1) * EC : r * EC, 0 : 3 * EC]

    for r in range(1, ER - 1):
        one = mm(table_of(r), pxe_ref[(r - 1) * EC : (r + 2) * EC, :])
        f1_ref[(r - 1) * EC : r * EC, :] = one.astype(BF)
        if HR <= r < HR + R:
            f1c_ref[(r - HR) * C : (r - HR + 1) * C, :] = one[HC : HC + C].astype(BF)
    for r in range(2, ER - 2):
        two = 2.0 * mm(table_of(r), f1_ref[(r - 2) * EC : (r + 1) * EC, :])
        two = two - pxe_ref[r * EC : (r + 1) * EC, :].astype(F32)
        f2_ref[(r - 2) * EC : (r - 1) * EC, :] = two.astype(BF)
        if HR <= r < HR + R:
            f2c_ref[(r - HR) * C : (r - HR + 1) * C, :] = two[HC : HC + C].astype(BF)
    poolf_ref[...] = jnp.zeros_like(poolf_ref)
    p1f_ref[...] = jnp.zeros_like(p1f_ref)
    midf_ref[...] = jnp.zeros_like(midf_ref)
    for b in range(6):
        r = 2 + 4 * b
        act = mm(pxe_ref[r * EC : (r + 4) * EC, :], w1_ref[0])
        act = act + mm(f1_ref[(r - 1) * EC : (r + 3) * EC, :], w1_ref[1])
        act = act + mm(f2_ref[(r - 2) * EC : (r + 2) * EC, :], w1_ref[2])
        sig = 1.0 / (1.0 + jnp.exp(-act))
        slope_ref[(r - 2) * EC : (r + 2) * EC, :] = sig * (1.0 + act * (1.0 - sig))
        hid = act * sig
        for n in (0, 1):
            half = hid[:, n * 128 : (n + 1) * 128]
            ref = hid_ref.at[2 * b + n]
            ref[0:EC, :] = half[0:EC] + half[EC : 2 * EC]
            ref[EC : 2 * EC, :] = half[2 * EC : 3 * EC] + half[3 * EC : 4 * EC]
            pooled = 0.25 * (ref[pl.ds(0, EC, stride=2), :] + ref[pl.ds(1, EC, stride=2), :])
            pooled = pooled.astype(BF).astype(F32)
            poolf_ref[(1 + 2 * b) * QC : (3 + 2 * b) * QC, n * 128 : (n + 1) * 128] = pooled
    pb_ref[...] = poolf_ref[...].astype(BF)

    def ptable_of(b):
        return ptab_ref[b * 160 : (b + 1) * 160, 0 : 6 * QC]

    for b in range(3):
        one = mm(ptable_of(b), pb_ref[b * 160 : b * 160 + 6 * QC, :])
        p1f_ref[(1 + 4 * b) * QC : (5 + 4 * b) * QC, :] = one
    p1b_ref[...] = p1f_ref[...].astype(BF)
    for b in range(3):
        two = 2.0 * mm(ptable_of(b), p1b_ref[b * 160 : b * 160 + 6 * QC, :])
        lines = slice((1 + 4 * b) * QC, (5 + 4 * b) * QC)
        p2f_ref[lines, :] = two - poolf_ref[lines, :]
    own = slice(3 * QC, 11 * QC)
    terms = [poolf_ref[own, :].astype(BF), p1f_ref[own, :].astype(BF), p2f_ref[own, :].astype(BF)]
    low_ref[...] = sum(mm(term, w2_ref[n]) for n, term in enumerate(terms))
    for r in range(PR):
        level_ref[r * PC : (r + 1) * PC, :] = low_ref[r * QC + 4 : r * QC + 4 + PC, :].astype(BF)
    col = lax.broadcasted_iota(jnp.int32, (QC, F), 0)
    keep = ((col >= 4) & (col < 4 + PC)).astype(F32)
    cot_own = (ctf_ref[own, :].reshape(PR, QC, F) * keep[None]).reshape(PR * QC, F).astype(BF)
    for n, term in enumerate(terms):
        sums_ref[(3 + n) * F : (4 + n) * F, :] = mm_tn(term, cot_own).astype(sums_ref.dtype)

    cot = ctb_ref[...]
    topb_ref[...] = mm_nt(cot, w2_ref[2]).astype(BF)
    from_one = mm_nt(cot, w2_ref[1])
    for b in range(3):
        lines = slice((1 + 4 * b) * QC, (5 + 4 * b) * QC)
        mid = 2.0 * mm(ptable_of(b), topb_ref[b * 160 : b * 160 + 6 * QC, :])
        midf_ref[lines, :] = from_one[lines] + mid
    midb_ref[...] = midf_ref[...].astype(BF)
    from_zero = mm_nt(cot, w2_ref[0]) - topb_ref[...].astype(F32)
    for b in range(3):
        lines = slice((1 + 4 * b) * QC, (5 + 4 * b) * QC)
        pgf_ref[lines, :] = from_zero[lines] + mm(ptable_of(b), midb_ref[b * 160 : b * 160 + 6 * QC, :])
    for b in range(5):
        u = 2 + 2 * b
        grad = 0.25 * pgf_ref[u * QC : (u + 2) * QC, :]
        for n in (0, 1):
            ref = sp_ref.at[2 * b + n]
            ref[pl.ds(0, 2 * QC, stride=2), :] = grad[:, n * 128 : (n + 1) * 128]
            ref[pl.ds(1, 2 * QC, stride=2), :] = grad[:, n * 128 : (n + 1) * 128]
        for n in range(4):
            r = 2 * u + n
            lines = slice((n // 2) * EC, (n // 2 + 1) * EC)
            spread = jnp.concatenate([sp_ref[2 * b, lines, :], sp_ref[2 * b + 1, lines, :]], 1)
            grad_row = spread * slope_ref[(r - 2) * EC : (r - 1) * EC, :]
            grad_ref[(r - 4) * EC : (r - 3) * EC, :] = grad_row.astype(BF)
            if HR <= r < HR + R:
                agc_ref[(r - HR) * C : (r - HR + 1) * C, :] = grad_row[HC : HC + C].astype(BF)
    for n, ref in enumerate((px_ref, f1c_ref, f2c_ref)):
        sums_ref[n * F : (n + 1) * F, :] = mm_tn(ref[...], agc_ref[...]).astype(sums_ref.dtype)


def main_stage(pixels, cotangent, offsets, first_weights, second_weights, got):
    fine, pooled = ER * EC, QR * QC
    scratch = [
        ((OR, 128), F32),
        ((OR + OR // 2, 256), F32),
        ((OR + OR // 2, 256), F32),
        ((fine, F), BF),
        ((26 * EC, F), BF),
        ((24 * EC, F), BF),
        ((R * C, F), BF),
        ((R * C, F), BF),
        ((24 * EC, F), F32),
        ((12, 2 * EC, 128), F32),
        ((pooled, F), F32),
        ((pooled, F), F32),
        ((pooled, F), F32),
        ((pooled, F), F32),
        ((480, 256), BF),
        ((pooled, F), BF),
        ((pooled, F), BF),
        ((pooled, F), BF),
        ((pooled, F), BF),
        ((pooled, F), F32),
        ((pooled, F), BF),
        ((pooled, F), F32),
        ((10, 2 * EC, 128), F32),
        ((R * C, F), BF),
        ((PR * QC, F), F32),
    ]
    return pl.pallas_call(
        main_kernel,
        out_shape=[
            jax.ShapeDtypeStruct((PR * PC, F), BF),
            jax.ShapeDtypeStruct((6 * F, F), BF),
            jax.ShapeDtypeStruct((26 * EC, 256), BF),
            jax.ShapeDtypeStruct((20 * EC, F), BF),
        ],
        scratch_shapes=[pltpu.VMEM(shape, dtype) for shape, dtype in scratch],
        compiler_params=pltpu.CompilerParams(vmem_limit_bytes=56 << 20),
        name="main",
    )(pixels, cotangent, offsets, first_weights, second_weights, *got)


def tail_kernel(table_ref, grad_ref, w_ref, out_ref, top_ref, mid_ref):
    top_ref[...] = mm_nt(grad_ref[...], w_ref[2]).astype(BF)
    for b in range(9):
        r = 5 + 2 * b
        base = mm_nt(grad_ref[(r - 4) * EC : (r - 2) * EC, :], w_ref[1])
        for n in (0, 1):
            table = table_ref[(r + n - 1) * EC : (r + n) * EC, 0 : 3 * EC]
            mid = 2.0 * mm(table, top_ref[(r + n - 5) * EC : (r + n - 2) * EC, :])
            mid = base[n * EC : (n + 1) * EC] + mid
            mid_ref[(r + n - 5) * EC : (r + n - 4) * EC, :] = mid.astype(BF)
    for b in range(8):
        r = 6 + 2 * b
        base = mm_nt(grad_ref[(r - 4) * EC : (r - 2) * EC, :], w_ref[0])
        base = base - top_ref[(r - 4) * EC : (r - 2) * EC, :].astype(F32)
        for n in (0, 1):
            table = table_ref[(r + n - 1) * EC : (r + n) * EC, 0 : 3 * EC]
            line = base[n * EC : (n + 1) * EC] + mm(table, mid_ref[(r + n - 6) * EC : (r + n - 3) * EC, :])
            at = (r + n - HR) * C
            out_ref[at : at + C, :] = line[HC : HC + C].astype(BF)


def tail_stage(table, grad, first_weights):
    return pl.pallas_call(
        tail_kernel,
        out_shape=jax.ShapeDtypeStruct((R * C, F), BF),
        scratch_shapes=[pltpu.VMEM((20 * EC, F), BF), pltpu.VMEM((18 * EC, F), BF)],
        compiler_params=pltpu.CompilerParams(vmem_limit_bytes=56 << 20),
        name="tail",
    )(table, grad, first_weights)


def sum_at_owner(value, axes):
    size = lax.axis_size(axes)
    tiles = lax.all_to_all(value.reshape(size, -1, F), axes, 0, 0, tiled=True)
    return jnp.sum(tiles.astype(F32), axis=0).astype(BF)


def sent_to_all(value, axes):
    copies = jnp.broadcast_to(value, (lax.axis_size(axes), *value.shape))
    return lax.all_to_all(copies, axes, 0, 0, tiled=True).reshape(-1, F)


def total_of(value):
    stages = (("grp_1", "dev_0"), ("grp_0", "dev_1"))
    for axes in stages:
        value = sum_at_owner(value, axes)
    for axes in stages[::-1]:
        value = sent_to_all(value, axes)
    return value


def clip_kernel(sums_ref, first_ref, second_ref):
    total = jnp.zeros((8, F), F32)
    for n in range(6):
        part = sums_ref[n * F : (n + 1) * F, :].astype(F32)
        total = total + jnp.sum((part * part).reshape(F // 8, 8, F), axis=0)
    square_sum = jnp.sum(jnp.sum(total, axis=1, keepdims=True), axis=0, keepdims=True)
    factor = jnp.minimum(1.0, 2.0 * F * lax.rsqrt(square_sum + 1e-06))
    for n in range(3):
        first_ref[n] = sums_ref[n * F : (n + 1) * F, :].astype(F32) * factor
        second_ref[n] = sums_ref[(3 + n) * F : (4 + n) * F, :].astype(F32) * factor


def clipped(sums):
    shape = jax.ShapeDtypeStruct((3, F, F), F32)
    return pl.pallas_call(clip_kernel, out_shape=[shape, shape], name="clip")(sums)


def shards(pixels, offsets, first_weights, second_weights, cotangent):
    px = pixels.reshape(R * C, F)
    ct = cotangent.reshape(PR * PC, F)
    got = exchanged(packed_messages(px, ct, offsets))
    level, sums, table, grad = main_stage(px, ct, offsets, first_weights, second_weights, got)
    first, second = clipped(total_of(sums))
    grad_pixels = tail_stage(table, grad, first_weights)
    return grad_pixels.reshape(R, C, F), first, second, level.reshape(PR, PC, F)


def solution(mesh):
    finer = Mesh(mesh.devices.reshape(-1, 2, 4, mesh.devices.shape[1] // 4), EVERY)
    in_specs = (P(GRP, DEV, None), P(GRP, DEV), P(), P(), P(GRP, DEV, None))
    out_specs = (P(GRP, DEV, None), P(), P(), P(GRP, DEV, None))
    return jax.shard_map(
        shards, mesh=finer, in_specs=in_specs, out_specs=out_specs, check_vma=False
    )
```

time: 222 us -> 133 us (0.60)
  starting transfers between devices: 63.9 us -> 31.5 us
  Pallas kernels: 0 us -> 16.5 us
  waiting for transfers between devices: 33.4 us -> 17.3 us
  local copies, waits for them, and re-layouts: 18.5 us -> 3.44 us
  blocking collectives: 77.1 us -> 62.8 us
  other arithmetic: 12.4 us -> 0.2 us
  matrix products: 10.2 us -> 0 us
  between operations: 3.76 us -> 0.81 us
    ppermute x20 -> x8, starting transfers between devices: 58.5 us -> 25 us  [exchanged(): got.append(lax.ppermute(messages[SIDES.index((-di, -dj))], EVERY, pairs))]
    ppermute x20 -> x8, waiting for transfers between devices: 33.4 us -> 9.37 us  [exchanged(): got.append(lax.ppermute(messages[SIDES.index((-di, -dj))], EVERY, pairs))]
    pallas_call x0 -> x4, Pallas kernels: none -> 16.5 us  [the longest x1 7.71 us: main_stage(): pl.pallas_call(main_kernel, out_shape=[jax.ShapeDtypeStruct((PR * PC, F),...]
    all_to_all x3, blocking collectives: 77.1 us -> 62.8 us  [the longest x2 47.2 us: sum_at_owner(): tiles = lax.all_to_all(value.reshape(size, -1, F), axes, 0, 0, tiled=True)]
    dot_general x10 -> x0, matrix products: 10.2 us -> none  [the longest x6 6.24 us: project_back(): jnp.dot(flattened, weights[order_index].T, preferred_element_type=jnp.flo...]
    slice x44 -> x0, local copies, waits for them, and re-layouts: 10 us -> none  [the longest x33 7.15 us: trim(): tensor[margin_cut:tensor.shape[0] - margin_cut, margin_cut:tensor.shape[1...]
    all_to_all x1, waiting for transfers between devices: 0.01 us -> 7.93 us  [sent_to_all(): return lax.all_to_all(copies, axes, 0, 0, tiled=True).reshape(-1, F)]
    mul x7 -> x0, other arithmetic: 4.64 us -> none  [the longest x4 4.28 us: apply_operator(): scaled = root_ext[:, :, None] * extended.astype(jnp.float32)]
  transfers between devices with their start and end apart: 21 -> 9, of which waited for: 6 -> 3; matrix products, arithmetic and copies ran while one was open for 10% -> 0% of each run, Pallas kernels for 0% -> 3%
where the time goes in v1:
time: 133 us
  blocking collectives  62.8 us (47%)
  starting transfers between devices  31.5 us (24%)
  waiting for transfers between devices  17.3 us (13%)
  Pallas kernels  16.5 us (12%)
  local copies, waits for them, and re-layouts  3.44 us (3%)
    all_to_all x2, blocking collectives, sum_at_owner(): tiles = lax.all_to_all(value.reshape(size, -1, F), axes, 0, 0, tiled=True)  47.2 us
    ppermute x8, starting transfers between devices, exchanged(): got.append(lax.ppermute(messages[SIDES.index((-di, -dj))], EVERY, pairs))  25 us
    all_to_all x1, blocking collectives, sent_to_all(): return lax.all_to_all(copies, axes, 0, 0, tiled=True).reshape(-1, F)  15.6 us
    ppermute x8, waiting for transfers between devices, exchanged(): got.append(lax.ppermute(messages[SIDES.index((-di, -dj))], EVERY, pairs))  9.37 us
    all_to_all x1, waiting for transfers between devices, sent_to_all(): return lax.all_to_all(copies, axes, 0, 0, tiled=True).reshape(-1, F)  7.93 us
    pallas_call x1, Pallas kernels, main_stage(): pl.pallas_call(main_kernel, out_shape=[jax.ShapeDtypeStruct((PR * PC, F),...  7.71 us
    all_to_all x1, starting transfers between devices, sent_to_all(): return lax.all_to_all(copies, axes, 0, 0, tiled=True).reshape(-1, F)  6.5 us
    pallas_call x1, Pallas kernels, tail_stage(): pl.pallas_call(tail_kernel, out_shape=jax.ShapeDtypeStruct((R * C, F), BF...  4.24 us
  transfers between devices with their start and end apart: 9, of which 3 were waited for; matrix products, arithmetic and copies ran while one was open for 0% of the time, Pallas kernels for 3%

profile of v1, /device:TPU:1, one launch (start us, length us, event | category | flops | bytes accessed | tf_op | source)
XLA Modules:
  0.0 132.5 jit_solution(4262921410329548768)
XLA Ops:
  0.6 2.1 %pack.1 = (bf16[512,256]{1,0:T(8,128)(2,1)}, bf16[512,256]{1,0:T(8,128)(2,1)}, bf16[240,256]{1,0:T(8,128)(2,1)}, bf16[240,256]{1,0:T(8,128)(2,1)}, bf16[112,256]...) custom-call(bf16[1024,256]{1,0:T(8,128)(2,1)} %bitcast.7, ...), custom_call_target="tpu_custom_call" | custom-call | tf_op jit(solution)/shard_map/pack/pallas_call | solution.py:129
  2.7 4.6 %collective-permute-start = (bf16[512,256]{1,0:T(8,128)(2,1)}, bf16[512,256]{1,0:T(8,128)(2,1)S(1)}, u32[]{:S(2)}, u32[]{:S(2)}) collective-permute-start(bf16[512,256]{1,0:T(8,128)(2,1)} %get-tuple-element.18), channel_id=1, source_target_pairs={{0,32},{1,33},{2,34},{3,35},{4,36},{5,37},{6,38},{7,39},{8,40},{9,... | collective-permute-start | bytes 786440 | tf_op jit(solution)/shard_map/ppermute | solution.py:147
  7.3 5.5 %collective-permute-start.1 = (bf16[512,256]{1,0:T(8,128)(2,1)}, bf16[512,256]{1,0:T(8,128)(2,1)S(1)}, u32[]{:S(2)}, u32[]{:S(2)}) collective-permute-start(bf16[512,256]{1,0:T(8,128)(2,1)} %get-tuple-element.19), channel_id=1, source_target_pairs={{32,0},{33,1},{34,2},{35,3},{36,4},{37,5},{38,6},{39,7},{40,8},{41... | collective-permute-start | bytes 786440 | tf_op jit(solution)/shard_map/ppermute | solution.py:147
  12.8 1.9 %collective-permute-start.4 = (bf16[112,256]{1,0:T(8,128)(2,1)}, bf16[112,256]{1,0:T(8,128)(2,1)S(1)}, u32[]{:S(2)}, u32[]{:S(2)}) collective-permute-start(bf16[112,256]{1,0:T(8,128)(2,1)} %get-tuple-element.22), channel_id=1, source_target_pairs={{0,33},{1,34},{2,35},{3,36},{4,37},{5,38},{6,39},{7,40},{8,41},{9,... | collective-permute-start | bytes 172040 | tf_op jit(solution)/shard_map/ppermute | solution.py:147
  14.7 1.3 collective-permute-start.5
  16.0 4.6 %collective-permute-start.2 = (bf16[240,256]{1,0:T(8,128)(2,1)}, bf16[240,256]{1,0:T(8,128)(2,1)S(1)}, u32[]{:S(2)}, u32[]{:S(2)}) collective-permute-start(bf16[240,256]{1,0:T(8,128)(2,1)} %get-tuple-element.20), channel_id=1, source_target_pairs={{0,1},{1,2},{2,3},{3,4},{4,5},{5,6},{6,7},{7,8},{8,9},{9,10},{10,1... | collective-permute-start | bytes 368648 | tf_op jit(solution)/shard_map/ppermute | solution.py:147
  20.6 0.0 collective-permute-done.4.rest_4_
  20.6 0.0 copy-start.5
  20.7 1.3 collective-permute-start.3
  22.0 0.0 collective-permute-done.5.rest_5_
  22.0 0.0 copy-start.6
  22.0 4.5 %collective-permute-start.6 = (bf16[112,256]{1,0:T(8,128)(2,1)}, bf16[112,256]{1,0:T(8,128)(2,1)S(1)}, u32[]{:S(2)}, u32[]{:S(2)}) collective-permute-start(bf16[112,256]{1,0:T(8,128)(2,1)} %get-tuple-element.24), channel_id=1, source_target_pairs={{32,1},{33,2},{34,3},{35,4},{36,5},{37,6},{38,7},{39,8},{40,9},{41... | collective-permute-start | bytes 172040 | tf_op jit(solution)/shard_map/ppermute | solution.py:147
  26.5 1.6 %collective-permute-done.6.rest_6_ = bf16[112,256]{1,0:T(8,128)(2,1)S(1)} collective-permute-done((bf16[112,256]{1,0:T(8,128)(2,1)}, bf16[112,256]{1,0:T(8,128)(2,1)S(1)}, u32[]{:S(2)}, u32[]{:S(2)}) %collective-permute-start.6) | collective-permute-done | bytes 57376 | tf_op jit(solution)/shard_map/ppermute | solution.py:147
  28.1 0.0 copy-start.7
  28.1 1.3 collective-permute-start.7
  29.4 7.8 %collective-permute-done.7.rest_7_ = bf16[112,256]{1,0:T(8,128)(2,1)S(1)} collective-permute-done((bf16[112,256]{1,0:T(8,128)(2,1)}, bf16[112,256]{1,0:T(8,128)(2,1)S(1)}, u32[]{:S(2)}, u32[]{:S(2)}) %collective-permute-start.7) | collective-permute-done | bytes 57376 | tf_op jit(solution)/shard_map/ppermute | solution.py:147
  37.2 0.0 copy-start.8
  37.2 0.0 collective-permute-done.2.rest_2_
  37.2 0.0 copy-start.3
  37.2 0.0 collective-permute-done.3.rest_3_
  37.2 0.0 copy-start.4
  37.2 0.0 collective-permute-done.rest_0_
  37.2 0.0 copy-start.1
  37.2 0.0 collective-permute-done.1.rest_1_
  37.2 0.0 copy-done.5
  37.2 0.0 copy-done.6
  37.2 0.0 copy-done.7
  37.3 0.5 copy-done.8
  37.8 0.1 copy-done.3
  37.8 0.1 copy-done.4
  37.9 0.1 copy-done.1
  38.0 0.0 copy-start.2
  38.0 0.7 copy-done.2
  38.7 7.7 %main.1 = (bf16[256,256]{1,0:T(8,128)(2,1)}, bf16[1536,256]{1,0:T(8,128)(2,1)}, bf16[2080,256]{1,0:T(8,128)(2,1)}, bf16[1600,256]{1,0:T(8,128)(2,1)}) custom-call(bf16[1024,256]{1,0:T(8,128)(2,1)} %bitcast.8, bf16[256,256]{1,0:T(8,128)(2,1)} %bitcast.11, f32[16,64]{1,0:T(8,128)} %off_ref.3, bf16[3,256,256]{2,1,0:T(8,128)(2,1)} %w_ref.1, ...), custom_call_target="tpu_custom_call" | custom-call | tf_op jit(solution)/shard_map/main/pallas_call | solution.py:426
  46.4 25.4 %all_to_all.20 = bf16[8,192,256]{2,1,0:T(8,128)(2,1)S(1)} all-to-all(bf16[8,192,256]{2,1,0:T(8,128)(2,1)} %bitcast.9), channel_id=1, replica_groups=mesh['grp_0'=8,'grp_1'=2,'dev_0'=4,'dev_1'=8] {'grp_1','dev_0'}, dimensions={0} | all-to-all | bytes 1572864 | tf_op jit(solution)/shard_map/all_to_all | solution.py:473
  71.8 0.1 reduce_sum.24
  71.9 0.1 reshape.36
  72.0 21.8 %all_to_all.21 = bf16[64,3,256]{2,1,0:T(4,128)(2,1)S(1)} all-to-all(bf16[64,3,256]{2,1,0:T(4,128)(2,1)S(1)} %reshape.36), channel_id=1, replica_groups=mesh['grp_0'=8,'grp_1'=2,'dev_0'=4,'dev_1'=8] {'grp_0','dev_1'}, dimensions={0} | all-to-all | bytes 196608 | tf_op jit(solution)/shard_map/all_to_all | solution.py:473
  93.7 0.1 reduce_sum.25
  93.9 15.6 %all_to_all.22 = bf16[64,3,256]{2,1,0:T(4,128)(2,1)S(1)} all-to-all(bf16[64,3,256]{2,1,0:T(4,128)(2,1)S(1)} %broadcast_in_dim.6), channel_id=1, replica_groups=mesh['grp_0'=8,'grp_1'=2,'dev_0'=4,'dev_1'=8] {'grp_0','dev_1'}, dimensions={0} | all-to-all | bytes 196608 | tf_op jit(solution)/shard_map/all_to_all | solution.py:479
  109.5 0.1 reshape.37
  109.6 0.9 broadcast_in_dim.7
  110.5 6.5 %all-to-all-start.3 = ((bf16[8,192,256]{2,1,0:T(8,128)(2,1)}), bf16[8,192,256]{2,1,0:T(8,128)(2,1)S(1)}, u32[]{:S(2)}, u32[]{:S(2)}) async-start(bf16[8,192,256]{2,1,0:T(8,128)(2,1)} %broadcast_in_dim.7), calls=%async_computation.3 | async-start | bytes 1572864 | tf_op jit(solution)/shard_map/all_to_all | solution.py:479
  117.0 4.2 %tail.1 = bf16[1024,256]{1,0:T(8,128)(2,1)} custom-call(bf16[2080,256]{1,0:T(8,128)(2,1)} %get-tuple-element.26.table_ref, bf16[1600,256]{1,0:T(8,128)(2,1)} %get-tuple-element.27.grad_ref, bf16[3,256,256]{2,1,0:T(8,128)(2,1)} %w_ref.1), custom_call_target="tpu_custom_call" | custom-call | tf_op jit(solution)/shard_map/tail/pallas_call | solution.py:462
  121.3 7.9 %all-to-all-done.3 = bf16[8,192,256]{2,1,0:T(8,128)(2,1)S(1)} async-done(((bf16[8,192,256]{2,1,0:T(8,128)(2,1)}), bf16[8,192,256]{2,1,0:T(8,128)(2,1)S(1)}, u32[]{:S(2)}, u32[]{:S(2)}) %all-to-all-start.3) | async-done | bytes 786464 | tf_op jit(solution)/shard_map/all_to_all | solution.py:479
  129.2 0.0 copy-start
  129.2 0.9 copy-done
  130.1 2.5 %clip.1 = (f32[3,256,256]{2,1,0:T(8,128)}, f32[3,256,256]{2,1,0:T(8,128)}) custom-call(bf16[1536,256]{1,0:T(8,128)(2,1)} %bitcast.6), custom_call_target="tpu_custom_call" | custom-call | tf_op jit(solution)/shard_map/clip/pallas_call | solution.py:505
  (1 shorter events, 0.0 us)
Async XLA Ops:
  2.7 34.5 %collective-permute-start = (bf16[512,256]{1,0:T(8,128)(2,1)}, bf16[512,256]{1,0:T(8,128)(2,1)S(1)}, u32[]{:S(2)}, u32[]{:S(2)}) collective-permute-start(bf16[512,256]{1,0:T(8,128)(2,1)} %get-tuple-element.18), channel_id=1, source_target_pairs={{0,32},{1,33},{2,34},{3,35},{4,36},{5,37},{6,38},{7,39},{8,40},{9,... | collective-permute-start | bytes 786440 | tf_op jit(solution)/shard_map/ppermute | solution.py:147
  7.3 29.9 %collective-permute-start.1 = (bf16[512,256]{1,0:T(8,128)(2,1)}, bf16[512,256]{1,0:T(8,128)(2,1)S(1)}, u32[]{:S(2)}, u32[]{:S(2)}) collective-permute-start(bf16[512,256]{1,0:T(8,128)(2,1)} %get-tuple-element.19), channel_id=1, source_target_pairs={{32,0},{33,1},{34,2},{35,3},{36,4},{37,5},{38,6},{39,7},{40,8},{41... | collective-permute-start | bytes 786440 | tf_op jit(solution)/shard_map/ppermute | solution.py:147
  12.8 7.8 %collective-permute-start.4 = (bf16[112,256]{1,0:T(8,128)(2,1)}, bf16[112,256]{1,0:T(8,128)(2,1)S(1)}, u32[]{:S(2)}, u32[]{:S(2)}) collective-permute-start(bf16[112,256]{1,0:T(8,128)(2,1)} %get-tuple-element.22), channel_id=1, source_target_pairs={{0,33},{1,34},{2,35},{3,36},{4,37},{5,38},{6,39},{7,40},{8,41},{9,... | collective-permute-start | bytes 172040 | tf_op jit(solution)/shard_map/ppermute | solution.py:147
  14.7 7.3 %collective-permute-start.5 = (bf16[112,256]{1,0:T(8,128)(2,1)}, bf16[112,256]{1,0:T(8,128)(2,1)S(1)}, u32[]{:S(2)}, u32[]{:S(2)}) collective-permute-start(bf16[112,256]{1,0:T(8,128)(2,1)} %get-tuple-element.23), channel_id=1, source_target_pairs={{1,32},{2,33},{3,34},{4,35},{5,36},{6,37},{7,38},{8,39},{9,40},{10... | collective-permute-start | bytes 172040 | tf_op jit(solution)/shard_map/ppermute | solution.py:147
  16.0 21.2 %collective-permute-start.2 = (bf16[240,256]{1,0:T(8,128)(2,1)}, bf16[240,256]{1,0:T(8,128)(2,1)S(1)}, u32[]{:S(2)}, u32[]{:S(2)}) collective-permute-start(bf16[240,256]{1,0:T(8,128)(2,1)} %get-tuple-element.20), channel_id=1, source_target_pairs={{0,1},{1,2},{2,3},{3,4},{4,5},{5,6},{6,7},{7,8},{8,9},{9,10},{10,1... | collective-permute-start | bytes 368648 | tf_op jit(solution)/shard_map/ppermute | solution.py:147
  20.6 16.6 %copy-start.5 = (bf16[112,256]{1,0:T(8,128)(2,1)}, bf16[112,256]{1,0:T(8,128)(2,1)S(1)}, u32[]{:S(2)}) copy-start(bf16[112,256]{1,0:T(8,128)(2,1)S(1)} %collective-permute-done.4.rest_4_) | copy-start | bytes 172036
  20.7 16.5 %collective-permute-start.3 = (bf16[240,256]{1,0:T(8,128)(2,1)}, bf16[240,256]{1,0:T(8,128)(2,1)S(1)}, u32[]{:S(2)}, u32[]{:S(2)}) collective-permute-start(bf16[240,256]{1,0:T(8,128)(2,1)} %get-tuple-element.21), channel_id=1, source_target_pairs={{1,0},{2,1},{3,2},{4,3},{5,4},{6,5},{7,6},{8,7},{9,8},{10,9},{11,1... | collective-permute-start | bytes 368648 | tf_op jit(solution)/shard_map/ppermute | solution.py:147
  22.0 15.3 %copy-start.6 = (bf16[112,256]{1,0:T(8,128)(2,1)}, bf16[112,256]{1,0:T(8,128)(2,1)S(1)}, u32[]{:S(2)}) copy-start(bf16[112,256]{1,0:T(8,128)(2,1)S(1)} %collective-permute-done.5.rest_5_) | copy-start | bytes 172036
  22.0 6.1 %collective-permute-start.6 = (bf16[112,256]{1,0:T(8,128)(2,1)}, bf16[112,256]{1,0:T(8,128)(2,1)S(1)}, u32[]{:S(2)}, u32[]{:S(2)}) collective-permute-start(bf16[112,256]{1,0:T(8,128)(2,1)} %get-tuple-element.24), channel_id=1, source_target_pairs={{32,1},{33,2},{34,3},{35,4},{36,5},{37,6},{38,7},{39,8},{40,9},{41... | collective-permute-start | bytes 172040 | tf_op jit(solution)/shard_map/ppermute | solution.py:147
  28.1 9.2 %copy-start.7 = (bf16[112,256]{1,0:T(8,128)(2,1)}, bf16[112,256]{1,0:T(8,128)(2,1)S(1)}, u32[]{:S(2)}) copy-start(bf16[112,256]{1,0:T(8,128)(2,1)S(1)} %collective-permute-done.6.rest_6_) | copy-start | bytes 172036
  28.1 9.1 %collective-permute-start.7 = (bf16[112,256]{1,0:T(8,128)(2,1)}, bf16[112,256]{1,0:T(8,128)(2,1)S(1)}, u32[]{:S(2)}, u32[]{:S(2)}) collective-permute-start(bf16[112,256]{1,0:T(8,128)(2,1)} %get-tuple-element.25), channel_id=1, source_target_pairs={{33,0},{34,1},{35,2},{36,3},{37,4},{38,5},{39,6},{40,7},{41,8},{42... | collective-permute-start | bytes 172040 | tf_op jit(solution)/shard_map/ppermute | solution.py:147
  37.2 0.6 copy-start.8
  37.2 0.7 copy-start.3
  37.2 0.7 copy-start.4
  37.2 0.8 copy-start.1
  38.0 0.7 copy-start.2
  110.5 18.7 %all-to-all-start.3 = ((bf16[8,192,256]{2,1,0:T(8,128)(2,1)}), bf16[8,192,256]{2,1,0:T(8,128)(2,1)S(1)}, u32[]{:S(2)}, u32[]{:S(2)}) async-start(bf16[8,192,256]{2,1,0:T(8,128)(2,1)} %broadcast_in_dim.7), calls=%async_computation.3 | async-start | bytes 1572864 | tf_op jit(solution)/shard_map/all_to_all | solution.py:479
  129.2 0.9 copy-start

commit v2 on v1

--- a/solution.py
+++ b/solution.py
@@ -21,7 +21,6 @@
 QR, QC = PR + 6, PC + 8
 OR = R + 16
 
-SIDES = ((-1, 0), (1, 0), (0, -1), (0, 1), (-1, -1), (-1, 1), (1, -1), (1, 1))
 STEPS = (
     (-1, 0, 1.0),
     (1, 0, 1.0),
@@ -46,106 +45,106 @@
     return lax.dot_general(a, b, (((0,), (0,)), ((), ())), preferred_element_type=F32)
 
 
-def px_rows(di):
-    return {-1: (0, HR), 1: (R - HR, HR), 0: (0, R)}[di]
-
-
-def ct_rows(di):
-    return {-1: (0, 3), 1: (PR - 3, 3), 0: (0, PR)}[di]
-
-
-def off_rows(di):
-    return {-1: (0, 8), 1: (R - 8, 8), 0: (0, R)}[di]
-
-
-def message_parts(di, dj):
-    px = px_rows(di)[1] * (HC if dj else C)
-    ct = ct_rows(di)[1] * (8 if dj else PC)
-    ct += -ct % 16
-    off = 48 if di == 0 else 32
-    return px, px + ct, px + ct + off
+ROW_CT = HR * C
+ROW_OFF = ROW_CT + 3 * PC
+ROW_END = ROW_OFF + 32
+COL_CT = ER * HC
+COL_OFF = COL_CT + 64
+COL_END = COL_OFF + OR
 
 
 def rolled(x, shift, axis):
     return pltpu.roll(x, shift % x.shape[axis], axis)
 
 
-def pack_kernel(px_ref, ct_ref, off_ref, *rest):
-    outs, wide = rest[:8], rest[8]
+def in_parts(x):
+    high = x.astype(BF).astype(F32)
+    left = x - high
+    middle = left.astype(BF).astype(F32)
+    return high, middle, left - middle
+
+
+def row_pack_kernel(px_ref, ct_ref, off_ref, up_ref, down_ref, wide):
     wide[...] = jnp.zeros_like(wide)
     wide[:, 0:C] = off_ref[...]
-    lane = lax.broadcasted_iota(jnp.int32, (R, 128), 1)
-    for (di, dj), out in zip(SIDES, outs):
-        ct_at, off_at, _ = message_parts(di, dj)
-        first, count = px_rows(di)
-        if dj == 0:
-            out[0 : count * C, :] = px_ref[first * C : (first + count) * C, :]
-        else:
-            start = 0 if dj < 0 else C - 16
-            half = slice(0, 8) if dj < 0 else slice(8, 16)
-            for r in range(0, count, 2):
+    for out, px_at, ct_at, off_at in ((up_ref, 0, 0, 0), (down_ref, R - HR, PR - 3, R - 8)):
+        out[0:ROW_CT, :] = px_ref[px_at * C : (px_at + HR) * C, :]
+        out[ROW_CT:ROW_OFF, :] = ct_ref[ct_at * PC : (ct_at + 3) * PC, :]
+        high, middle, low = in_parts(wide[off_at : off_at + 8, :])
+        packed = jnp.concatenate([high, middle, low, jnp.zeros_like(low)], 0)
+        out[ROW_OFF:ROW_END, :] = jnp.concatenate([packed, jnp.zeros_like(packed)], 1).astype(BF)
+
+
+def row_messages(pixels, cotangent, offsets):
+    shape = jax.ShapeDtypeStruct((ROW_END, F), BF)
+    return pl.pallas_call(
+        row_pack_kernel,
+        out_shape=[shape, shape],
+        scratch_shapes=[pltpu.VMEM((R, 128), F32)],
+        name="row_pack",
+    )(pixels, cotangent, offsets)
+
+
+def row_offsets(ref):
+    parts = ref[ROW_OFF:ROW_END, 0:128].astype(F32)
+    return parts[0:8] + parts[8:16] + parts[16:24]
+
+
+def col_pack_kernel(px_ref, ct_ref, off_ref, above_ref, below_ref, left_ref, right_ref, wide):
+    wide[...] = jnp.zeros_like(wide)
+    wide[8 : 8 + R, 0:C] = off_ref[...]
+    wide[0:8, :] = row_offsets(above_ref)
+    wide[8 + R : OR, :] = row_offsets(below_ref)
+    lane = lax.broadcasted_iota(jnp.int32, (OR, 128), 1)
+    near = lax.broadcasted_iota(jnp.int32, (8, F), 0) < 4
+    for out, px_at, ct_at, half in (
+        (left_ref, 0, 0, slice(0, 8)),
+        (right_ref, C - 16, PC - 16, slice(8, 16)),
+    ):
+        for first, n, ref in ((0, HR, above_ref), (HR, R, px_ref), (HR + R, HR, below_ref)):
+            for r in range(0, n, 2):
                 tiles = []
-                for k in (0, 1):
-                    at = (first + r + k) * C + start
-                    tiles.append(px_ref[at : at + 16, :].astype(F32)[half])
-                out[r * 8 : r * 8 + 16, :] = jnp.concatenate(tiles, 0).astype(BF)
-        first, count = ct_rows(di)
-        if dj == 0:
-            out[ct_at : ct_at + count * PC, :] = ct_ref[first * PC : (first + count) * PC, :]
-        else:
-            start = 0 if dj < 0 else PC - 16
-            half = slice(0, 8) if dj < 0 else slice(8, 16)
-            for r in range(0, count, 2):
-                tiles = []
-                for k in (0, 1):
-                    if r + k < count:
-                        at = (first + r + k) * PC + start
-                        tiles.append(ct_ref[at : at + 16, :].astype(F32)[half])
-                    else:
-                        tiles.append(jnp.zeros((8, F), F32))
-                at = ct_at + r * 8
+                for k in (r, r + 1):
+                    at = k * C + px_at
+                    tiles.append(ref[at : at + 16, :].astype(F32)[half])
+                at = (first + r) * HC
                 out[at : at + 16, :] = jnp.concatenate(tiles, 0).astype(BF)
-        first, count = off_rows(di)
-        part = wide[first : first + count, :]
-        lanes = lane[0:count]
-        if dj < 0:
-            part = jnp.where(lanes < HC, part, 0.0)
-        elif dj > 0:
-            part = jnp.where(lanes < HC, rolled(part, HC - C, 1), 0.0)
-        high = part.astype(BF).astype(F32)
-        left = part - high
-        middle = left.astype(BF).astype(F32)
-        low = left - middle
-        if di == 0:
-            packed = jnp.concatenate([high, middle, low], 0)
-        else:
-            packed = jnp.concatenate([high, middle, low, jnp.zeros_like(low)], 0)
-        packed = jnp.concatenate([packed, jnp.zeros_like(packed)], 1)
-        out[off_at : off_at + packed.shape[0], :] = packed.astype(BF)
-
-
-def packed_messages(pixels, cotangent, offsets):
-    shapes = [jax.ShapeDtypeStruct((message_parts(*side)[2], F), BF) for side in SIDES]
+        lines = []
+        for base, n, ref in ((ROW_CT, 3, above_ref), (0, PR, ct_ref), (ROW_CT, 3, below_ref)):
+            for r in range(n):
+                at = base + r * PC + ct_at
+                lines.append(ref[at : at + 16, :].astype(F32)[half])
+        tiles = []
+        for e in range(0, QR, 2):
+            first, second = lines[e], lines[e + 1]
+            if out is left_ref:
+                second = rolled(second, 4, 0)
+            else:
+                first = rolled(first, 4, 0)
+            tiles.append(jnp.where(near, first, second))
+        tiles.append(jnp.zeros((8, F), F32))
+        out[COL_CT:COL_OFF, :] = jnp.concatenate(tiles, 0).astype(BF)
+        part = wide[...] if out is left_ref else rolled(wide[...], HC - C, 1)
+        high, middle, low = in_parts(jnp.where(lane < HC, part, 0.0))
+        packed = high + rolled(middle, HC, 1) + rolled(low, 2 * HC, 1)
+        out[COL_OFF:COL_END, :] = jnp.concatenate([packed, jnp.zeros_like(packed)], 1).astype(BF)
+
+
+def col_messages(pixels, cotangent, offsets, above, below):
+    shape = jax.ShapeDtypeStruct((COL_END, F), BF)
     return pl.pallas_call(
-        pack_kernel,
-        out_shape=shapes,
-        scratch_shapes=[pltpu.VMEM((R, 128), F32)],
-        name="pack",
-    )(pixels, cotangent, offsets)
-
-
-def exchanged(messages):
-    rows = lax.axis_size(GRP)
-    cols = lax.axis_size(DEV)
-    got = []
-    for di, dj in SIDES:
-        pairs = []
-        for i in range(rows):
-            for j in range(cols):
-                if 0 <= i + di < rows and 0 <= j + dj < cols:
-                    pairs.append(((i + di) * cols + j + dj, i * cols + j))
-        got.append(lax.ppermute(messages[SIDES.index((-di, -dj))], EVERY, pairs))
-    return got
+        col_pack_kernel,
+        out_shape=[shape, shape],
+        scratch_shapes=[pltpu.VMEM((OR, 128), F32)],
+        name="col_pack",
+    )(pixels, cotangent, offsets, above, below)
+
+
+def exchanged(first, last, axis):
+    count = lax.axis_size(axis)
+    forward = [(i, i + 1) for i in range(count - 1)]
+    backward = [(i + 1, i) for i in range(count - 1)]
+    return lax.ppermute(last, axis, forward), lax.ppermute(first, axis, backward)
 
 
 def inverse_roots(h, inside):
@@ -190,18 +189,28 @@
     return jnp.concatenate([low, high], 1)
 
 
+def in_two(x):
+    high = x.astype(BF)
+    return jnp.concatenate([high, (x - high.astype(F32)).astype(BF)], 0)
+
+
+def applied(table, values):
+    both = mm(table, values)
+    half = both.shape[0] // 2
+    return both[0:half] + both[half:]
+
+
 def transposed(x):
     if x.shape[0] < 128:
         x = jnp.concatenate([x, jnp.zeros((128 - x.shape[0], 128), F32)], 0)
     return x.T
 
 
-def main_kernel(px_ref, ct_ref, off_ref, w1_ref, w2_ref, *rest):
-    got = dict(zip(SIDES, rest[:8]))
-    level_ref, sums_ref, table_ref, grad_ref = rest[8:12]
+def main_kernel(px_ref, ct_ref, off_ref, w1_ref, w2_ref, above_ref, below_ref, left_ref, right_ref, *rest):
+    level_ref, sums_ref, table_ref, grad_ref = rest[:4]
     (h_ref, hw_ref, sw_ref, pxe_ref, f1_ref, f2_ref, f1c_ref, f2c_ref, slope_ref, hid_ref,
      poolf_ref, p1f_ref, p2f_ref, ctf_ref, ptab_ref, pb_ref, p1b_ref, ctb_ref, topb_ref,
-     midf_ref, midb_ref, pgf_ref, sp_ref, agc_ref, low_ref) = rest[12:]
+     midf_ref, midb_ref, pgf_ref, sp_ref, agc_ref, low_ref) = rest[4:]
 
     row0 = (lax.axis_index("grp_0") * 2 + lax.axis_index("grp_1")) * R
     col0 = (lax.axis_index("dev_0") * lax.axis_size("dev_1") + lax.axis_index("dev_1")) * C
@@ -210,19 +219,17 @@
 
     h_ref[...] = jnp.zeros_like(h_ref)
     h_ref[8 : 8 + R, 0:C] = off_ref[...]
-
-    def offsets_of(side):
-        ref = got[side]
-        _, at, end = message_parts(*side)
-        all_parts = ref[at:end, 0:128].astype(F32)
-        n = R if side[0] == 0 else 8
-        return all_parts[0:n] + all_parts[n : 2 * n] + all_parts[2 * n : 3 * n]
-
-    for di, at, n in ((-1, 0, 8), (0, 8, R), (1, 8 + R, 8)):
-        middle = h_ref[at : at + n, :] if di == 0 else offsets_of((di, 0))
-        h_ref[at : at + n, :] = (
-            offsets_of((di, -1)) + rolled(middle, HC, 1) + rolled(offsets_of((di, 1)), HC + C, 1)
-        )
+    h_ref[0:8, :] = row_offsets(above_ref)
+    h_ref[8 + R : OR, :] = row_offsets(below_ref)
+
+    def col_offsets(ref):
+        parts = ref[COL_OFF:COL_END, 0:128].astype(F32)
+        whole = parts + rolled(parts, -HC, 1) + rolled(parts, -2 * HC, 1)
+        return jnp.where(lax.broadcasted_iota(jnp.int32, (OR, 128), 1) < HC, whole, 0.0)
+
+    h_ref[...] = (
+        col_offsets(left_ref) + rolled(h_ref[...], HC, 1) + rolled(col_offsets(right_ref), HC + C, 1)
+    )
     h = h_ref[...]
     q = lax.broadcasted_iota(jnp.int32, (OR, 128), 0)
     c = lax.broadcasted_iota(jnp.int32, (OR, 128), 1)
@@ -262,8 +269,7 @@
         at = r + 2
         gap = ht[0:EC, at : at + 1] - hw_ref[at : at + 1, :]
         scale = st[0:EC, at : at + 1] * sw_ref[at : at + 1, :]
-        table = link * jnp.exp(-gap * gap) * scale
-        table_ref[(r - 1) * EC : r * EC, :] = table.astype(BF)
+        table_ref[2 * (r - 1) * EC : 2 * r * EC, :] = in_two(link * jnp.exp(-gap * gap) * scale)
     k = lax.broadcasted_iota(jnp.int32, (QC, 256), 1)
     i = lax.broadcasted_iota(jnp.int32, (QC, 256), 0)
     block = sum((k >= QC * j).astype(jnp.int32) for j in range(1, 6))
@@ -277,45 +283,40 @@
                 gap = pht[0:QC, col : col + 1] - hw_ref[OR + at : OR + at + 1, :]
                 scale = pst[0:QC, col : col + 1] * sw_ref[OR + at : OR + at + 1, :]
                 both.append(plinks[jj] * jnp.exp(-gap * gap) * scale)
-            ptab_ref[b * 160 + j * QC : b * 160 + (j + 2) * QC, :] = jnp.concatenate(both, 0).astype(BF)
-
-    for di, at, n in ((-1, 0, HR), (0, HR, R), (1, HR + R, HR)):
-        lefts, rights = got[(di, -1)], got[(di, 1)]
-        middles = px_ref if di == 0 else got[(di, 0)]
+            two = in_two(jnp.concatenate(both, 0))
+            at_row = 2 * b * 160 + j * QC
+            ptab_ref[at_row : at_row + 2 * QC, :] = two[0 : 2 * QC]
+            ptab_ref[at_row + 160 : at_row + 160 + 2 * QC, :] = two[2 * QC :]
+
+    for at, n, ref in ((0, HR, above_ref), (HR, R, px_ref), (HR + R, HR, below_ref)):
         for r in range(0, n, 2):
-            left = lefts[r * 8 : r * 8 + 16, :].astype(F32)
-            right = rights[r * 8 : r * 8 + 16, :].astype(F32)
-            middle = middles[r * C : (r + 2) * C, :].astype(F32)
+            side = slice((at + r) * HC, (at + r + 2) * HC)
+            left, right = left_ref[side, :].astype(F32), right_ref[side, :].astype(F32)
+            middle = ref[r * C : (r + 2) * C, :].astype(F32)
             lines = [left[0:8], middle[0:C], right[0:8], left[8:16], middle[C:], right[8:16]]
             row = (at + r) * EC
             pxe_ref[row : row + 2 * EC, :] = jnp.concatenate(lines, 0).astype(BF)
 
-    for di, at, n in ((-1, 0, 3), (0, 3, PR), (1, 3 + PR, 3)):
-        lefts, rights = got[(di, -1)], got[(di, 1)]
-        side_at = message_parts(di, 1)[0]
-        middles = ct_ref if di == 0 else got[(di, 0)]
-        mid_at = 0 if di == 0 else message_parts(di, 0)[0]
-        for r in range(0, n, 2):
-            left = lefts[side_at + r * 8 : side_at + r * 8 + 16, :].astype(F32)
-            right = rights[side_at + r * 8 : side_at + r * 8 + 16, :].astype(F32)
-            for kk in range(min(2, n - r)):
-                base = (at + r + kk) * QC
-                ctf_ref[base : base + 4, :] = left[kk * 8 + 4 : kk * 8 + 8]
-                from_at = mid_at + (r + kk) * PC
-                ctf_ref[base + 4 : base + 4 + PC, :] = middles[from_at : from_at + PC, :].astype(F32)
-                ctf_ref[base + 4 + PC : base + QC, :] = right[kk * 8 : kk * 8 + 4]
+    left = left_ref[COL_CT:COL_OFF, :].astype(F32)
+    right = right_ref[COL_CT:COL_OFF, :].astype(F32)
+    for at, n, base, ref in ((0, 3, ROW_CT, above_ref), (3, PR, 0, ct_ref), (3 + PR, 3, ROW_CT, below_ref)):
+        for r in range(n):
+            e = at + r
+            ctf_ref[e * QC : e * QC + 4, :] = left[e * 4 : e * 4 + 4]
+            ctf_ref[e * QC + 4 : e * QC + 4 + PC, :] = ref[base + r * PC : base + (r + 1) * PC, :].astype(F32)
+            ctf_ref[e * QC + 4 + PC : (e + 1) * QC, :] = right[e * 4 : e * 4 + 4]
     ctb_ref[...] = ctf_ref[...].astype(BF)
 
     def table_of(r):
-        return table_ref[(r - 1) * EC : r * EC, 0 : 3 * EC]
+        return table_ref[2 * (r - 1) * EC : 2 * r * EC, 0 : 3 * EC]
 
     for r in range(1, ER - 1):
-        one = mm(table_of(r), pxe_ref[(r - 1) * EC : (r + 2) * EC, :])
+        one = applied(table_of(r), pxe_ref[(r - 1) * EC : (r + 2) * EC, :])
         f1_ref[(r - 1) * EC : r * EC, :] = one.astype(BF)
         if HR <= r < HR + R:
             f1c_ref[(r - HR) * C : (r - HR + 1) * C, :] = one[HC : HC + C].astype(BF)
     for r in range(2, ER - 2):
-        two = 2.0 * mm(table_of(r), f1_ref[(r - 2) * EC : (r + 1) * EC, :])
+        two = 2.0 * applied(table_of(r), f1_ref[(r - 2) * EC : (r + 1) * EC, :])
         two = two - pxe_ref[r * EC : (r + 1) * EC, :].astype(F32)
         f2_ref[(r - 2) * EC : (r - 1) * EC, :] = two.astype(BF)
         if HR <= r < HR + R:
@@ -342,14 +343,14 @@
     pb_ref[...] = poolf_ref[...].astype(BF)
 
     def ptable_of(b):
-        return ptab_ref[b * 160 : (b + 1) * 160, 0 : 6 * QC]
+        return ptab_ref[b * 320 : (b + 1) * 320, 0 : 6 * QC]
 
     for b in range(3):
-        one = mm(ptable_of(b), pb_ref[b * 160 : b * 160 + 6 * QC, :])
+        one = applied(ptable_of(b), pb_ref[b * 160 : b * 160 + 6 * QC, :])
         p1f_ref[(1 + 4 * b) * QC : (5 + 4 * b) * QC, :] = one
     p1b_ref[...] = p1f_ref[...].astype(BF)
     for b in range(3):
-        two = 2.0 * mm(ptable_of(b), p1b_ref[b * 160 : b * 160 + 6 * QC, :])
+        two = 2.0 * applied(ptable_of(b), p1b_ref[b * 160 : b * 160 + 6 * QC, :])
         lines = slice((1 + 4 * b) * QC, (5 + 4 * b) * QC)
         p2f_ref[lines, :] = two - poolf_ref[lines, :]
     own = slice(3 * QC, 11 * QC)
@@ -368,13 +369,13 @@
     from_one = mm_nt(cot, w2_ref[1])
     for b in range(3):
         lines = slice((1 + 4 * b) * QC, (5 + 4 * b) * QC)
-        mid = 2.0 * mm(ptable_of(b), topb_ref[b * 160 : b * 160 + 6 * QC, :])
+        mid = 2.0 * applied(ptable_of(b), topb_ref[b * 160 : b * 160 + 6 * QC, :])
         midf_ref[lines, :] = from_one[lines] + mid
     midb_ref[...] = midf_ref[...].astype(BF)
     from_zero = mm_nt(cot, w2_ref[0]) - topb_ref[...].astype(F32)
     for b in range(3):
         lines = slice((1 + 4 * b) * QC, (5 + 4 * b) * QC)
-        pgf_ref[lines, :] = from_zero[lines] + mm(ptable_of(b), midb_ref[b * 160 : b * 160 + 6 * QC, :])
+        pgf_ref[lines, :] = from_zero[lines] + applied(ptable_of(b), midb_ref[b * 160 : b * 160 + 6 * QC, :])
     for b in range(5):
         u = 2 + 2 * b
         grad = 0.25 * pgf_ref[u * QC : (u + 2) * QC, :]
@@ -411,7 +412,7 @@
         ((pooled, F), F32),
         ((pooled, F), F32),
         ((pooled, F), F32),
-        ((480, 256), BF),
+        ((960, 256), BF),
         ((pooled, F), BF),
         ((pooled, F), BF),
         ((pooled, F), BF),
@@ -428,7 +429,7 @@
         out_shape=[
             jax.ShapeDtypeStruct((PR * PC, F), BF),
             jax.ShapeDtypeStruct((6 * F, F), BF),
-            jax.ShapeDtypeStruct((26 * EC, 256), BF),
+            jax.ShapeDtypeStruct((52 * EC, 256), BF),
             jax.ShapeDtypeStruct((20 * EC, F), BF),
         ],
         scratch_shapes=[pltpu.VMEM(shape, dtype) for shape, dtype in scratch],
@@ -443,8 +444,8 @@
         r = 5 + 2 * b
         base = mm_nt(grad_ref[(r - 4) * EC : (r - 2) * EC, :], w_ref[1])
         for n in (0, 1):
-            table = table_ref[(r + n - 1) * EC : (r + n) * EC, 0 : 3 * EC]
-            mid = 2.0 * mm(table, top_ref[(r + n - 5) * EC : (r + n - 2) * EC, :])
+            table = table_ref[2 * (r + n - 1) * EC : 2 * (r + n) * EC, 0 : 3 * EC]
+            mid = 2.0 * applied(table, top_ref[(r + n - 5) * EC : (r + n - 2) * EC, :])
             mid = base[n * EC : (n + 1) * EC] + mid
             mid_ref[(r + n - 5) * EC : (r + n - 4) * EC, :] = mid.astype(BF)
     for b in range(8):
@@ -452,8 +453,8 @@
         base = mm_nt(grad_ref[(r - 4) * EC : (r - 2) * EC, :], w_ref[0])
         base = base - top_ref[(r - 4) * EC : (r - 2) * EC, :].astype(F32)
         for n in (0, 1):
-            table = table_ref[(r + n - 1) * EC : (r + n) * EC, 0 : 3 * EC]
-            line = base[n * EC : (n + 1) * EC] + mm(table, mid_ref[(r + n - 6) * EC : (r + n - 3) * EC, :])
+            table = table_ref[2 * (r + n - 1) * EC : 2 * (r + n) * EC, 0 : 3 * EC]
+            line = base[n * EC : (n + 1) * EC] + applied(table, mid_ref[(r + n - 6) * EC : (r + n - 3) * EC, :])
             at = (r + n - HR) * C
             out_ref[at : at + C, :] = line[HC : HC + C].astype(BF)
 
@@ -469,23 +470,20 @@
 
 
 def sum_at_owner(value, axes):
-    size = lax.axis_size(axes)
-    tiles = lax.all_to_all(value.reshape(size, -1, F), axes, 0, 0, tiled=True)
+    tiles = lax.all_to_all(value.reshape(lax.axis_size(axes), -1, F), axes, 0, 0, tiled=True)
     return jnp.sum(tiles.astype(F32), axis=0).astype(BF)
 
 
 def sent_to_all(value, axes):
     copies = jnp.broadcast_to(value, (lax.axis_size(axes), *value.shape))
-    return lax.all_to_all(copies, axes, 0, 0, tiled=True).reshape(-1, F)
+    return lax.all_to_all(copies, axes, 0, 0, tiled=True)
 
 
 def total_of(value):
-    stages = (("grp_1", "dev_0"), ("grp_0", "dev_1"))
-    for axes in stages:
-        value = sum_at_owner(value, axes)
-    for axes in stages[::-1]:
-        value = sent_to_all(value, axes)
-    return value
+    value = sum_at_owner(sum_at_owner(value, ("grp_1",)), DEV)
+    value = jnp.sum(sent_to_all(value, ("grp_0",)).astype(F32), axis=0).astype(BF)
+    value = sent_to_all(value, DEV).reshape(-1, F)
+    return sent_to_all(value, ("grp_1",)).reshape(-1, F)
 
 
 def clip_kernel(sums_ref, first_ref, second_ref):
@@ -508,7 +506,9 @@
 def shards(pixels, offsets, first_weights, second_weights, cotangent):
     px = pixels.reshape(R * C, F)
     ct = cotangent.reshape(PR * PC, F)
-    got = exchanged(packed_messages(px, ct, offsets))
+    above, below = exchanged(*row_messages(px, ct, offsets), GRP)
+    left, right = exchanged(*col_messages(px, ct, offsets, above, below), DEV)
+    got = (above, below, left, right)
     level, sums, table, grad = main_stage(px, ct, offsets, first_weights, second_weights, got)
     first, second = clipped(total_of(sums))
     grad_pixels = tail_stage(table, grad, first_weights)

time: 133 us -> 115 us (0.86)
  starting transfers between devices: 31.5 us -> 23 us
  blocking collectives: 62.8 us -> 54.7 us
  waiting for transfers between devices: 17.3 us -> 13.7 us
  Pallas kernels: 16.5 us -> 19.6 us
    ppermute x8 -> x4, starting transfers between devices: 25 us -> 15.3 us  [the longest x2 8.56 us: exchanged(): lax.ppermute(last, axis, forward)]
    all_to_all x3 -> x4, blocking collectives: 62.8 us -> 54.7 us  [the longest x2 29 us: sum_at_owner(): lax.all_to_all(value.reshape(lax.axis_size(axes), -1, F), axes, 0, 0, til...]
    all_to_all x1, waiting for transfers between devices: 7.93 us -> 5.69 us  [sent_to_all(): return lax.all_to_all(copies, axes, 0, 0, tiled=True)]
    pallas_call x1 -> x2, Pallas kernels: 2.1 us -> 4.03 us  [the longest x1 2.09 us: col_messages(): pl.pallas_call(col_pack_kernel, out_shape=[shape, shape], scratch_shapes=...]
    ppermute x8 -> x4, waiting for transfers between devices: 9.37 us -> 8.01 us  [the longest x2 6.75 us: exchanged(): lax.ppermute(first, axis, backward)]
  transfers between devices with their start and end apart: 9 -> 5, of which waited for: 3 -> 4; matrix products, arithmetic and copies ran while one was open for 0% -> 0% of each run, Pallas kernels for 3% -> 4%
where the time goes in v2:
time: 115 us; the launch traced here: 114 us
  blocking collectives  54.7 us (48%)
  starting transfers between devices  23 us (20%)
  Pallas kernels  19.6 us (17%)
  waiting for transfers between devices  13.7 us (12%)
  local copies, waits for them, and re-layouts  2.21 us (2%)
    all_to_all x2, blocking collectives, sum_at_owner(): lax.all_to_all(value.reshape(lax.axis_size(axes), -1, F), axes, 0, 0, til...  29 us
    all_to_all x2, blocking collectives, sent_to_all(): return lax.all_to_all(copies, axes, 0, 0, tiled=True)  25.7 us
    pallas_call x1, Pallas kernels, main_stage(): pl.pallas_call(main_kernel, out_shape=[jax.ShapeDtypeStruct((PR * PC, F),...  8.57 us
    ppermute x2, starting transfers between devices, exchanged(): lax.ppermute(last, axis, forward)  8.56 us
    all_to_all x1, starting transfers between devices, sent_to_all(): return lax.all_to_all(copies, axes, 0, 0, tiled=True)  7.64 us
    ppermute x2, starting transfers between devices, exchanged(): lax.ppermute(first, axis, backward)  6.76 us
    ppermute x2, waiting for transfers between devices, exchanged(): lax.ppermute(first, axis, backward)  6.75 us
    all_to_all x1, waiting for transfers between devices, sent_to_all(): return lax.all_to_all(copies, axes, 0, 0, tiled=True)  5.69 us
  transfers between devices with their start and end apart: 5, of which 4 were waited for; matrix products, arithmetic and copies ran while one was open for 0% of the time, Pallas kernels for 4%

profile of v2, /device:TPU:1, one launch (start us, length us, event | category | flops | bytes accessed | tf_op | source)
XLA Modules:
  0.0 114.4 jit_solution(16538823502893504269)
XLA Ops:
  0.6 1.9 %row_pack.1 = (bf16[512,256]{1,0:T(8,128)(2,1)}, bf16[512,256]{1,0:T(8,128)(2,1)}) custom-call(bf16[1024,256]{1,0:T(8,128)(2,1)} %bitcast.8, bf16[256,256]{1,0:T(8,128)(2,1)} %bitcast.14, f32[16,64]{1,0:T(8,128)} %off_ref.5), custom_call_target="tpu_custom_call" | custom-call | tf_op jit(solution)/shard_map/row_pack/pallas_call | solution.py:80
  2.6 4.6 %collective-permute-start = (bf16[512,256]{1,0:T(8,128)(2,1)}, bf16[512,256]{1,0:T(8,128)(2,1)S(1)}, u32[]{:S(2)}, u32[]{:S(2)}) collective-permute-start(bf16[512,256]{1,0:T(8,128)(2,1)} %get-tuple-element.14), channel_id=1, source_target_pairs={{0,32},{32,64},{64,96},{96,128},{128,160},{160,192},{192,224},{224... | collective-permute-start | bytes 786440 | tf_op jit(solution)/shard_map/ppermute | solution.py:147
  7.1 5.5 %collective-permute-start.1 = (bf16[512,256]{1,0:T(8,128)(2,1)}, bf16[512,256]{1,0:T(8,128)(2,1)S(1)}, u32[]{:S(2)}, u32[]{:S(2)}) collective-permute-start(bf16[512,256]{1,0:T(8,128)(2,1)} %get-tuple-element.15), channel_id=1, source_target_pairs={{32,0},{64,32},{96,64},{128,96},{160,128},{192,160},{224,192},{256... | collective-permute-start | bytes 786440 | tf_op jit(solution)/shard_map/ppermute | solution.py:147
  12.6 0.0 collective-permute-done.above_ref
  12.6 0.0 copy-start
  12.6 2.4 %collective-permute-done.1.below_ref = bf16[512,256]{1,0:T(8,128)(2,1)S(1)} collective-permute-done((bf16[512,256]{1,0:T(8,128)(2,1)}, bf16[512,256]{1,0:T(8,128)(2,1)S(1)}, u32[]{:S(2)}, u32[]{:S(2)}) %collective-permute-start.1) | collective-permute-done | bytes 262176 | tf_op jit(solution)/shard_map/ppermute | solution.py:147
  15.0 0.0 copy-done
  15.1 0.0 copy-start.1
  15.1 0.7 copy-done.1
  15.8 2.1 %col_pack.1 = (bf16[320,256]{1,0:T(8,128)(2,1)}, bf16[320,256]{1,0:T(8,128)(2,1)}) custom-call(bf16[1024,256]{1,0:T(8,128)(2,1)} %bitcast.9, bf16[256,256]{1,0:T(8,128)(2,1)} %bitcast.15, f32[16,64]{1,0:T(8,128)} %off_ref.5, bf16[512,256]{1,0:T(8,128)(2,1)} %copy-done, bf16[512,256]{1,0:T(8,128)(2,1)} %copy-done.1), custom_call_target="tpu_custom_call" | custom-call | tf_op jit(solution)/shard_map/col_pack/pallas_call | solution.py:135
  17.9 4.0 %collective-permute-start.2 = (bf16[320,256]{1,0:T(8,128)(2,1)}, bf16[320,256]{1,0:T(8,128)(2,1)S(1)}, u32[]{:S(2)}, u32[]{:S(2)}) collective-permute-start(bf16[320,256]{1,0:T(8,128)(2,1)} %get-tuple-element.16), channel_id=1, source_target_pairs={{0,1},{1,2},{2,3},{3,4},{4,5},{5,6},{6,7},{7,8},{8,9},{9,10},{10,1... | collective-permute-start | bytes 491528 | tf_op jit(solution)/shard_map/ppermute | solution.py:147
  21.9 1.3 %collective-permute-start.3 = (bf16[320,256]{1,0:T(8,128)(2,1)}, bf16[320,256]{1,0:T(8,128)(2,1)S(1)}, u32[]{:S(2)}, u32[]{:S(2)}) collective-permute-start(bf16[320,256]{1,0:T(8,128)(2,1)} %get-tuple-element.17), channel_id=1, source_target_pairs={{1,0},{2,1},{3,2},{4,3},{5,4},{6,5},{7,6},{8,7},{9,8},{10,9},{11,1... | collective-permute-start | bytes 491528 | tf_op jit(solution)/shard_map/ppermute | solution.py:147
  23.2 1.3 %collective-permute-done.2.left_ref = bf16[320,256]{1,0:T(8,128)(2,1)S(1)} collective-permute-done((bf16[320,256]{1,0:T(8,128)(2,1)}, bf16[320,256]{1,0:T(8,128)(2,1)S(1)}, u32[]{:S(2)}, u32[]{:S(2)}) %collective-permute-start.2) | collective-permute-done | bytes 163872 | tf_op jit(solution)/shard_map/ppermute | solution.py:147
  24.4 0.0 copy-start.2
  24.4 4.4 %collective-permute-done.3.right_ref = bf16[320,256]{1,0:T(8,128)(2,1)S(1)} collective-permute-done((bf16[320,256]{1,0:T(8,128)(2,1)}, bf16[320,256]{1,0:T(8,128)(2,1)S(1)}, u32[]{:S(2)}, u32[]{:S(2)}) %collective-permute-start.3) | collective-permute-done | bytes 163872 | tf_op jit(solution)/shard_map/ppermute | solution.py:147
  28.8 0.0 copy-done.2
  28.8 0.0 copy-start.3
  28.8 0.7 copy-done.3
  29.4 8.6 %main.1 = (bf16[256,256]{1,0:T(8,128)(2,1)}, bf16[1536,256]{1,0:T(8,128)(2,1)}, bf16[4160,256]{1,0:T(8,128)(2,1)}, bf16[1600,256]{1,0:T(8,128)(2,1)}) custom-call(bf16[1024,256]{1,0:T(8,128)(2,1)} %bitcast.10, bf16[256,256]{1,0:T(8,128)(2,1)} %bitcast.16, f32[16,64]{1,0:T(8,128)} %off_ref.5, bf16[3,256,256]{2,1,0:T(8,128)(2,1)} %w_ref.1, ...), custom_call_target="tpu_custom_call" | custom-call | tf_op jit(solution)/shard_map/main/pallas_call | solution.py:427
  38.0 5.1 %all_to_all.25 = bf16[2,768,256]{2,1,0:T(8,128)(2,1)S(1)} all-to-all(bf16[2,768,256]{2,1,0:T(8,128)(2,1)} %bitcast.17), channel_id=1, replica_groups=mesh['grp_0'=8,'grp_1'=2,'dev_0'=4,'dev_1'=8] {'grp_1'}, dimensions={0} | all-to-all | bytes 1572864 | tf_op jit(solution)/shard_map/all_to_all | solution.py:473
  43.1 0.3 reduce_sum.36
  43.4 23.9 %all_to_all.26 = bf16[32,24,256]{2,1,0:T(8,128)(2,1)S(1)} all-to-all(bf16[32,24,256]{2,1,0:T(8,128)(2,1)S(1)} %bitcast.13), channel_id=1, replica_groups=mesh['grp_0'=8,'grp_1'=2,'dev_0'=4,'dev_1'=8] {'dev_0','dev_1'}, dimensions={0} | all-to-all | bytes 786432 | tf_op jit(solution)/shard_map/all_to_all | solution.py:473
  67.3 0.1 reduce_sum.37
  67.4 15.7 %all_to_all.27 = bf16[8,24,256]{2,1,0:T(8,128)(2,1)S(1)} all-to-all(bf16[8,24,256]{2,1,0:T(8,128)(2,1)S(1)} %broadcast_in_dim.9), channel_id=1, replica_groups=mesh['grp_0'=8,'grp_1'=2,'dev_0'=4,'dev_1'=8] {'grp_0'}, dimensions={0} | all-to-all | bytes 196608 | tf_op jit(solution)/shard_map/all_to_all | solution.py:479
  83.2 0.8 broadcast_in_dim.10
  84.0 7.6 %all-to-all-start.3 = ((bf16[32,24,256]{2,1,0:T(8,128)(2,1)}), bf16[32,24,256]{2,1,0:T(8,128)(2,1)S(1)}, u32[]{:S(2)}, u32[]{:S(2)}) async-start(bf16[32,24,256]{2,1,0:T(8,128)(2,1)} %broadcast_in_dim.10), calls=%async_computation.3 | async-start | bytes 786432 | tf_op jit(solution)/shard_map/all_to_all | solution.py:479
  91.6 4.6 %tail.1 = bf16[1024,256]{1,0:T(8,128)(2,1)} custom-call(bf16[4160,256]{1,0:T(8,128)(2,1)} %get-tuple-element.18.table_ref, bf16[1600,256]{1,0:T(8,128)(2,1)} %get-tuple-element.19.grad_ref, bf16[3,256,256]{2,1,0:T(8,128)(2,1)} %w_ref.1), custom_call_target="tpu_custom_call" | custom-call | tf_op jit(solution)/shard_map/tail/pallas_call | solution.py:463
  96.2 5.7 %all-to-all-done.3 = bf16[32,24,256]{2,1,0:T(8,128)(2,1)S(1)} async-done(((bf16[32,24,256]{2,1,0:T(8,128)(2,1)}), bf16[32,24,256]{2,1,0:T(8,128)(2,1)S(1)}, u32[]{:S(2)}, u32[]{:S(2)}) %all-to-all-start.3) | async-done | bytes 393248 | tf_op jit(solution)/shard_map/all_to_all | solution.py:479
  101.8 0.1 broadcast_in_dim.11
  101.9 10.0 %all_to_all.28 = bf16[2,768,256]{2,1,0:T(8,128)(2,1)} all-to-all(bf16[2,768,256]{2,1,0:T(8,128)(2,1)S(1)} %broadcast_in_dim.11), channel_id=1, replica_groups=mesh['grp_0'=8,'grp_1'=2,'dev_0'=4,'dev_1'=8] {'grp_1'}, dimensions={0} | all-to-all | bytes 1572864 | tf_op jit(solution)/shard_map/all_to_all | solution.py:479
  111.9 2.5 %clip.1 = (f32[3,256,256]{2,1,0:T(8,128)}, f32[3,256,256]{2,1,0:T(8,128)}) custom-call(bf16[1536,256]{1,0:T(8,128)(2,1)} %bitcast.11), custom_call_target="tpu_custom_call" | custom-call | tf_op jit(solution)/shard_map/clip/pallas_call | solution.py:503
  (2 shorter events, 0.0 us)
Async XLA Ops:
  2.6 10.1 %collective-permute-start = (bf16[512,256]{1,0:T(8,128)(2,1)}, bf16[512,256]{1,0:T(8,128)(2,1)S(1)}, u32[]{:S(2)}, u32[]{:S(2)}) collective-permute-start(bf16[512,256]{1,0:T(8,128)(2,1)} %get-tuple-element.14), channel_id=1, source_target_pairs={{0,32},{32,64},{64,96},{96,128},{128,160},{160,192},{192,224},{224... | collective-permute-start | bytes 786440 | tf_op jit(solution)/shard_map/ppermute | solution.py:147
  7.1 7.9 %collective-permute-start.1 = (bf16[512,256]{1,0:T(8,128)(2,1)}, bf16[512,256]{1,0:T(8,128)(2,1)S(1)}, u32[]{:S(2)}, u32[]{:S(2)}) collective-permute-start(bf16[512,256]{1,0:T(8,128)(2,1)} %get-tuple-element.15), channel_id=1, source_target_pairs={{32,0},{64,32},{96,64},{128,96},{160,128},{192,160},{224,192},{256... | collective-permute-start | bytes 786440 | tf_op jit(solution)/shard_map/ppermute | solution.py:147
  12.6 2.4 %copy-start = (bf16[512,256]{1,0:T(8,128)(2,1)}, bf16[512,256]{1,0:T(8,128)(2,1)S(1)}, u32[]{:S(2)}) copy-start(bf16[512,256]{1,0:T(8,128)(2,1)S(1)} %collective-permute-done.above_ref) | copy-start | bytes 786436
  15.1 0.7 copy-start.1
  17.9 6.6 %collective-permute-start.2 = (bf16[320,256]{1,0:T(8,128)(2,1)}, bf16[320,256]{1,0:T(8,128)(2,1)S(1)}, u32[]{:S(2)}, u32[]{:S(2)}) collective-permute-start(bf16[320,256]{1,0:T(8,128)(2,1)} %get-tuple-element.16), channel_id=1, source_target_pairs={{0,1},{1,2},{2,3},{3,4},{4,5},{5,6},{6,7},{7,8},{8,9},{9,10},{10,1... | collective-permute-start | bytes 491528 | tf_op jit(solution)/shard_map/ppermute | solution.py:147
  21.9 6.9 %collective-permute-start.3 = (bf16[320,256]{1,0:T(8,128)(2,1)}, bf16[320,256]{1,0:T(8,128)(2,1)S(1)}, u32[]{:S(2)}, u32[]{:S(2)}) collective-permute-start(bf16[320,256]{1,0:T(8,128)(2,1)} %get-tuple-element.17), channel_id=1, source_target_pairs={{1,0},{2,1},{3,2},{4,3},{5,4},{6,5},{7,6},{8,7},{9,8},{10,9},{11,1... | collective-permute-start | bytes 491528 | tf_op jit(solution)/shard_map/ppermute | solution.py:147
  24.4 4.4 %copy-start.2 = (bf16[320,256]{1,0:T(8,128)(2,1)}, bf16[320,256]{1,0:T(8,128)(2,1)S(1)}, u32[]{:S(2)}) copy-start(bf16[320,256]{1,0:T(8,128)(2,1)S(1)} %collective-permute-done.2.left_ref) | copy-start | bytes 491524
  28.8 0.7 copy-start.3
  84.0 17.9 %all-to-all-start.3 = ((bf16[32,24,256]{2,1,0:T(8,128)(2,1)}), bf16[32,24,256]{2,1,0:T(8,128)(2,1)S(1)}, u32[]{:S(2)}, u32[]{:S(2)}) async-start(bf16[32,24,256]{2,1,0:T(8,128)(2,1)} %broadcast_in_dim.10), calls=%async_computation.3 | async-start | bytes 786432 | tf_op jit(solution)/shard_map/all_to_all | solution.py:479

commit v3 on v2

--- a/solution.py
+++ b/solution.py
@@ -53,6 +53,14 @@
 COL_END = COL_OFF + OR
 
 
+def on_chip(*arrays):
+    return [pltpu.with_memory_space_constraint(a, pltpu.VMEM) for a in arrays]
+
+
+def in_hbm(*arrays):
+    return [pltpu.with_memory_space_constraint(a, pltpu.HBM) for a in arrays]
+
+
 def rolled(x, shift, axis):
     return pltpu.roll(x, shift % x.shape[axis], axis)
 
@@ -64,25 +72,54 @@
     return high, middle, left - middle
 
 
-def row_pack_kernel(px_ref, ct_ref, off_ref, up_ref, down_ref, wide):
+def started(sems, pairs):
+    copies = [pltpu.make_async_copy(src, dst, sems.at[n]) for n, (src, dst) in enumerate(pairs)]
+    for copy in copies:
+        copy.start()
+    return copies
+
+
+def row_pack_kernel(px_ref, ct_ref, px_rows, ct_rows, off_ref, *rest):
+    up_ref, down_ref, pxl_ref, pxr_ref, ctl_ref, ctr_ref, wide, off_buf, sems = rest
+    pairs = [(off_ref, off_buf)]
+    for out, px_at, ct_at in ((up_ref, 0, 0), (down_ref, R - HR, PR - 3)):
+        for ref, at, size, to in ((px_ref, px_at * C, HR * C, 0), (ct_ref, ct_at * PC, 3 * PC, ROW_CT)):
+            pairs.append((ref.at[pl.ds(at, size), :], out.at[pl.ds(to, size), :]))
+    pairs += [
+        (px_rows.at[:, pl.ds(0, 16), :], pxl_ref),
+        (px_rows.at[:, pl.ds(C - 16, 16), :], pxr_ref),
+        (ct_rows.at[:, pl.ds(0, 16), :], ctl_ref),
+        (ct_rows.at[:, pl.ds(PC - 16, 16), :], ctr_ref),
+    ]
+    copies = started(sems, pairs)
     wide[...] = jnp.zeros_like(wide)
-    wide[:, 0:C] = off_ref[...]
-    for out, px_at, ct_at, off_at in ((up_ref, 0, 0, 0), (down_ref, R - HR, PR - 3, R - 8)):
-        out[0:ROW_CT, :] = px_ref[px_at * C : (px_at + HR) * C, :]
-        out[ROW_CT:ROW_OFF, :] = ct_ref[ct_at * PC : (ct_at + 3) * PC, :]
+    copies[0].wait()
+    wide[:, 0:C] = off_buf[...]
+    for out, off_at in ((up_ref, 0), (down_ref, R - 8)):
         high, middle, low = in_parts(wide[off_at : off_at + 8, :])
         packed = jnp.concatenate([high, middle, low, jnp.zeros_like(low)], 0)
         out[ROW_OFF:ROW_END, :] = jnp.concatenate([packed, jnp.zeros_like(packed)], 1).astype(BF)
+    for copy in copies[1:]:
+        copy.wait()
 
 
 def row_messages(pixels, cotangent, offsets):
-    shape = jax.ShapeDtypeStruct((ROW_END, F), BF)
     return pl.pallas_call(
         row_pack_kernel,
-        out_shape=[shape, shape],
-        scratch_shapes=[pltpu.VMEM((R, 128), F32)],
+        in_specs=[pl.BlockSpec(memory_space=pltpu.HBM)] * 5,
+        out_shape=[
+            pltpu.VMEM((ROW_END, F), BF),
+            pltpu.VMEM((ROW_END, F), BF),
+            pltpu.VMEM((R, 16, F), BF),
+            pltpu.VMEM((R, 16, F), BF),
+            pltpu.VMEM((PR, 16, F), BF),
+            pltpu.VMEM((PR, 16, F), BF),
+            pltpu.VMEM((R, 128), F32),
+        ],
+        scratch_shapes=[pltpu.VMEM((R, C), F32), pltpu.SemaphoreType.DMA((9,))],
+        compiler_params=pltpu.CompilerParams(vmem_limit_bytes=4 << 20),
         name="row_pack",
-    )(pixels, cotangent, offsets)
+    )(*in_hbm(pixels, cotangent, pixels.reshape(R, C, F), cotangent.reshape(PR, PC, F), offsets))
 
 
 def row_offsets(ref):
@@ -90,30 +127,31 @@
     return parts[0:8] + parts[8:16] + parts[16:24]
 
 
-def col_pack_kernel(px_ref, ct_ref, off_ref, above_ref, below_ref, left_ref, right_ref, wide):
-    wide[...] = jnp.zeros_like(wide)
-    wide[8 : 8 + R, 0:C] = off_ref[...]
+def col_pack_kernel(*refs):
+    pxl_ref, pxr_ref, ctl_ref, ctr_ref, off_ref, above_ref, below_ref, left_ref, right_ref, wide = refs
+    wide[8 : 8 + R, :] = off_ref[...]
     wide[0:8, :] = row_offsets(above_ref)
     wide[8 + R : OR, :] = row_offsets(below_ref)
     lane = lax.broadcasted_iota(jnp.int32, (OR, 128), 1)
     near = lax.broadcasted_iota(jnp.int32, (8, F), 0) < 4
-    for out, px_at, ct_at, half in (
-        (left_ref, 0, 0, slice(0, 8)),
-        (right_ref, C - 16, PC - 16, slice(8, 16)),
+    for out, px_ref, ct_ref, px_at, ct_at, half in (
+        (left_ref, pxl_ref, ctl_ref, 0, 0, slice(0, 8)),
+        (right_ref, pxr_ref, ctr_ref, C - 16, PC - 16, slice(8, 16)),
     ):
+
+        def line(ref, k, base, width, at):
+            if ref is above_ref or ref is below_ref:
+                return ref[base + k * width + at : base + k * width + at + 16, :].astype(F32)[half]
+            return ref[k].astype(F32)[half]
+
         for first, n, ref in ((0, HR, above_ref), (HR, R, px_ref), (HR + R, HR, below_ref)):
             for r in range(0, n, 2):
-                tiles = []
-                for k in (r, r + 1):
-                    at = k * C + px_at
-                    tiles.append(ref[at : at + 16, :].astype(F32)[half])
+                tiles = [line(ref, k, 0, C, px_at) for k in (r, r + 1)]
                 at = (first + r) * HC
                 out[at : at + 16, :] = jnp.concatenate(tiles, 0).astype(BF)
         lines = []
-        for base, n, ref in ((ROW_CT, 3, above_ref), (0, PR, ct_ref), (ROW_CT, 3, below_ref)):
-            for r in range(n):
-                at = base + r * PC + ct_at
-                lines.append(ref[at : at + 16, :].astype(F32)[half])
+        for n, ref in ((3, above_ref), (PR, ct_ref), (3, below_ref)):
+            lines += [line(ref, k, ROW_CT, PC, ct_at) for k in range(n)]
         tiles = []
         for e in range(0, QR, 2):
             first, second = lines[e], lines[e + 1]
@@ -130,14 +168,15 @@
         out[COL_OFF:COL_END, :] = jnp.concatenate([packed, jnp.zeros_like(packed)], 1).astype(BF)
 
 
-def col_messages(pixels, cotangent, offsets, above, below):
-    shape = jax.ShapeDtypeStruct((COL_END, F), BF)
+def col_messages(*parts):
+    shape = pltpu.VMEM((COL_END, F), BF)
     return pl.pallas_call(
         col_pack_kernel,
         out_shape=[shape, shape],
         scratch_shapes=[pltpu.VMEM((OR, 128), F32)],
+        compiler_params=pltpu.CompilerParams(vmem_limit_bytes=4 << 20),
         name="col_pack",
-    )(pixels, cotangent, offsets, above, below)
+    )(*on_chip(*parts))
 
 
 def exchanged(first, last, axis):
@@ -206,19 +245,23 @@
     return x.T
 
 
-def main_kernel(px_ref, ct_ref, off_ref, w1_ref, w2_ref, above_ref, below_ref, left_ref, right_ref, *rest):
-    level_ref, sums_ref, table_ref, grad_ref = rest[:4]
+def main_kernel(px_hbm, ct_hbm, w1_hbm, w2_hbm, off_ref, above_ref, below_ref, left_ref, right_ref, *rest):
+    terms_hbm, keep_ref, send_ref, table_ref, grad_hbm = rest[:5]
     (h_ref, hw_ref, sw_ref, pxe_ref, f1_ref, f2_ref, f1c_ref, f2c_ref, slope_ref, hid_ref,
      poolf_ref, p1f_ref, p2f_ref, ctf_ref, ptab_ref, pb_ref, p1b_ref, ctb_ref, topb_ref,
-     midf_ref, midb_ref, pgf_ref, sp_ref, agc_ref, low_ref) = rest[4:]
+     midf_ref, midb_ref, pgf_ref, sp_ref, agc_ref, halves_ref, px_ref, ct_ref, w1_ref, w2_ref,
+     terms_ref, grad_ref, sems, out_sems) = rest[5:]
+    copies = started(
+        sems, [(px_hbm, px_ref), (ct_hbm, ct_ref), (w1_hbm, w1_ref), (w2_hbm, w2_ref)]
+    )
+    core = lax.axis_index("grp_1")
 
     row0 = (lax.axis_index("grp_0") * 2 + lax.axis_index("grp_1")) * R
     col0 = (lax.axis_index("dev_0") * lax.axis_size("dev_1") + lax.axis_index("dev_1")) * C
     rows_all = lax.axis_size("grp_0") * lax.axis_size("grp_1") * R
     cols_all = lax.axis_size("dev_0") * lax.axis_size("dev_1") * C
 
-    h_ref[...] = jnp.zeros_like(h_ref)
-    h_ref[8 : 8 + R, 0:C] = off_ref[...]
+    h_ref[8 : 8 + R, :] = off_ref[...]
     h_ref[0:8, :] = row_offsets(above_ref)
     h_ref[8 + R : OR, :] = row_offsets(below_ref)
 
@@ -288,6 +331,8 @@
             ptab_ref[at_row : at_row + 2 * QC, :] = two[0 : 2 * QC]
             ptab_ref[at_row + 160 : at_row + 160 + 2 * QC, :] = two[2 * QC :]
 
+    copies[0].wait()
+    copies[1].wait()
     for at, n, ref in ((0, HR, above_ref), (HR, R, px_ref), (HR + R, HR, below_ref)):
         for r in range(0, n, 2):
             side = slice((at + r) * HC, (at + r + 2) * HC)
@@ -306,6 +351,9 @@
             ctf_ref[e * QC + 4 : e * QC + 4 + PC, :] = ref[base + r * PC : base + (r + 1) * PC, :].astype(F32)
             ctf_ref[e * QC + 4 + PC : (e + 1) * QC, :] = right[e * 4 : e * 4 + 4]
     ctb_ref[...] = ctf_ref[...].astype(BF)
+
+    copies[2].wait()
+    copies[3].wait()
 
     def table_of(r):
         return table_ref[2 * (r - 1) * EC : 2 * r * EC, 0 : 3 * EC]
@@ -355,14 +403,15 @@
         p2f_ref[lines, :] = two - poolf_ref[lines, :]
     own = slice(3 * QC, 11 * QC)
     terms = [poolf_ref[own, :].astype(BF), p1f_ref[own, :].astype(BF), p2f_ref[own, :].astype(BF)]
-    low_ref[...] = sum(mm(term, w2_ref[n]) for n, term in enumerate(terms))
-    for r in range(PR):
-        level_ref[r * PC : (r + 1) * PC, :] = low_ref[r * QC + 4 : r * QC + 4 + PC, :].astype(BF)
+    for n, term in enumerate(terms):
+        terms_ref[n] = term
+    outward = [pltpu.make_async_copy(terms_ref, terms_hbm, out_sems.at[0])]
+    outward[0].start()
     col = lax.broadcasted_iota(jnp.int32, (QC, F), 0)
     keep = ((col >= 4) & (col < 4 + PC)).astype(F32)
     cot_own = (ctf_ref[own, :].reshape(PR, QC, F) * keep[None]).reshape(PR * QC, F).astype(BF)
     for n, term in enumerate(terms):
-        sums_ref[(3 + n) * F : (4 + n) * F, :] = mm_tn(term, cot_own).astype(sums_ref.dtype)
+        halves_ref[1 - core, n * F : (n + 1) * F, :] = mm_tn(term, cot_own).astype(BF)
 
     cot = ctb_ref[...]
     topb_ref[...] = mm_nt(cot, w2_ref[2]).astype(BF)
@@ -391,8 +440,14 @@
             grad_ref[(r - 4) * EC : (r - 3) * EC, :] = grad_row.astype(BF)
             if HR <= r < HR + R:
                 agc_ref[(r - HR) * C : (r - HR + 1) * C, :] = grad_row[HC : HC + C].astype(BF)
+    outward.append(pltpu.make_async_copy(grad_ref, grad_hbm, out_sems.at[1]))
+    outward[1].start()
     for n, ref in enumerate((px_ref, f1c_ref, f2c_ref)):
-        sums_ref[n * F : (n + 1) * F, :] = mm_tn(ref[...], agc_ref[...]).astype(sums_ref.dtype)
+        halves_ref[core, n * F : (n + 1) * F, :] = mm_tn(ref[...], agc_ref[...]).astype(BF)
+    keep_ref[...] = halves_ref[0]
+    send_ref[...] = halves_ref[1]
+    for copy in outward:
+        copy.wait()
 
 
 def main_stage(pixels, cotangent, offsets, first_weights, second_weights, got):
@@ -422,23 +477,33 @@
         ((pooled, F), F32),
         ((10, 2 * EC, 128), F32),
         ((R * C, F), BF),
-        ((PR * QC, F), F32),
+        ((2, 3 * F, F), BF),
+        ((R * C, F), BF),
+        ((PR * PC, F), BF),
+        ((3, F, F), BF),
+        ((3, F, F), BF),
+        ((3, PR * QC, F), BF),
+        ((20 * EC, F), BF),
     ]
     return pl.pallas_call(
         main_kernel,
         out_shape=[
-            jax.ShapeDtypeStruct((PR * PC, F), BF),
-            jax.ShapeDtypeStruct((6 * F, F), BF),
-            jax.ShapeDtypeStruct((52 * EC, 256), BF),
-            jax.ShapeDtypeStruct((20 * EC, F), BF),
+            pltpu.HBM((3, PR * QC, F), BF),
+            pltpu.VMEM((3 * F, F), BF),
+            pltpu.VMEM((3 * F, F), BF),
+            pltpu.VMEM((52 * EC, 256), BF),
+            pltpu.HBM((20 * EC, F), BF),
         ],
-        scratch_shapes=[pltpu.VMEM(shape, dtype) for shape, dtype in scratch],
-        compiler_params=pltpu.CompilerParams(vmem_limit_bytes=56 << 20),
+        in_specs=[pl.BlockSpec(memory_space=pl.ANY)] * 4
+        + [pl.BlockSpec(memory_space=pltpu.VMEM)] * 5,
+        scratch_shapes=[pltpu.VMEM(shape, dtype) for shape, dtype in scratch]
+        + [pltpu.SemaphoreType.DMA((4,)), pltpu.SemaphoreType.DMA((2,))],
+        compiler_params=pltpu.CompilerParams(vmem_limit_bytes=20 << 20),
         name="main",
-    )(pixels, cotangent, offsets, first_weights, second_weights, *got)
-
-
-def tail_kernel(table_ref, grad_ref, w_ref, out_ref, top_ref, mid_ref):
+    )(pixels, cotangent, first_weights, second_weights, *on_chip(offsets, *got))
+
+
+def tail_kernel(terms_ref, table_ref, grad_ref, w_ref, w2_ref, out_ref, level_ref, top_ref, mid_ref, low_ref):
     top_ref[...] = mm_nt(grad_ref[...], w_ref[2]).astype(BF)
     for b in range(9):
         r = 5 + 2 * b
@@ -457,16 +522,26 @@
             line = base[n * EC : (n + 1) * EC] + applied(table, mid_ref[(r + n - 6) * EC : (r + n - 3) * EC, :])
             at = (r + n - HR) * C
             out_ref[at : at + C, :] = line[HC : HC + C].astype(BF)
-
-
-def tail_stage(table, grad, first_weights):
+    low_ref[...] = sum(mm(terms_ref[n], w2_ref[n]) for n in range(3))
+    for r in range(PR):
+        level_ref[r * PC : (r + 1) * PC, :] = low_ref[r * QC + 4 : r * QC + 4 + PC, :].astype(BF)
+
+
+def tail_stage(terms, table, grad, first_weights, second_weights):
     return pl.pallas_call(
         tail_kernel,
-        out_shape=jax.ShapeDtypeStruct((R * C, F), BF),
-        scratch_shapes=[pltpu.VMEM((20 * EC, F), BF), pltpu.VMEM((18 * EC, F), BF)],
-        compiler_params=pltpu.CompilerParams(vmem_limit_bytes=56 << 20),
+        out_shape=[
+            jax.ShapeDtypeStruct((R * C, F), BF),
+            jax.ShapeDtypeStruct((PR * PC, F), BF),
+        ],
+        scratch_shapes=[
+            pltpu.VMEM((20 * EC, F), BF),
+            pltpu.VMEM((18 * EC, F), BF),
+            pltpu.VMEM((PR * QC, F), F32),
+        ],
+        compiler_params=pltpu.CompilerParams(vmem_limit_bytes=8 << 20),
         name="tail",
-    )(table, grad, first_weights)
+    )(*in_hbm(terms), *on_chip(table), *in_hbm(grad), first_weights, second_weights)
 
 
 def sum_at_owner(value, axes):
@@ -479,39 +554,57 @@
     return lax.all_to_all(copies, axes, 0, 0, tiled=True)
 
 
-def total_of(value):
-    value = sum_at_owner(sum_at_owner(value, ("grp_1",)), DEV)
+def swapped(value):
+    return lax.ppermute(value, "grp_1", [(0, 1), (1, 0)])
+
+
+def total_of(keep, send):
+    value = (keep.astype(F32) + swapped(send).astype(F32)).astype(BF)
+    value = sum_at_owner(value, DEV)
     value = jnp.sum(sent_to_all(value, ("grp_0",)).astype(F32), axis=0).astype(BF)
-    value = sent_to_all(value, DEV).reshape(-1, F)
-    return sent_to_all(value, ("grp_1",)).reshape(-1, F)
-
-
-def clip_kernel(sums_ref, first_ref, second_ref):
+    return sent_to_all(value, DEV).reshape(-1, F)
+
+
+def clip_kernel(own_ref, other_ref, first_ref, second_ref):
     total = jnp.zeros((8, F), F32)
-    for n in range(6):
-        part = sums_ref[n * F : (n + 1) * F, :].astype(F32)
-        total = total + jnp.sum((part * part).reshape(F // 8, 8, F), axis=0)
+    for ref in (own_ref, other_ref):
+        for n in range(3):
+            part = ref[n * F : (n + 1) * F, :].astype(F32)
+            total = total + jnp.sum((part * part).reshape(F // 8, 8, F), axis=0)
     square_sum = jnp.sum(jnp.sum(total, axis=1, keepdims=True), axis=0, keepdims=True)
     factor = jnp.minimum(1.0, 2.0 * F * lax.rsqrt(square_sum + 1e-06))
+    is_first = lax.axis_index("grp_1") == 0
     for n in range(3):
-        first_ref[n] = sums_ref[n * F : (n + 1) * F, :].astype(F32) * factor
-        second_ref[n] = sums_ref[(3 + n) * F : (4 + n) * F, :].astype(F32) * factor
-
-
-def clipped(sums):
+        own = own_ref[n * F : (n + 1) * F, :].astype(F32) * factor
+        other = other_ref[n * F : (n + 1) * F, :].astype(F32) * factor
+        first_ref[n] = jnp.where(is_first, own, other)
+        second_ref[n] = jnp.where(is_first, other, own)
+
+
+def clipped(own, other):
     shape = jax.ShapeDtypeStruct((3, F, F), F32)
-    return pl.pallas_call(clip_kernel, out_shape=[shape, shape], name="clip")(sums)
+    return pl.pallas_call(
+        clip_kernel,
+        out_shape=[shape, shape],
+        compiler_params=pltpu.CompilerParams(vmem_limit_bytes=8 << 20),
+        name="clip",
+    )(*on_chip(own, other))
 
 
 def shards(pixels, offsets, first_weights, second_weights, cotangent):
     px = pixels.reshape(R * C, F)
     ct = cotangent.reshape(PR * PC, F)
-    above, below = exchanged(*row_messages(px, ct, offsets), GRP)
-    left, right = exchanged(*col_messages(px, ct, offsets, above, below), DEV)
+    up, down, *strips, wide = row_messages(px, ct, offsets)
+    above, below = exchanged(up, down, GRP)
+    left, right = exchanged(*col_messages(*strips, wide, above, below), DEV)
     got = (above, below, left, right)
-    level, sums, table, grad = main_stage(px, ct, offsets, first_weights, second_weights, got)
-    first, second = clipped(total_of(sums))
-    grad_pixels = tail_stage(table, grad, first_weights)
+    terms, keep, send, table, grad = main_stage(
+        px, ct, wide, first_weights, second_weights, got
+    )
+    own = total_of(keep, send)
+    grad_pixels, level = tail_stage(terms, table, grad, first_weights, second_weights)
+    own, grad_pixels, level = lax.optimization_barrier((own, grad_pixels, level))
+    first, second = clipped(own, swapped(own))
     return grad_pixels.reshape(R, C, F), first, second, level.reshape(PR, PC, F)
 
 

time: 115 us -> 106 us (0.922)
  blocking collectives: 54.7 us -> 39.3 us
  starting transfers between devices: 23 us -> 32 us
  Pallas kernels: 19.6 us -> 15.7 us
  waiting for transfers between devices: 13.7 us -> 16.8 us
  local copies, waits for them, and re-layouts: 2.21 us -> 0.8 us
    all_to_all x2 -> x1, blocking collectives: 25.7 us -> 15 us  [sent_to_all(): return lax.all_to_all(copies, axes, 0, 0, tiled=True)]
    ppermute x0 -> x2, starting transfers between devices: none -> 9.07 us  [swapped(): return lax.ppermute(value, 'grp_1', [(0, 1), (1, 0)])]
    all_to_all x2 -> x1, blocking collectives: 29 us -> 24.2 us  [sum_at_owner(): lax.all_to_all(value.reshape(lax.axis_size(axes), -1, F), axes, 0, 0, til...]
    ppermute x0 -> x2, waiting for transfers between devices: none -> 3.02 us  [swapped(): return lax.ppermute(value, 'grp_1', [(0, 1), (1, 0)])]
    pallas_call x4, Pallas kernels: 17.5 us -> 15.5 us  [the longest x1 8.55 us: main_stage(): pl.pallas_call(main_kernel, out_shape=[pltpu.HBM((3, PR * QC, F), BF), pl...]
    pallas_call x1, Pallas kernels: 2.09 us -> 0.17 us  [col_messages(): pl.pallas_call(col_pack_kernel, out_shape=[shape, shape], scratch_shapes=...]
    unnamed x8, local copies, waits for them, and re-layouts: 1.37 us -> 0.02 us
  transfers between devices with their start and end apart: 5 -> 7, of which waited for: 4 -> 6; matrix products, arithmetic and copies ran while one was open for 0% -> 0% of each run, Pallas kernels for 4% -> 4%
where the time goes in v3:
time: 106 us
  blocking collectives  39.3 us (37%)
  starting transfers between devices  32 us (30%)
  waiting for transfers between devices  16.8 us (16%)
  Pallas kernels  15.7 us (15%)
    all_to_all x1, blocking collectives, sum_at_owner(): lax.all_to_all(value.reshape(lax.axis_size(axes), -1, F), axes, 0, 0, til...  24.2 us
    all_to_all x1, blocking collectives, sent_to_all(): return lax.all_to_all(copies, axes, 0, 0, tiled=True)  15 us
    ppermute x2, starting transfers between devices, swapped(): return lax.ppermute(value, 'grp_1', [(0, 1), (1, 0)])  9.07 us
    ppermute x2, starting transfers between devices, exchanged(): lax.ppermute(last, axis, forward)  8.58 us
    pallas_call x1, Pallas kernels, main_stage(): pl.pallas_call(main_kernel, out_shape=[pltpu.HBM((3, PR * QC, F), BF), pl...  8.55 us
    all_to_all x1, starting transfers between devices, sent_to_all(): return lax.all_to_all(copies, axes, 0, 0, tiled=True)  7.64 us
    ppermute x2, starting transfers between devices, exchanged(): lax.ppermute(first, axis, backward)  6.76 us
    ppermute x2, waiting for transfers between devices, exchanged(): lax.ppermute(first, axis, backward)  6.66 us
  transfers between devices with their start and end apart: 7, of which 6 were waited for; matrix products, arithmetic and copies ran while one was open for 0% of the time, Pallas kernels for 4%

profile of v3, /device:TPU:1, one launch (start us, length us, event | category | flops | bytes accessed | tf_op | source)
XLA Modules:
  0.0 105.6 jit_solution(13821454722623898336)
XLA Ops:
  0.6 0.0 copy-start.3
  0.6 0.0 copy-start
  0.7 0.0 copy-start.2
  0.7 0.0 copy-start.1
  0.7 1.4 %row_pack.1 = (bf16[512,256]{1,0:T(8,128)(2,1)S(1)}, bf16[512,256]{1,0:T(8,128)(2,1)S(1)}, bf16[16,16,256]{2,1,0:T(8,128)(2,1)S(1)}, bf16[16,16,256]{2,1,0:T(8,1...) custom-call(bf16[1024,256]{1,0:T(8,128)(2,1)} %bitcast.6, ...), custom_call_target="tpu_custom_call" | custom-call | tf_op jit(solution)/shard_map/row_pack/pallas_call | solution.py:107
  2.1 4.6 %collective-permute-start = (bf16[512,256]{1,0:T(8,128)(2,1)S(1)}, bf16[512,256]{1,0:T(8,128)(2,1)S(1)}, u32[]{:S(2)}, u32[]{:S(2)}) collective-permute-start(bf16[512,256]{1,0:T(8,128)(2,1)S(1)} %get-tuple-element.26), channel_id=1, source_target_pairs={{0,32},{32,64},{64,96},{96,128},{128,160},{160,192},{192,224},{224... | collective-permute-start | bytes 786440 | tf_op jit(solution)/shard_map/ppermute | solution.py:186
  6.7 5.5 %collective-permute-start.1 = (bf16[512,256]{1,0:T(8,128)(2,1)S(1)}, bf16[512,256]{1,0:T(8,128)(2,1)S(1)}, u32[]{:S(2)}, u32[]{:S(2)}) collective-permute-start(bf16[512,256]{1,0:T(8,128)(2,1)S(1)} %get-tuple-element.27), channel_id=1, source_target_pairs={{32,0},{64,32},{96,64},{128,96},{160,128},{192,160},{224,192},{256... | collective-permute-start | bytes 786440 | tf_op jit(solution)/shard_map/ppermute | solution.py:186
  12.2 0.0 collective-permute-done.refs_5_.above_ref
  12.2 2.2 %collective-permute-done.1.refs_6_.below_ref = bf16[512,256]{1,0:T(8,128)(2,1)S(1)} collective-permute-done((bf16[512,256]{1,0:T(8,128)(2,1)S(1)}, bf16[512,256]{1,0:T(8,128)(2,1)S(1)}, u32[]{:S(2)}, u32[]{:S(2)}) %collective-permute-start.1) | collective-permute-done | bytes 262176 | tf_op jit(solution)/shard_map/ppermute | solution.py:186
  14.4 0.2 col_pack.1
  14.5 4.0 %collective-permute-start.2 = (bf16[320,256]{1,0:T(8,128)(2,1)S(1)}, bf16[320,256]{1,0:T(8,128)(2,1)S(1)}, u32[]{:S(2)}, u32[]{:S(2)}) collective-permute-start(bf16[320,256]{1,0:T(8,128)(2,1)S(1)} %get-tuple-element.32), channel_id=1, source_target_pairs={{0,1},{1,2},{2,3},{3,4},{4,5},{5,6},{6,7},{7,8},{8,9},{9,10},{10,1... | collective-permute-start | bytes 491528 | tf_op jit(solution)/shard_map/ppermute | solution.py:186
  18.6 1.3 %collective-permute-start.3 = (bf16[320,256]{1,0:T(8,128)(2,1)S(1)}, bf16[320,256]{1,0:T(8,128)(2,1)S(1)}, u32[]{:S(2)}, u32[]{:S(2)}) collective-permute-start(bf16[320,256]{1,0:T(8,128)(2,1)S(1)} %get-tuple-element.33), channel_id=1, source_target_pairs={{1,0},{2,1},{3,2},{4,3},{5,4},{6,5},{7,6},{8,7},{9,8},{10,9},{11,1... | collective-permute-start | bytes 491528 | tf_op jit(solution)/shard_map/ppermute | solution.py:186
  19.9 0.9 collective-permute-done.2.left_ref
  20.8 4.5 %collective-permute-done.3.right_ref = bf16[320,256]{1,0:T(8,128)(2,1)S(1)} collective-permute-done((bf16[320,256]{1,0:T(8,128)(2,1)S(1)}, bf16[320,256]{1,0:T(8,128)(2,1)S(1)}, u32[]{:S(2)}, u32[]{:S(2)}) %collective-permute-start.3) | collective-permute-done | bytes 163872 | tf_op jit(solution)/shard_map/ppermute | solution.py:186
  25.2 0.0 copy-done.3
  25.3 0.0 copy-done
  25.3 0.0 copy-done.2
  25.3 0.0 copy-done.1
  25.3 8.5 %main.1 = (bf16[3,320,256]{2,1,0:T(8,128)(2,1)}, bf16[768,256]{1,0:T(8,128)(2,1)S(1)}, bf16[768,256]{1,0:T(8,128)(2,1)S(1)}, bf16[4160,256]{1,0:T(8,128)(2,1)S(1)}, bf16[1600,256]{1,0:T(8,128)(2,1)}) custom-call(bf16[1024,256]{1,0:T(8,128)(2,1)S(1)} %bitcast.7, bf16[256,256]{1,0:T(8,128)(2,1)S(1)} %bitcast.11, bf16[3,256,256]{2,1,0:T(8,128)(2,1)S(1)} %copy-done.1, ...), custom_call_target="tpu_custom_call" | custom-call | tf_op jit(solution)/shard_map/main/pallas_call | solution.py:488
  33.8 1.9 %collective-permute-start.4 = (bf16[768,256]{1,0:T(8,128)(2,1)S(1)}, bf16[768,256]{1,0:T(8,128)(2,1)S(1)}, u32[]{:S(2)}, u32[]{:S(2)}) collective-permute-start(bf16[768,256]{1,0:T(8,128)(2,1)S(1)} %get-tuple-element.35), channel_id=1, source_target_pairs={{0,32},{32,0},{1,33},{33,1},{2,34},{34,2},{3,35},{35,3},{4,36},{36... | collective-permute-start | bytes 1179656 | tf_op jit(solution)/shard_map/ppermute | solution.py:558
  35.8 1.7 %collective-permute-done.4 = bf16[768,256]{1,0:T(8,128)(2,1)S(1)} collective-permute-done((bf16[768,256]{1,0:T(8,128)(2,1)S(1)}, bf16[768,256]{1,0:T(8,128)(2,1)S(1)}, u32[]{:S(2)}, u32[]{:S(2)}) %collective-permute-start.4) | collective-permute-done | bytes 393248 | tf_op jit(solution)/shard_map/ppermute | solution.py:558
  37.4 0.1 add_convert_fusion
  37.6 24.2 %all_to_all.15 = bf16[32,24,256]{2,1,0:T(8,128)(2,1)S(1)} all-to-all(bf16[32,24,256]{2,1,0:T(8,128)(2,1)S(1)} %bitcast.12), channel_id=1, replica_groups=mesh['grp_0'=8,'grp_1'=2,'dev_0'=4,'dev_1'=8] {'dev_0','dev_1'}, dimensions={0} | all-to-all | bytes 786432 | tf_op jit(solution)/shard_map/all_to_all | solution.py:548
  61.8 0.1 reduce_sum.24
  61.9 15.0 %all_to_all.16 = bf16[8,24,256]{2,1,0:T(8,128)(2,1)S(1)} all-to-all(bf16[8,24,256]{2,1,0:T(8,128)(2,1)S(1)} %broadcast_in_dim.6), channel_id=1, replica_groups=mesh['grp_0'=8,'grp_1'=2,'dev_0'=4,'dev_1'=8] {'grp_0'}, dimensions={0} | all-to-all | bytes 196608 | tf_op jit(solution)/shard_map/all_to_all | solution.py:554
  76.9 0.8 broadcast_in_dim.7
  77.7 7.6 %all-to-all-start.2 = ((bf16[32,24,256]{2,1,0:T(8,128)(2,1)}), bf16[32,24,256]{2,1,0:T(8,128)(2,1)S(1)}, u32[]{:S(2)}, u32[]{:S(2)}) async-start(bf16[32,24,256]{2,1,0:T(8,128)(2,1)} %broadcast_in_dim.7), calls=%async_computation.2 | async-start | bytes 786432 | tf_op jit(solution)/shard_map/all_to_all | solution.py:554
  85.4 4.0 %tail.1 = (bf16[1024,256]{1,0:T(8,128)(2,1)}, bf16[256,256]{1,0:T(8,128)(2,1)}) custom-call(bf16[3,320,256]{2,1,0:T(8,128)(2,1)} %get-tuple-element.36.terms_ref, bf16[4160,256]{1,0:T(8,128)(2,1)S(1)} %get-tuple-element.37.table_ref, bf16[1600,256]{1,0:T(8,128)(2,1)} %get-tuple-element.38.grad_ref, bf16[3,256,256]{2,1,0:T(8,128)(2,1)S(1)} %copy-done.1, ...), custom_call_target="tpu_custom_call" | custom-call | tf_op jit(solution)/shard_map/tail/pallas_call | solution.py:531
  89.4 6.2 %all-to-all-done.2 = bf16[32,24,256]{2,1,0:T(8,128)(2,1)S(1)} async-done(((bf16[32,24,256]{2,1,0:T(8,128)(2,1)}), bf16[32,24,256]{2,1,0:T(8,128)(2,1)S(1)}, u32[]{:S(2)}, u32[]{:S(2)}) %all-to-all-start.2) | async-done | bytes 393248 | tf_op jit(solution)/shard_map/all_to_all | solution.py:554
  95.6 7.2 %collective-permute-start.5 = (bf16[768,256]{1,0:T(8,128)(2,1)S(1)}, bf16[768,256]{1,0:T(8,128)(2,1)S(1)}, u32[]{:S(2)}, u32[]{:S(2)}) collective-permute-start(bf16[768,256]{1,0:T(8,128)(2,1)S(1)} %bitcast.8), channel_id=1, source_target_pairs={{0,32},{32,0},{1,33},{33,1},{2,34},{34,2},{3,35},{35,3},{4,36},{36... | collective-permute-start | bytes 1179656 | tf_op jit(solution)/shard_map/ppermute | solution.py:558
  102.8 1.3 %collective-permute-done.5.other_ref = bf16[768,256]{1,0:T(8,128)(2,1)S(1)} collective-permute-done((bf16[768,256]{1,0:T(8,128)(2,1)S(1)}, bf16[768,256]{1,0:T(8,128)(2,1)S(1)}, u32[]{:S(2)}, u32[]{:S(2)}) %collective-permute-start.5) | collective-permute-done | bytes 393248 | tf_op jit(solution)/shard_map/ppermute | solution.py:558
  104.1 1.5 %clip.1 = (f32[3,256,256]{2,1,0:T(8,128)}, f32[3,256,256]{2,1,0:T(8,128)}) custom-call(bf16[768,256]{1,0:T(8,128)(2,1)S(1)} %bitcast.9, bf16[768,256]{1,0:T(8,128)(2,1)S(1)} %collective-permute-done.5.other_ref), custom_call_target="tpu_custom_call" | custom-call | tf_op jit(solution)/shard_map/clip/pallas_call | solution.py:586
  (2 shorter events, 0.0 us)
Async XLA Ops:
  0.6 24.6 %copy-start.3 = (bf16[8,32,256]{2,1,0:T(8,128)(2,1)S(1)}, bf16[8,32,256]{2,1,0:T(8,128)(2,1)}, u32[]{:S(2)}) copy-start(bf16[8,32,256]{2,1,0:T(8,128)(2,1)} %ct_rows.1) | copy-start | bytes 393220
  0.6 24.6 %copy-start = (bf16[16,64,256]{2,1,0:T(8,128)(2,1)S(1)}, bf16[16,64,256]{2,1,0:T(8,128)(2,1)}, u32[]{:S(2)}) copy-start(bf16[16,64,256]{2,1,0:T(8,128)(2,1)} %px_rows.1) | copy-start | bytes 1572868
  0.7 24.6 %copy-start.2 = (bf16[3,256,256]{2,1,0:T(8,128)(2,1)S(1)}, bf16[3,256,256]{2,1,0:T(8,128)(2,1)}, u32[]{:S(2)}) copy-start(bf16[3,256,256]{2,1,0:T(8,128)(2,1)} %w2_ref.1) | copy-start | bytes 1179652
  0.7 24.6 %copy-start.1 = (bf16[3,256,256]{2,1,0:T(8,128)(2,1)S(1)}, bf16[3,256,256]{2,1,0:T(8,128)(2,1)}, u32[]{:S(2)}) copy-start(bf16[3,256,256]{2,1,0:T(8,128)(2,1)} %w_ref.1) | copy-start | bytes 1179652
  2.1 10.1 %collective-permute-start = (bf16[512,256]{1,0:T(8,128)(2,1)S(1)}, bf16[512,256]{1,0:T(8,128)(2,1)S(1)}, u32[]{:S(2)}, u32[]{:S(2)}) collective-permute-start(bf16[512,256]{1,0:T(8,128)(2,1)S(1)} %get-tuple-element.26), channel_id=1, source_target_pairs={{0,32},{32,64},{64,96},{96,128},{128,160},{160,192},{192,224},{224... | collective-permute-start | bytes 786440 | tf_op jit(solution)/shard_map/ppermute | solution.py:186
  6.7 7.7 %collective-permute-start.1 = (bf16[512,256]{1,0:T(8,128)(2,1)S(1)}, bf16[512,256]{1,0:T(8,128)(2,1)S(1)}, u32[]{:S(2)}, u32[]{:S(2)}) collective-permute-start(bf16[512,256]{1,0:T(8,128)(2,1)S(1)} %get-tuple-element.27), channel_id=1, source_target_pairs={{32,0},{64,32},{96,64},{128,96},{160,128},{192,160},{224,192},{256... | collective-permute-start | bytes 786440 | tf_op jit(solution)/shard_map/ppermute | solution.py:186
  14.5 6.2 %collective-permute-start.2 = (bf16[320,256]{1,0:T(8,128)(2,1)S(1)}, bf16[320,256]{1,0:T(8,128)(2,1)S(1)}, u32[]{:S(2)}, u32[]{:S(2)}) collective-permute-start(bf16[320,256]{1,0:T(8,128)(2,1)S(1)} %get-tuple-element.32), channel_id=1, source_target_pairs={{0,1},{1,2},{2,3},{3,4},{4,5},{5,6},{6,7},{7,8},{8,9},{9,10},{10,1... | collective-permute-start | bytes 491528 | tf_op jit(solution)/shard_map/ppermute | solution.py:186
  18.6 6.7 %collective-permute-start.3 = (bf16[320,256]{1,0:T(8,128)(2,1)S(1)}, bf16[320,256]{1,0:T(8,128)(2,1)S(1)}, u32[]{:S(2)}, u32[]{:S(2)}) collective-permute-start(bf16[320,256]{1,0:T(8,128)(2,1)S(1)} %get-tuple-element.33), channel_id=1, source_target_pairs={{1,0},{2,1},{3,2},{4,3},{5,4},{6,5},{7,6},{8,7},{9,8},{10,9},{11,1... | collective-permute-start | bytes 491528 | tf_op jit(solution)/shard_map/ppermute | solution.py:186
  33.8 3.6 %collective-permute-start.4 = (bf16[768,256]{1,0:T(8,128)(2,1)S(1)}, bf16[768,256]{1,0:T(8,128)(2,1)S(1)}, u32[]{:S(2)}, u32[]{:S(2)}) collective-permute-start(bf16[768,256]{1,0:T(8,128)(2,1)S(1)} %get-tuple-element.35), channel_id=1, source_target_pairs={{0,32},{32,0},{1,33},{33,1},{2,34},{34,2},{3,35},{35,3},{4,36},{36... | collective-permute-start | bytes 1179656 | tf_op jit(solution)/shard_map/ppermute | solution.py:558
  77.7 17.9 %all-to-all-start.2 = ((bf16[32,24,256]{2,1,0:T(8,128)(2,1)}), bf16[32,24,256]{2,1,0:T(8,128)(2,1)S(1)}, u32[]{:S(2)}, u32[]{:S(2)}) async-start(bf16[32,24,256]{2,1,0:T(8,128)(2,1)} %broadcast_in_dim.7), calls=%async_computation.2 | async-start | bytes 786432 | tf_op jit(solution)/shard_map/all_to_all | solution.py:554
  95.6 8.5 %collective-permute-start.5 = (bf16[768,256]{1,0:T(8,128)(2,1)S(1)}, bf16[768,256]{1,0:T(8,128)(2,1)S(1)}, u32[]{:S(2)}, u32[]{:S(2)}) collective-permute-start(bf16[768,256]{1,0:T(8,128)(2,1)S(1)} %bitcast.8), channel_id=1, source_target_pairs={{0,32},{32,0},{1,33},{33,1},{2,34},{34,2},{3,35},{35,3},{4,36},{36... | collective-permute-start | bytes 1179656 | tf_op jit(solution)/shard_map/ppermute | solution.py:558

commit v4 on v3

--- a/solution.py
+++ b/solution.py
@@ -188,11 +188,13 @@
 
 def inverse_roots(h, inside):
     degree = jnp.zeros_like(h)
+    edges = {}
     for row_step, col_step, coupling in STEPS:
-        other = rolled(rolled(h, -row_step, 0), -col_step, 1)
-        present = rolled(rolled(inside, -row_step, 0), -col_step, 1)
-        degree = degree + coupling * present * jnp.exp(-(h - other) * (h - other))
-    return lax.rsqrt(degree + 1.0 - inside) * inside
+        other = rolled(rolled(h, row_step, 0), col_step, 1)
+        present = rolled(rolled(inside, row_step, 0), col_step, 1)
+        edges[row_step, col_step] = jnp.exp(-(h - other) * (h - other))
+        degree = degree + coupling * present * edges[row_step, col_step]
+    return lax.rsqrt(degree + 1.0 - inside) * inside, edges
 
 
 def couplings(row_gap, col_gap):
@@ -202,11 +204,11 @@
     return jnp.where(row_gap == 0, own, jnp.where(jnp.abs(row_gap) == 1, side, 0.0))
 
 
-def fine_windows(x):
-    lane = lax.broadcasted_iota(jnp.int32, x.shape, 1)
-    over = rolled(x, EC, 1)
-    low = jnp.where(lane < EC, rolled(x, 1, 0), over)
-    high = jnp.where(lane < 2 * EC - 128, over, rolled(rolled(x, -1, 0), 2 * EC - 128, 1))
+def fine_windows(above, own, below):
+    lane = lax.broadcasted_iota(jnp.int32, own.shape, 1)
+    over = rolled(own, EC, 1)
+    low = jnp.where(lane < EC, rolled(above, 1, 0), over)
+    high = jnp.where(lane < 2 * EC - 128, over, rolled(rolled(below, -1, 0), 2 * EC - 128, 1))
     return jnp.concatenate([low, high], 1)
 
 
@@ -247,10 +249,10 @@
 
 def main_kernel(px_hbm, ct_hbm, w1_hbm, w2_hbm, off_ref, above_ref, below_ref, left_ref, right_ref, *rest):
     terms_hbm, keep_ref, send_ref, table_ref, grad_hbm = rest[:5]
-    (h_ref, hw_ref, sw_ref, pxe_ref, f1_ref, f2_ref, f1c_ref, f2c_ref, slope_ref, hid_ref,
+    (h_ref, hw_ref, pick_ref, phw_ref, psw_ref, pxe_ref, f1_ref, f2_ref, f1c_ref, f2c_ref, slope_ref, hid_ref,
      poolf_ref, p1f_ref, p2f_ref, ctf_ref, ptab_ref, pb_ref, p1b_ref, ctb_ref, topb_ref,
      midf_ref, midb_ref, pgf_ref, sp_ref, agc_ref, halves_ref, px_ref, ct_ref, w1_ref, w2_ref,
-     terms_ref, grad_ref, sems, out_sems) = rest[5:]
+     terms_ref, grad_ref, pxt_ref, f1t_ref, f2t_ref, sems, out_sems) = rest[5:]
     copies = started(
         sems, [(px_hbm, px_ref), (ct_hbm, ct_ref), (w1_hbm, w1_ref), (w2_hbm, w2_ref)]
     )
@@ -281,7 +283,7 @@
     inside = (
         (row_id >= 0) & (row_id < rows_all) & (col_id >= 0) & (col_id < cols_all) & (c < EC)
     ).astype(F32)
-    s = inverse_roots(h, inside)
+    s, edges = inverse_roots(h, inside)
 
     pick_r = lax.broadcasted_iota(jnp.int32, (OR // 2, OR), 1) // 2
     pick_r = jnp.where(pick_r == lax.broadcasted_iota(jnp.int32, (OR // 2, OR), 0), 0.5, 0.0)
@@ -296,23 +298,42 @@
     pinside = (
         (prow >= 0) & (prow < rows_all // 2) & (pcol >= 0) & (pcol < cols_all // 2) & (pc < QC)
     ).astype(F32)
-    ps = inverse_roots(ph, pinside)
-
-    hw_ref[0:OR, :] = fine_windows(h)
-    sw_ref[0:OR, :] = fine_windows(s)
-    hw_ref[OR : OR + OR // 2, :] = pooled_windows(ph)
-    sw_ref[OR : OR + OR // 2, :] = pooled_windows(ps)
-    ht, st = transposed(h), transposed(s)
-    pht, pst = transposed(ph), transposed(ps)
+    ps, _ = inverse_roots(ph, pinside)
+
     k = lax.broadcasted_iota(jnp.int32, (EC, 256), 1)
     i = lax.broadcasted_iota(jnp.int32, (EC, 256), 0)
     block = (k >= EC).astype(jnp.int32) + (k >= 2 * EC).astype(jnp.int32)
-    link = -couplings(block - 1, k - block * EC - i)
+    gap = jnp.where(k < 3 * EC, k - block * EC - i, 9)
+    for n, col_step in enumerate((-1, 0, 1)):
+        parts = []
+        for row_step in (-1, 0, 1):
+            if (row_step, col_step) == (0, 0):
+                parts.append(jnp.zeros_like(h))
+                continue
+            coupling = 0.5 if row_step and col_step else 1.0
+            other = rolled(rolled(s, row_step, 0), col_step, 1)
+            parts.append(-coupling * edges[row_step, col_step] * (s * other))
+        window = fine_windows(*parts)
+        high = window.astype(BF).astype(F32)
+        hw_ref[n] = high
+        hw_ref[3 + n] = window - high
+        pick_ref[n] = jnp.where(gap == col_step, 1.0, 0.0).astype(BF)
     for r in range(1, ER - 1):
         at = r + 2
-        gap = ht[0:EC, at : at + 1] - hw_ref[at : at + 1, :]
-        scale = st[0:EC, at : at + 1] * sw_ref[at : at + 1, :]
-        table_ref[2 * (r - 1) * EC : 2 * r * EC, :] = in_two(link * jnp.exp(-gap * gap) * scale)
+        for part in (0, 1):
+            lines = []
+            for n in range(3):
+                line = hw_ref[3 * part + n, at : at + 1, :]
+                lines.append(jnp.broadcast_to(line, (16, 256)).astype(BF))
+            base = (2 * (r - 1) + part) * EC
+            for t in range(0, EC, 16):
+                picked = pick_ref[0, t : t + 16, :] * lines[0]
+                picked = picked + pick_ref[1, t : t + 16, :] * lines[1]
+                picked = picked + pick_ref[2, t : t + 16, :] * lines[2]
+                table_ref[base + t : base + t + 16, :] = picked
+    phw_ref[...] = pooled_windows(ph)
+    psw_ref[...] = pooled_windows(ps)
+    pht, pst = transposed(ph), transposed(ps)
     k = lax.broadcasted_iota(jnp.int32, (QC, 256), 1)
     i = lax.broadcasted_iota(jnp.int32, (QC, 256), 0)
     block = sum((k >= QC * j).astype(jnp.int32) for j in range(1, 6))
@@ -323,8 +344,8 @@
             both = []
             for jj in (j, j + 1):
                 col = at + jj
-                gap = pht[0:QC, col : col + 1] - hw_ref[OR + at : OR + at + 1, :]
-                scale = pst[0:QC, col : col + 1] * sw_ref[OR + at : OR + at + 1, :]
+                gap = pht[0:QC, col : col + 1] - phw_ref[at : at + 1, :]
+                scale = pst[0:QC, col : col + 1] * psw_ref[at : at + 1, :]
                 both.append(plinks[jj] * jnp.exp(-gap * gap) * scale)
             two = in_two(jnp.concatenate(both, 0))
             at_row = 2 * b * 160 + j * QC
@@ -358,12 +379,19 @@
     def table_of(r):
         return table_ref[2 * (r - 1) * EC : 2 * r * EC, 0 : 3 * EC]
 
+    def turn(ref, to_ref, n):
+        to_ref[:, n * 128 : (n + 1) * 128] = ref[n * 128 : (n + 1) * 128, :].T
+
     for r in range(1, ER - 1):
+        if 4 <= r < 20 and r % 2 == 0:
+            turn(px_ref, pxt_ref, (r - 4) // 2)
         one = applied(table_of(r), pxe_ref[(r - 1) * EC : (r + 2) * EC, :])
         f1_ref[(r - 1) * EC : r * EC, :] = one.astype(BF)
         if HR <= r < HR + R:
             f1c_ref[(r - HR) * C : (r - HR + 1) * C, :] = one[HC : HC + C].astype(BF)
     for r in range(2, ER - 2):
+        if 4 <= r < 20 and r % 2 == 0:
+            turn(f1c_ref, f1t_ref, (r - 4) // 2)
         two = 2.0 * applied(table_of(r), f1_ref[(r - 2) * EC : (r + 1) * EC, :])
         two = two - pxe_ref[r * EC : (r + 1) * EC, :].astype(F32)
         f2_ref[(r - 2) * EC : (r - 1) * EC, :] = two.astype(BF)
@@ -374,12 +402,17 @@
     midf_ref[...] = jnp.zeros_like(midf_ref)
     for b in range(6):
         r = 2 + 4 * b
-        act = mm(pxe_ref[r * EC : (r + 4) * EC, :], w1_ref[0])
-        act = act + mm(f1_ref[(r - 1) * EC : (r + 3) * EC, :], w1_ref[1])
-        act = act + mm(f2_ref[(r - 2) * EC : (r + 2) * EC, :], w1_ref[2])
-        sig = 1.0 / (1.0 + jnp.exp(-act))
-        slope_ref[(r - 2) * EC : (r + 2) * EC, :] = sig * (1.0 + act * (1.0 - sig))
+        terms = [
+            pxe_ref[r * EC : (r + 4) * EC, :],
+            f1_ref[(r - 1) * EC : (r + 3) * EC, :],
+            f2_ref[(r - 2) * EC : (r + 2) * EC, :],
+        ]
+        act = mm(jnp.concatenate(terms, 1), w1_ref[...].reshape(3 * F, F))
+        sig = 0.5 * jnp.tanh(0.5 * act) + 0.5
         hid = act * sig
+        slope_ref[(r - 2) * EC : (r + 2) * EC, :] = sig + hid * (1.0 - sig)
+        for n in ((0, 1), (2, 3), (4,), (5,), (6,), (7,))[b]:
+            turn(f2c_ref, f2t_ref, n)
         for n in (0, 1):
             half = hid[:, n * 128 : (n + 1) * 128]
             ref = hid_ref.at[2 * b + n]
@@ -442,8 +475,8 @@
                 agc_ref[(r - HR) * C : (r - HR + 1) * C, :] = grad_row[HC : HC + C].astype(BF)
     outward.append(pltpu.make_async_copy(grad_ref, grad_hbm, out_sems.at[1]))
     outward[1].start()
-    for n, ref in enumerate((px_ref, f1c_ref, f2c_ref)):
-        halves_ref[core, n * F : (n + 1) * F, :] = mm_tn(ref[...], agc_ref[...]).astype(BF)
+    for n, ref in enumerate((pxt_ref, f1t_ref, f2t_ref)):
+        halves_ref[core, n * F : (n + 1) * F, :] = mm(ref[...], agc_ref[...]).astype(BF)
     keep_ref[...] = halves_ref[0]
     send_ref[...] = halves_ref[1]
     for copy in outward:
@@ -454,8 +487,10 @@
     fine, pooled = ER * EC, QR * QC
     scratch = [
         ((OR, 128), F32),
-        ((OR + OR // 2, 256), F32),
-        ((OR + OR // 2, 256), F32),
+        ((6, OR, 256), F32),
+        ((3, EC, 256), BF),
+        ((OR // 2, 256), F32),
+        ((OR // 2, 256), F32),
         ((fine, F), BF),
         ((26 * EC, F), BF),
         ((24 * EC, F), BF),
@@ -484,6 +519,9 @@
         ((3, F, F), BF),
         ((3, PR * QC, F), BF),
         ((20 * EC, F), BF),
+        ((F, R * C), BF),
+        ((F, R * C), BF),
+        ((F, R * C), BF),
     ]
     return pl.pallas_call(
         main_kernel,

time: 106 us -> 106 us (level)
  no operation moved by 1% of the time
where the time goes in v4:
time: 106 us; the launch traced here: 105 us
  blocking collectives  39.3 us (37%)
  starting transfers between devices  32 us (30%)
  waiting for transfers between devices  16.8 us (16%)
  Pallas kernels  15.3 us (14%)
    all_to_all x1, blocking collectives, sum_at_owner(): lax.all_to_all(value.reshape(lax.axis_size(axes), -1, F), axes, 0, 0, til...  24.2 us
    all_to_all x1, blocking collectives, sent_to_all(): return lax.all_to_all(copies, axes, 0, 0, tiled=True)  15 us
    ppermute x2, starting transfers between devices, swapped(): return lax.ppermute(value, 'grp_1', [(0, 1), (1, 0)])  9.07 us
    ppermute x2, starting transfers between devices, exchanged(): lax.ppermute(last, axis, forward)  8.58 us
    pallas_call x1, Pallas kernels, main_stage(): pl.pallas_call(main_kernel, out_shape=[pltpu.HBM((3, PR * QC, F), BF), pl...  8.16 us
    all_to_all x1, starting transfers between devices, sent_to_all(): return lax.all_to_all(copies, axes, 0, 0, tiled=True)  7.64 us
    ppermute x2, starting transfers between devices, exchanged(): lax.ppermute(first, axis, backward)  6.76 us
    ppermute x2, waiting for transfers between devices, exchanged(): lax.ppermute(first, axis, backward)  6.66 us
  transfers between devices with their start and end apart: 7, of which 6 were waited for; matrix products, arithmetic and copies ran while one was open for 0% of the time, Pallas kernels for 4%

profile of v4, /device:TPU:1, one launch (start us, length us, event | category | flops | bytes accessed | tf_op | source)
XLA Modules:
  0.0 105.2 jit_solution(69415438489729548)
XLA Ops:
  0.6 0.0 copy-start.3
  0.6 0.0 copy-start
  0.7 0.0 copy-start.2
  0.7 0.0 copy-start.1
  0.7 1.4 %row_pack.1 = (bf16[512,256]{1,0:T(8,128)(2,1)S(1)}, bf16[512,256]{1,0:T(8,128)(2,1)S(1)}, bf16[16,16,256]{2,1,0:T(8,128)(2,1)S(1)}, bf16[16,16,256]{2,1,0:T(8,1...) custom-call(bf16[1024,256]{1,0:T(8,128)(2,1)} %bitcast.6, ...), custom_call_target="tpu_custom_call" | custom-call | tf_op jit(solution)/shard_map/row_pack/pallas_call | solution.py:107
  2.1 4.6 %collective-permute-start = (bf16[512,256]{1,0:T(8,128)(2,1)S(1)}, bf16[512,256]{1,0:T(8,128)(2,1)S(1)}, u32[]{:S(2)}, u32[]{:S(2)}) collective-permute-start(bf16[512,256]{1,0:T(8,128)(2,1)S(1)} %get-tuple-element.26), channel_id=1, source_target_pairs={{0,32},{32,64},{64,96},{96,128},{128,160},{160,192},{192,224},{224... | collective-permute-start | bytes 786440 | tf_op jit(solution)/shard_map/ppermute | solution.py:186
  6.7 5.5 %collective-permute-start.1 = (bf16[512,256]{1,0:T(8,128)(2,1)S(1)}, bf16[512,256]{1,0:T(8,128)(2,1)S(1)}, u32[]{:S(2)}, u32[]{:S(2)}) collective-permute-start(bf16[512,256]{1,0:T(8,128)(2,1)S(1)} %get-tuple-element.27), channel_id=1, source_target_pairs={{32,0},{64,32},{96,64},{128,96},{160,128},{192,160},{224,192},{256... | collective-permute-start | bytes 786440 | tf_op jit(solution)/shard_map/ppermute | solution.py:186
  12.2 0.0 collective-permute-done.refs_5_.above_ref
  12.2 2.2 %collective-permute-done.1.refs_6_.below_ref = bf16[512,256]{1,0:T(8,128)(2,1)S(1)} collective-permute-done((bf16[512,256]{1,0:T(8,128)(2,1)S(1)}, bf16[512,256]{1,0:T(8,128)(2,1)S(1)}, u32[]{:S(2)}, u32[]{:S(2)}) %collective-permute-start.1) | collective-permute-done | bytes 262176 | tf_op jit(solution)/shard_map/ppermute | solution.py:186
  14.4 0.2 col_pack.1
  14.5 4.0 %collective-permute-start.2 = (bf16[320,256]{1,0:T(8,128)(2,1)S(1)}, bf16[320,256]{1,0:T(8,128)(2,1)S(1)}, u32[]{:S(2)}, u32[]{:S(2)}) collective-permute-start(bf16[320,256]{1,0:T(8,128)(2,1)S(1)} %get-tuple-element.32), channel_id=1, source_target_pairs={{0,1},{1,2},{2,3},{3,4},{4,5},{5,6},{6,7},{7,8},{8,9},{9,10},{10,1... | collective-permute-start | bytes 491528 | tf_op jit(solution)/shard_map/ppermute | solution.py:186
  18.6 1.3 %collective-permute-start.3 = (bf16[320,256]{1,0:T(8,128)(2,1)S(1)}, bf16[320,256]{1,0:T(8,128)(2,1)S(1)}, u32[]{:S(2)}, u32[]{:S(2)}) collective-permute-start(bf16[320,256]{1,0:T(8,128)(2,1)S(1)} %get-tuple-element.33), channel_id=1, source_target_pairs={{1,0},{2,1},{3,2},{4,3},{5,4},{6,5},{7,6},{8,7},{9,8},{10,9},{11,1... | collective-permute-start | bytes 491528 | tf_op jit(solution)/shard_map/ppermute | solution.py:186
  19.9 0.9 collective-permute-done.2.left_ref
  20.8 4.5 %collective-permute-done.3.right_ref = bf16[320,256]{1,0:T(8,128)(2,1)S(1)} collective-permute-done((bf16[320,256]{1,0:T(8,128)(2,1)S(1)}, bf16[320,256]{1,0:T(8,128)(2,1)S(1)}, u32[]{:S(2)}, u32[]{:S(2)}) %collective-permute-start.3) | collective-permute-done | bytes 163872 | tf_op jit(solution)/shard_map/ppermute | solution.py:186
  25.2 0.0 copy-done.3
  25.3 0.0 copy-done
  25.3 0.0 copy-done.2
  25.3 0.0 copy-done.1
  25.3 8.2 %main.1 = (bf16[3,320,256]{2,1,0:T(8,128)(2,1)}, bf16[768,256]{1,0:T(8,128)(2,1)S(1)}, bf16[768,256]{1,0:T(8,128)(2,1)S(1)}, bf16[4160,256]{1,0:T(8,128)(2,1)S(1)}, bf16[1600,256]{1,0:T(8,128)(2,1)}) custom-call(bf16[1024,256]{1,0:T(8,128)(2,1)S(1)} %bitcast.7, bf16[256,256]{1,0:T(8,128)(2,1)S(1)} %bitcast.11, bf16[3,256,256]{2,1,0:T(8,128)(2,1)S(1)} %copy-done.1, ...), custom_call_target="tpu_custom_call" | custom-call | tf_op jit(solution)/shard_map/main/pallas_call | solution.py:526
  33.4 1.9 %collective-permute-start.4 = (bf16[768,256]{1,0:T(8,128)(2,1)S(1)}, bf16[768,256]{1,0:T(8,128)(2,1)S(1)}, u32[]{:S(2)}, u32[]{:S(2)}) collective-permute-start(bf16[768,256]{1,0:T(8,128)(2,1)S(1)} %get-tuple-element.35), channel_id=1, source_target_pairs={{0,32},{32,0},{1,33},{33,1},{2,34},{34,2},{3,35},{35,3},{4,36},{36... | collective-permute-start | bytes 1179656 | tf_op jit(solution)/shard_map/ppermute | solution.py:596
  35.4 1.7 %collective-permute-done.4 = bf16[768,256]{1,0:T(8,128)(2,1)S(1)} collective-permute-done((bf16[768,256]{1,0:T(8,128)(2,1)S(1)}, bf16[768,256]{1,0:T(8,128)(2,1)S(1)}, u32[]{:S(2)}, u32[]{:S(2)}) %collective-permute-start.4) | collective-permute-done | bytes 393248 | tf_op jit(solution)/shard_map/ppermute | solution.py:596
  37.1 0.1 add_convert_fusion
  37.2 24.2 %all_to_all.15 = bf16[32,24,256]{2,1,0:T(8,128)(2,1)S(1)} all-to-all(bf16[32,24,256]{2,1,0:T(8,128)(2,1)S(1)} %bitcast.12), channel_id=1, replica_groups=mesh['grp_0'=8,'grp_1'=2,'dev_0'=4,'dev_1'=8] {'dev_0','dev_1'}, dimensions={0} | all-to-all | bytes 786432 | tf_op jit(solution)/shard_map/all_to_all | solution.py:586
  61.4 0.1 reduce_sum.24
  61.5 15.0 %all_to_all.16 = bf16[8,24,256]{2,1,0:T(8,128)(2,1)S(1)} all-to-all(bf16[8,24,256]{2,1,0:T(8,128)(2,1)S(1)} %broadcast_in_dim.6), channel_id=1, replica_groups=mesh['grp_0'=8,'grp_1'=2,'dev_0'=4,'dev_1'=8] {'grp_0'}, dimensions={0} | all-to-all | bytes 196608 | tf_op jit(solution)/shard_map/all_to_all | solution.py:592
  76.6 0.8 broadcast_in_dim.7
  77.3 7.6 %all-to-all-start.2 = ((bf16[32,24,256]{2,1,0:T(8,128)(2,1)}), bf16[32,24,256]{2,1,0:T(8,128)(2,1)S(1)}, u32[]{:S(2)}, u32[]{:S(2)}) async-start(bf16[32,24,256]{2,1,0:T(8,128)(2,1)} %broadcast_in_dim.7), calls=%async_computation.2 | async-start | bytes 786432 | tf_op jit(solution)/shard_map/all_to_all | solution.py:592
  85.0 4.1 %tail.1 = (bf16[1024,256]{1,0:T(8,128)(2,1)}, bf16[256,256]{1,0:T(8,128)(2,1)}) custom-call(bf16[3,320,256]{2,1,0:T(8,128)(2,1)} %get-tuple-element.36.terms_ref, bf16[4160,256]{1,0:T(8,128)(2,1)S(1)} %get-tuple-element.37.table_ref, bf16[1600,256]{1,0:T(8,128)(2,1)} %get-tuple-element.38.grad_ref, bf16[3,256,256]{2,1,0:T(8,128)(2,1)S(1)} %copy-done.1, ...), custom_call_target="tpu_custom_call" | custom-call | tf_op jit(solution)/shard_map/tail/pallas_call | solution.py:569
  89.0 6.2 %all-to-all-done.2 = bf16[32,24,256]{2,1,0:T(8,128)(2,1)S(1)} async-done(((bf16[32,24,256]{2,1,0:T(8,128)(2,1)}), bf16[32,24,256]{2,1,0:T(8,128)(2,1)S(1)}, u32[]{:S(2)}, u32[]{:S(2)}) %all-to-all-start.2) | async-done | bytes 393248 | tf_op jit(solution)/shard_map/all_to_all | solution.py:592
  95.2 7.2 %collective-permute-start.5 = (bf16[768,256]{1,0:T(8,128)(2,1)S(1)}, bf16[768,256]{1,0:T(8,128)(2,1)S(1)}, u32[]{:S(2)}, u32[]{:S(2)}) collective-permute-start(bf16[768,256]{1,0:T(8,128)(2,1)S(1)} %bitcast.8), channel_id=1, source_target_pairs={{0,32},{32,0},{1,33},{33,1},{2,34},{34,2},{3,35},{35,3},{4,36},{36... | collective-permute-start | bytes 1179656 | tf_op jit(solution)/shard_map/ppermute | solution.py:596
  102.4 1.3 %collective-permute-done.5.other_ref = bf16[768,256]{1,0:T(8,128)(2,1)S(1)} collective-permute-done((bf16[768,256]{1,0:T(8,128)(2,1)S(1)}, bf16[768,256]{1,0:T(8,128)(2,1)S(1)}, u32[]{:S(2)}, u32[]{:S(2)}) %collective-permute-start.5) | collective-permute-done | bytes 393248 | tf_op jit(solution)/shard_map/ppermute | solution.py:596
  103.7 1.5 %clip.1 = (f32[3,256,256]{2,1,0:T(8,128)}, f32[3,256,256]{2,1,0:T(8,128)}) custom-call(bf16[768,256]{1,0:T(8,128)(2,1)S(1)} %bitcast.9, bf16[768,256]{1,0:T(8,128)(2,1)S(1)} %collective-permute-done.5.other_ref), custom_call_target="tpu_custom_call" | custom-call | tf_op jit(solution)/shard_map/clip/pallas_call | solution.py:624
  (2 shorter events, 0.0 us)
Async XLA Ops:
  0.6 24.6 %copy-start.3 = (bf16[8,32,256]{2,1,0:T(8,128)(2,1)S(1)}, bf16[8,32,256]{2,1,0:T(8,128)(2,1)}, u32[]{:S(2)}) copy-start(bf16[8,32,256]{2,1,0:T(8,128)(2,1)} %ct_rows.1) | copy-start | bytes 393220
  0.6 24.6 %copy-start = (bf16[16,64,256]{2,1,0:T(8,128)(2,1)S(1)}, bf16[16,64,256]{2,1,0:T(8,128)(2,1)}, u32[]{:S(2)}) copy-start(bf16[16,64,256]{2,1,0:T(8,128)(2,1)} %px_rows.1) | copy-start | bytes 1572868
  0.7 24.6 %copy-start.2 = (bf16[3,256,256]{2,1,0:T(8,128)(2,1)S(1)}, bf16[3,256,256]{2,1,0:T(8,128)(2,1)}, u32[]{:S(2)}) copy-start(bf16[3,256,256]{2,1,0:T(8,128)(2,1)} %w2_ref.1) | copy-start | bytes 1179652
  0.7 24.6 %copy-start.1 = (bf16[3,256,256]{2,1,0:T(8,128)(2,1)S(1)}, bf16[3,256,256]{2,1,0:T(8,128)(2,1)}, u32[]{:S(2)}) copy-start(bf16[3,256,256]{2,1,0:T(8,128)(2,1)} %w_ref.1) | copy-start | bytes 1179652
  2.1 10.1 %collective-permute-start = (bf16[512,256]{1,0:T(8,128)(2,1)S(1)}, bf16[512,256]{1,0:T(8,128)(2,1)S(1)}, u32[]{:S(2)}, u32[]{:S(2)}) collective-permute-start(bf16[512,256]{1,0:T(8,128)(2,1)S(1)} %get-tuple-element.26), channel_id=1, source_target_pairs={{0,32},{32,64},{64,96},{96,128},{128,160},{160,192},{192,224},{224... | collective-permute-start | bytes 786440 | tf_op jit(solution)/shard_map/ppermute | solution.py:186
  6.7 7.7 %collective-permute-start.1 = (bf16[512,256]{1,0:T(8,128)(2,1)S(1)}, bf16[512,256]{1,0:T(8,128)(2,1)S(1)}, u32[]{:S(2)}, u32[]{:S(2)}) collective-permute-start(bf16[512,256]{1,0:T(8,128)(2,1)S(1)} %get-tuple-element.27), channel_id=1, source_target_pairs={{32,0},{64,32},{96,64},{128,96},{160,128},{192,160},{224,192},{256... | collective-permute-start | bytes 786440 | tf_op jit(solution)/shard_map/ppermute | solution.py:186
  14.5 6.2 %collective-permute-start.2 = (bf16[320,256]{1,0:T(8,128)(2,1)S(1)}, bf16[320,256]{1,0:T(8,128)(2,1)S(1)}, u32[]{:S(2)}, u32[]{:S(2)}) collective-permute-start(bf16[320,256]{1,0:T(8,128)(2,1)S(1)} %get-tuple-element.32), channel_id=1, source_target_pairs={{0,1},{1,2},{2,3},{3,4},{4,5},{5,6},{6,7},{7,8},{8,9},{9,10},{10,1... | collective-permute-start | bytes 491528 | tf_op jit(solution)/shard_map/ppermute | solution.py:186
  18.6 6.7 %collective-permute-start.3 = (bf16[320,256]{1,0:T(8,128)(2,1)S(1)}, bf16[320,256]{1,0:T(8,128)(2,1)S(1)}, u32[]{:S(2)}, u32[]{:S(2)}) collective-permute-start(bf16[320,256]{1,0:T(8,128)(2,1)S(1)} %get-tuple-element.33), channel_id=1, source_target_pairs={{1,0},{2,1},{3,2},{4,3},{5,4},{6,5},{7,6},{8,7},{9,8},{10,9},{11,1... | collective-permute-start | bytes 491528 | tf_op jit(solution)/shard_map/ppermute | solution.py:186
  33.4 3.6 %collective-permute-start.4 = (bf16[768,256]{1,0:T(8,128)(2,1)S(1)}, bf16[768,256]{1,0:T(8,128)(2,1)S(1)}, u32[]{:S(2)}, u32[]{:S(2)}) collective-permute-start(bf16[768,256]{1,0:T(8,128)(2,1)S(1)} %get-tuple-element.35), channel_id=1, source_target_pairs={{0,32},{32,0},{1,33},{33,1},{2,34},{34,2},{3,35},{35,3},{4,36},{36... | collective-permute-start | bytes 1179656 | tf_op jit(solution)/shard_map/ppermute | solution.py:596
  77.3 17.9 %all-to-all-start.2 = ((bf16[32,24,256]{2,1,0:T(8,128)(2,1)}), bf16[32,24,256]{2,1,0:T(8,128)(2,1)S(1)}, u32[]{:S(2)}, u32[]{:S(2)}) async-start(bf16[32,24,256]{2,1,0:T(8,128)(2,1)} %broadcast_in_dim.7), calls=%async_computation.2 | async-start | bytes 786432 | tf_op jit(solution)/shard_map/all_to_all | solution.py:592
  95.2 8.5 %collective-permute-start.5 = (bf16[768,256]{1,0:T(8,128)(2,1)S(1)}, bf16[768,256]{1,0:T(8,128)(2,1)S(1)}, u32[]{:S(2)}, u32[]{:S(2)}) collective-permute-start(bf16[768,256]{1,0:T(8,128)(2,1)S(1)} %bitcast.8), channel_id=1, source_target_pairs={{0,32},{32,0},{1,33},{33,1},{2,34},{34,2},{3,35},{35,3},{4,36},{36... | collective-permute-start | bytes 1179656 | tf_op jit(solution)/shard_map/ppermute | solution.py:596

commit v5 on v4

--- a/solution.py
+++ b/solution.py
@@ -80,10 +80,14 @@
 
 
 def row_pack_kernel(px_ref, ct_ref, px_rows, ct_rows, off_ref, *rest):
-    up_ref, down_ref, pxl_ref, pxr_ref, ctl_ref, ctr_ref, wide, off_buf, sems = rest
+    chip_ref, cross_ref, pxl_ref, pxr_ref, ctl_ref, ctr_ref, wide, off_buf, sems = rest
+    core = lax.axis_index("grp_1")
+    ends = ((chip_ref, 1 - core), (cross_ref, core))
     pairs = [(off_ref, off_buf)]
-    for out, px_at, ct_at in ((up_ref, 0, 0), (down_ref, R - HR, PR - 3)):
-        for ref, at, size, to in ((px_ref, px_at * C, HR * C, 0), (ct_ref, ct_at * PC, 3 * PC, ROW_CT)):
+    for out, low_end in ends:
+        px_at = pl.multiple_of(low_end * ((R - HR) * C), 64)
+        ct_at = pl.multiple_of(low_end * ((PR - 3) * PC), 32)
+        for ref, at, size, to in ((px_ref, px_at, HR * C, 0), (ct_ref, ct_at, 3 * PC, ROW_CT)):
             pairs.append((ref.at[pl.ds(at, size), :], out.at[pl.ds(to, size), :]))
     pairs += [
         (px_rows.at[:, pl.ds(0, 16), :], pxl_ref),
@@ -95,8 +99,8 @@
     wide[...] = jnp.zeros_like(wide)
     copies[0].wait()
     wide[:, 0:C] = off_buf[...]
-    for out, off_at in ((up_ref, 0), (down_ref, R - 8)):
-        high, middle, low = in_parts(wide[off_at : off_at + 8, :])
+    for out, low_end in ends:
+        high, middle, low = in_parts(wide[pl.ds(pl.multiple_of(low_end * (R - 8), 8), 8), :])
         packed = jnp.concatenate([high, middle, low, jnp.zeros_like(low)], 0)
         out[ROW_OFF:ROW_END, :] = jnp.concatenate([packed, jnp.zeros_like(packed)], 1).astype(BF)
     for copy in copies[1:]:
@@ -128,19 +132,25 @@
 
 
 def col_pack_kernel(*refs):
-    pxl_ref, pxr_ref, ctl_ref, ctr_ref, off_ref, above_ref, below_ref, left_ref, right_ref, wide = refs
+    pxl_ref, pxr_ref, ctl_ref, ctr_ref, off_ref, chip_ref, cross_ref = refs[:7]
+    first_ref, second_ref, rows_ref, wide, sides = refs[7:]
+    core = lax.axis_index("grp_1")
+    rows_ref[1 - core] = chip_ref[...]
+    rows_ref[core] = cross_ref[...]
+    above_ref, below_ref = rows_ref.at[0], rows_ref.at[1]
+    odd = column_parity()
     wide[8 : 8 + R, :] = off_ref[...]
     wide[0:8, :] = row_offsets(above_ref)
     wide[8 + R : OR, :] = row_offsets(below_ref)
     lane = lax.broadcasted_iota(jnp.int32, (OR, 128), 1)
     near = lax.broadcasted_iota(jnp.int32, (8, F), 0) < 4
-    for out, px_ref, ct_ref, px_at, ct_at, half in (
-        (left_ref, pxl_ref, ctl_ref, 0, 0, slice(0, 8)),
-        (right_ref, pxr_ref, ctr_ref, C - 16, PC - 16, slice(8, 16)),
+    for is_left, out, px_ref, ct_ref, px_at, ct_at, half in (
+        (True, sides.at[1 - odd], pxl_ref, ctl_ref, 0, 0, slice(0, 8)),
+        (False, sides.at[odd], pxr_ref, ctr_ref, C - 16, PC - 16, slice(8, 16)),
     ):
 
         def line(ref, k, base, width, at):
-            if ref is above_ref or ref is below_ref:
+            if len(ref.shape) == 2:
                 return ref[base + k * width + at : base + k * width + at + 16, :].astype(F32)[half]
             return ref[k].astype(F32)[half]
 
@@ -155,35 +165,41 @@
         tiles = []
         for e in range(0, QR, 2):
             first, second = lines[e], lines[e + 1]
-            if out is left_ref:
+            if is_left:
                 second = rolled(second, 4, 0)
             else:
                 first = rolled(first, 4, 0)
             tiles.append(jnp.where(near, first, second))
         tiles.append(jnp.zeros((8, F), F32))
         out[COL_CT:COL_OFF, :] = jnp.concatenate(tiles, 0).astype(BF)
-        part = wide[...] if out is left_ref else rolled(wide[...], HC - C, 1)
+        part = wide[...] if is_left else rolled(wide[...], HC - C, 1)
         high, middle, low = in_parts(jnp.where(lane < HC, part, 0.0))
         packed = high + rolled(middle, HC, 1) + rolled(low, 2 * HC, 1)
         out[COL_OFF:COL_END, :] = jnp.concatenate([packed, jnp.zeros_like(packed)], 1).astype(BF)
+    first_ref[...] = sides[0]
+    second_ref[...] = sides[1]
+
+
+def column_parity():
+    return (lax.axis_index("dev_0") * lax.axis_size("dev_1") + lax.axis_index("dev_1")) % 2
 
 
 def col_messages(*parts):
     shape = pltpu.VMEM((COL_END, F), BF)
     return pl.pallas_call(
         col_pack_kernel,
-        out_shape=[shape, shape],
-        scratch_shapes=[pltpu.VMEM((OR, 128), F32)],
+        out_shape=[shape, shape, pltpu.VMEM((2, ROW_END, F), BF)],
+        scratch_shapes=[pltpu.VMEM((OR, 128), F32), pltpu.VMEM((2, COL_END, F), BF)],
         compiler_params=pltpu.CompilerParams(vmem_limit_bytes=4 << 20),
         name="col_pack",
     )(*on_chip(*parts))
 
 
-def exchanged(first, last, axis):
-    count = lax.axis_size(axis)
-    forward = [(i, i + 1) for i in range(count - 1)]
-    backward = [(i + 1, i) for i in range(count - 1)]
-    return lax.ppermute(last, axis, forward), lax.ppermute(first, axis, backward)
+def paired(message, axis, start):
+    pairs = []
+    for i in range(start, lax.axis_size(axis) - 1, 2):
+        pairs += [(i, i + 1), (i + 1, i)]
+    return lax.ppermute(message, axis, pairs)
 
 
 def inverse_roots(h, inside):
@@ -247,16 +263,21 @@
     return x.T
 
 
-def main_kernel(px_hbm, ct_hbm, w1_hbm, w2_hbm, off_ref, above_ref, below_ref, left_ref, right_ref, *rest):
+def main_kernel(px_hbm, ct_hbm, w1_hbm, w2_hbm, off_ref, first_ref, second_ref, rows_ref, *rest):
     terms_hbm, keep_ref, send_ref, table_ref, grad_hbm = rest[:5]
     (h_ref, hw_ref, pick_ref, phw_ref, psw_ref, pxe_ref, f1_ref, f2_ref, f1c_ref, f2c_ref, slope_ref, hid_ref,
      poolf_ref, p1f_ref, p2f_ref, ctf_ref, ptab_ref, pb_ref, p1b_ref, ctb_ref, topb_ref,
      midf_ref, midb_ref, pgf_ref, sp_ref, agc_ref, halves_ref, px_ref, ct_ref, w1_ref, w2_ref,
-     terms_ref, grad_ref, pxt_ref, f1t_ref, f2t_ref, sems, out_sems) = rest[5:]
+     terms_ref, grad_ref, pxt_ref, f1t_ref, f2t_ref, sides_ref, sems, out_sems) = rest[5:]
     copies = started(
         sems, [(px_hbm, px_ref), (ct_hbm, ct_ref), (w1_hbm, w1_ref), (w2_hbm, w2_ref)]
     )
     core = lax.axis_index("grp_1")
+    odd = column_parity()
+    sides_ref[1 - odd] = first_ref[...]
+    sides_ref[odd] = second_ref[...]
+    left_ref, right_ref = sides_ref.at[0], sides_ref.at[1]
+    above_ref, below_ref = rows_ref.at[0], rows_ref.at[1]
 
     row0 = (lax.axis_index("grp_0") * 2 + lax.axis_index("grp_1")) * R
     col0 = (lax.axis_index("dev_0") * lax.axis_size("dev_1") + lax.axis_index("dev_1")) * C
@@ -522,6 +543,7 @@
         ((F, R * C), BF),
         ((F, R * C), BF),
         ((F, R * C), BF),
+        ((2, COL_END, F), BF),
     ]
     return pl.pallas_call(
         main_kernel,
@@ -533,7 +555,7 @@
             pltpu.HBM((20 * EC, F), BF),
         ],
         in_specs=[pl.BlockSpec(memory_space=pl.ANY)] * 4
-        + [pl.BlockSpec(memory_space=pltpu.VMEM)] * 5,
+        + [pl.BlockSpec(memory_space=pltpu.VMEM)] * 4,
         scratch_shapes=[pltpu.VMEM(shape, dtype) for shape, dtype in scratch]
         + [pltpu.SemaphoreType.DMA((4,)), pltpu.SemaphoreType.DMA((2,))],
         compiler_params=pltpu.CompilerParams(vmem_limit_bytes=20 << 20),
@@ -632,10 +654,11 @@
 def shards(pixels, offsets, first_weights, second_weights, cotangent):
     px = pixels.reshape(R * C, F)
     ct = cotangent.reshape(PR * PC, F)
-    up, down, *strips, wide = row_messages(px, ct, offsets)
-    above, below = exchanged(up, down, GRP)
-    left, right = exchanged(*col_messages(*strips, wide, above, below), DEV)
-    got = (above, below, left, right)
+    chip, cross, *strips, wide = row_messages(px, ct, offsets)
+    cross = paired(cross, GRP, 1)
+    chip = paired(chip, GRP, 0)
+    first, second, rows = col_messages(*strips, wide, chip, cross)
+    got = (paired(first, DEV, 0), paired(second, DEV, 1), rows)
     terms, keep, send, table, grad = main_stage(
         px, ct, wide, first_weights, second_weights, got
     )

time: 106 us -> 106 us (level)
  starting transfers between devices: 32 us -> 30 us
  waiting for transfers between devices: 16.8 us -> 18.7 us
    ppermute x4, starting transfers between devices: 15.3 us -> 13.2 us  [paired(): return lax.ppermute(message, axis, pairs)]
    ppermute x4, waiting for transfers between devices: 7.6 us -> 9.51 us  [paired(): return lax.ppermute(message, axis, pairs)]
  transfers between devices with their start and end apart: 7 -> 7, of which waited for: 6 -> 5; matrix products, arithmetic and copies ran while one was open for 0% -> 0% of each run, Pallas kernels for 4% -> 4%
where the time goes in v5:
time: 106 us
  blocking collectives  39.7 us (37%)
  starting transfers between devices  30 us (28%)
  waiting for transfers between devices  18.7 us (18%)
  Pallas kernels  15.4 us (15%)
    all_to_all x1, blocking collectives, sum_at_owner(): lax.all_to_all(value.reshape(lax.axis_size(axes), -1, F), axes, 0, 0, til...  23.8 us
    all_to_all x1, blocking collectives, sent_to_all(): return lax.all_to_all(copies, axes, 0, 0, tiled=True)  15.9 us
    ppermute x4, starting transfers between devices, paired(): return lax.ppermute(message, axis, pairs)  13.2 us
    ppermute x4, waiting for transfers between devices, paired(): return lax.ppermute(message, axis, pairs)  9.51 us
    ppermute x2, starting transfers between devices, swapped(): return lax.ppermute(value, 'grp_1', [(0, 1), (1, 0)])  9.07 us
    pallas_call x1, Pallas kernels, main_stage(): pl.pallas_call(main_kernel, out_shape=[pltpu.HBM((3, PR * QC, F), BF), pl...  8.24 us
    all_to_all x1, starting transfers between devices, sent_to_all(): return lax.all_to_all(copies, axes, 0, 0, tiled=True)  7.64 us
    all_to_all x1, waiting for transfers between devices, sent_to_all(): return lax.all_to_all(copies, axes, 0, 0, tiled=True)  6.2 us
  transfers between devices with their start and end apart: 7, of which 5 were waited for; matrix products, arithmetic and copies ran while one was open for 0% of the time, Pallas kernels for 4%

profile of v5, /device:TPU:1, one launch (start us, length us, event | category | flops | bytes accessed | tf_op | source)
XLA Modules:
  0.0 105.6 jit_solution(18259639044511781362)
XLA Ops:
  0.6 0.0 copy-start.3
  0.6 0.0 copy-start
  0.7 0.0 copy-start.2
  0.7 0.0 copy-start.1
  0.7 1.4 %row_pack.1 = (bf16[512,256]{1,0:T(8,128)(2,1)S(1)}, bf16[512,256]{1,0:T(8,128)(2,1)S(1)}, bf16[16,16,256]{2,1,0:T(8,128)(2,1)S(1)}, bf16[16,16,256]{2,1,0:T(8,1...) custom-call(bf16[1024,256]{1,0:T(8,128)(2,1)} %bitcast.6, ...), custom_call_target="tpu_custom_call" | custom-call | tf_op jit(solution)/shard_map/row_pack/pallas_call | solution.py:111
  2.1 8.7 %collective-permute-start = (bf16[512,256]{1,0:T(8,128)(2,1)S(1)}, bf16[512,256]{1,0:T(8,128)(2,1)S(1)}, u32[]{:S(2)}, u32[]{:S(2)}) collective-permute-start(bf16[512,256]{1,0:T(8,128)(2,1)S(1)} %get-tuple-element.31), channel_id=1, source_target_pairs={{0,32},{32,0},{64,96},{96,64},{128,160},{160,128},{192,224},{224,1... | collective-permute-start | bytes 786440 | tf_op jit(solution)/shard_map/ppermute | solution.py:202
  10.8 1.9 %collective-permute-start.1 = (bf16[512,256]{1,0:T(8,128)(2,1)S(1)}, bf16[512,256]{1,0:T(8,128)(2,1)S(1)}, u32[]{:S(2)}, u32[]{:S(2)}) collective-permute-start(bf16[512,256]{1,0:T(8,128)(2,1)S(1)} %get-tuple-element.32), channel_id=1, source_target_pairs={{32,64},{64,32},{96,128},{128,96},{160,192},{192,160},{224,256},{2... | collective-permute-start | bytes 786440 | tf_op jit(solution)/shard_map/ppermute | solution.py:202
  12.8 0.0 collective-permute-done.refs_5_
  12.8 6.0 %collective-permute-done.1.refs_6_ = bf16[512,256]{1,0:T(8,128)(2,1)S(1)} collective-permute-done((bf16[512,256]{1,0:T(8,128)(2,1)S(1)}, bf16[512,256]{1,0:T(8,128)(2,1)S(1)}, u32[]{:S(2)}, u32[]{:S(2)}) %collective-permute-start.1) | collective-permute-done | bytes 262176 | tf_op jit(solution)/shard_map/ppermute | solution.py:202
  18.8 0.3 col_pack.1
  19.1 1.9 %collective-permute-start.2 = (bf16[320,256]{1,0:T(8,128)(2,1)S(1)}, bf16[320,256]{1,0:T(8,128)(2,1)S(1)}, u32[]{:S(2)}, u32[]{:S(2)}) collective-permute-start(bf16[320,256]{1,0:T(8,128)(2,1)S(1)} %get-tuple-element.33), channel_id=1, source_target_pairs={{0,1},{1,0},{2,3},{3,2},{4,5},{5,4},{6,7},{7,6},{8,9},{9,8},{10,11... | collective-permute-start | bytes 491528 | tf_op jit(solution)/shard_map/ppermute | solution.py:202
  21.0 0.7 collective-permute-start.3
  21.7 3.5 %collective-permute-done.2.first_ref = bf16[320,256]{1,0:T(8,128)(2,1)S(1)} collective-permute-done((bf16[320,256]{1,0:T(8,128)(2,1)S(1)}, bf16[320,256]{1,0:T(8,128)(2,1)S(1)}, u32[]{:S(2)}, u32[]{:S(2)}) %collective-permute-start.2) | collective-permute-done | bytes 163872 | tf_op jit(solution)/shard_map/ppermute | solution.py:202
  25.1 0.0 collective-permute-done.3.second_ref
  25.2 0.0 copy-done.3
  25.2 0.0 copy-done
  25.2 0.0 copy-done.2
  25.2 0.0 copy-done.1
  25.2 8.2 %main.1 = (bf16[3,320,256]{2,1,0:T(8,128)(2,1)}, bf16[768,256]{1,0:T(8,128)(2,1)S(1)}, bf16[768,256]{1,0:T(8,128)(2,1)S(1)}, bf16[4160,256]{1,0:T(8,128)(2,1)S(1)}, bf16[1600,256]{1,0:T(8,128)(2,1)}) custom-call(bf16[1024,256]{1,0:T(8,128)(2,1)S(1)} %bitcast.7, bf16[256,256]{1,0:T(8,128)(2,1)S(1)} %bitcast.11, bf16[3,256,256]{2,1,0:T(8,128)(2,1)S(1)} %copy-done.1, ...), custom_call_target="tpu_custom_call" | custom-call | tf_op jit(solution)/shard_map/main/pallas_call | solution.py:548
  33.4 1.9 %collective-permute-start.4 = (bf16[768,256]{1,0:T(8,128)(2,1)S(1)}, bf16[768,256]{1,0:T(8,128)(2,1)S(1)}, u32[]{:S(2)}, u32[]{:S(2)}) collective-permute-start(bf16[768,256]{1,0:T(8,128)(2,1)S(1)} %get-tuple-element.37), channel_id=1, source_target_pairs={{0,32},{32,0},{1,33},{33,1},{2,34},{34,2},{3,35},{35,3},{4,36},{36... | collective-permute-start | bytes 1179656 | tf_op jit(solution)/shard_map/ppermute | solution.py:618
  35.4 1.7 %collective-permute-done.4 = bf16[768,256]{1,0:T(8,128)(2,1)S(1)} collective-permute-done((bf16[768,256]{1,0:T(8,128)(2,1)S(1)}, bf16[768,256]{1,0:T(8,128)(2,1)S(1)}, u32[]{:S(2)}, u32[]{:S(2)}) %collective-permute-start.4) | collective-permute-done | bytes 393248 | tf_op jit(solution)/shard_map/ppermute | solution.py:618
  37.0 0.1 add_convert_fusion
  37.2 23.8 %all_to_all.15 = bf16[32,24,256]{2,1,0:T(8,128)(2,1)S(1)} all-to-all(bf16[32,24,256]{2,1,0:T(8,128)(2,1)S(1)} %bitcast.12), channel_id=1, replica_groups=mesh['grp_0'=8,'grp_1'=2,'dev_0'=4,'dev_1'=8] {'dev_0','dev_1'}, dimensions={0} | all-to-all | bytes 786432 | tf_op jit(solution)/shard_map/all_to_all | solution.py:608
  60.9 0.1 reduce_sum.24
  61.0 15.9 %all_to_all.16 = bf16[8,24,256]{2,1,0:T(8,128)(2,1)S(1)} all-to-all(bf16[8,24,256]{2,1,0:T(8,128)(2,1)S(1)} %broadcast_in_dim.6), channel_id=1, replica_groups=mesh['grp_0'=8,'grp_1'=2,'dev_0'=4,'dev_1'=8] {'grp_0'}, dimensions={0} | all-to-all | bytes 196608 | tf_op jit(solution)/shard_map/all_to_all | solution.py:614
  77.0 0.8 broadcast_in_dim.7
  77.8 7.6 %all-to-all-start.2 = ((bf16[32,24,256]{2,1,0:T(8,128)(2,1)}), bf16[32,24,256]{2,1,0:T(8,128)(2,1)S(1)}, u32[]{:S(2)}, u32[]{:S(2)}) async-start(bf16[32,24,256]{2,1,0:T(8,128)(2,1)} %broadcast_in_dim.7), calls=%async_computation.2 | async-start | bytes 786432 | tf_op jit(solution)/shard_map/all_to_all | solution.py:614
  85.4 4.0 %tail.1 = (bf16[1024,256]{1,0:T(8,128)(2,1)}, bf16[256,256]{1,0:T(8,128)(2,1)}) custom-call(bf16[3,320,256]{2,1,0:T(8,128)(2,1)} %get-tuple-element.38.terms_ref, bf16[4160,256]{1,0:T(8,128)(2,1)S(1)} %get-tuple-element.39.table_ref, bf16[1600,256]{1,0:T(8,128)(2,1)} %get-tuple-element.40.grad_ref, bf16[3,256,256]{2,1,0:T(8,128)(2,1)S(1)} %copy-done.1, ...), custom_call_target="tpu_custom_call" | custom-call | tf_op jit(solution)/shard_map/tail/pallas_call | solution.py:591
  89.5 6.2 %all-to-all-done.2 = bf16[32,24,256]{2,1,0:T(8,128)(2,1)S(1)} async-done(((bf16[32,24,256]{2,1,0:T(8,128)(2,1)}), bf16[32,24,256]{2,1,0:T(8,128)(2,1)S(1)}, u32[]{:S(2)}, u32[]{:S(2)}) %all-to-all-start.2) | async-done | bytes 393248 | tf_op jit(solution)/shard_map/all_to_all | solution.py:614
  95.7 7.2 %collective-permute-start.5 = (bf16[768,256]{1,0:T(8,128)(2,1)S(1)}, bf16[768,256]{1,0:T(8,128)(2,1)S(1)}, u32[]{:S(2)}, u32[]{:S(2)}) collective-permute-start(bf16[768,256]{1,0:T(8,128)(2,1)S(1)} %bitcast.8), channel_id=1, source_target_pairs={{0,32},{32,0},{1,33},{33,1},{2,34},{34,2},{3,35},{35,3},{4,36},{36... | collective-permute-start | bytes 1179656 | tf_op jit(solution)/shard_map/ppermute | solution.py:618
  102.8 1.3 %collective-permute-done.5.other_ref = bf16[768,256]{1,0:T(8,128)(2,1)S(1)} collective-permute-done((bf16[768,256]{1,0:T(8,128)(2,1)S(1)}, bf16[768,256]{1,0:T(8,128)(2,1)S(1)}, u32[]{:S(2)}, u32[]{:S(2)}) %collective-permute-start.5) | collective-permute-done | bytes 393248 | tf_op jit(solution)/shard_map/ppermute | solution.py:618
  104.2 1.5 %clip.1 = (f32[3,256,256]{2,1,0:T(8,128)}, f32[3,256,256]{2,1,0:T(8,128)}) custom-call(bf16[768,256]{1,0:T(8,128)(2,1)S(1)} %bitcast.9, bf16[768,256]{1,0:T(8,128)(2,1)S(1)} %collective-permute-done.5.other_ref), custom_call_target="tpu_custom_call" | custom-call | tf_op jit(solution)/shard_map/clip/pallas_call | solution.py:646
  (2 shorter events, 0.0 us)
Async XLA Ops:
  0.6 24.5 %copy-start.3 = (bf16[8,32,256]{2,1,0:T(8,128)(2,1)S(1)}, bf16[8,32,256]{2,1,0:T(8,128)(2,1)}, u32[]{:S(2)}) copy-start(bf16[8,32,256]{2,1,0:T(8,128)(2,1)} %ct_rows.1) | copy-start | bytes 393220
  0.6 24.5 %copy-start = (bf16[16,64,256]{2,1,0:T(8,128)(2,1)S(1)}, bf16[16,64,256]{2,1,0:T(8,128)(2,1)}, u32[]{:S(2)}) copy-start(bf16[16,64,256]{2,1,0:T(8,128)(2,1)} %px_rows.1) | copy-start | bytes 1572868
  0.7 24.5 %copy-start.2 = (bf16[3,256,256]{2,1,0:T(8,128)(2,1)S(1)}, bf16[3,256,256]{2,1,0:T(8,128)(2,1)}, u32[]{:S(2)}) copy-start(bf16[3,256,256]{2,1,0:T(8,128)(2,1)} %w2_ref.1) | copy-start | bytes 1179652
  0.7 24.5 %copy-start.1 = (bf16[3,256,256]{2,1,0:T(8,128)(2,1)S(1)}, bf16[3,256,256]{2,1,0:T(8,128)(2,1)}, u32[]{:S(2)}) copy-start(bf16[3,256,256]{2,1,0:T(8,128)(2,1)} %w_ref.1) | copy-start | bytes 1179652
  2.1 10.7 %collective-permute-start = (bf16[512,256]{1,0:T(8,128)(2,1)S(1)}, bf16[512,256]{1,0:T(8,128)(2,1)S(1)}, u32[]{:S(2)}, u32[]{:S(2)}) collective-permute-start(bf16[512,256]{1,0:T(8,128)(2,1)S(1)} %get-tuple-element.31), channel_id=1, source_target_pairs={{0,32},{32,0},{64,96},{96,64},{128,160},{160,128},{192,224},{224,1... | collective-permute-start | bytes 786440 | tf_op jit(solution)/shard_map/ppermute | solution.py:202
  10.8 8.0 %collective-permute-start.1 = (bf16[512,256]{1,0:T(8,128)(2,1)S(1)}, bf16[512,256]{1,0:T(8,128)(2,1)S(1)}, u32[]{:S(2)}, u32[]{:S(2)}) collective-permute-start(bf16[512,256]{1,0:T(8,128)(2,1)S(1)} %get-tuple-element.32), channel_id=1, source_target_pairs={{32,64},{64,32},{96,128},{128,96},{160,192},{192,160},{224,256},{2... | collective-permute-start | bytes 786440 | tf_op jit(solution)/shard_map/ppermute | solution.py:202
  19.1 6.1 %collective-permute-start.2 = (bf16[320,256]{1,0:T(8,128)(2,1)S(1)}, bf16[320,256]{1,0:T(8,128)(2,1)S(1)}, u32[]{:S(2)}, u32[]{:S(2)}) collective-permute-start(bf16[320,256]{1,0:T(8,128)(2,1)S(1)} %get-tuple-element.33), channel_id=1, source_target_pairs={{0,1},{1,0},{2,3},{3,2},{4,5},{5,4},{6,7},{7,6},{8,9},{9,8},{10,11... | collective-permute-start | bytes 491528 | tf_op jit(solution)/shard_map/ppermute | solution.py:202
  21.0 4.1 %collective-permute-start.3 = (bf16[320,256]{1,0:T(8,128)(2,1)S(1)}, bf16[320,256]{1,0:T(8,128)(2,1)S(1)}, u32[]{:S(2)}, u32[]{:S(2)}) collective-permute-start(bf16[320,256]{1,0:T(8,128)(2,1)S(1)} %get-tuple-element.34), channel_id=1, source_target_pairs={{1,2},{2,1},{3,4},{4,3},{5,6},{6,5},{7,8},{8,7},{9,10},{10,9},{11,... | collective-permute-start | bytes 491528 | tf_op jit(solution)/shard_map/ppermute | solution.py:202
  33.4 3.6 %collective-permute-start.4 = (bf16[768,256]{1,0:T(8,128)(2,1)S(1)}, bf16[768,256]{1,0:T(8,128)(2,1)S(1)}, u32[]{:S(2)}, u32[]{:S(2)}) collective-permute-start(bf16[768,256]{1,0:T(8,128)(2,1)S(1)} %get-tuple-element.37), channel_id=1, source_target_pairs={{0,32},{32,0},{1,33},{33,1},{2,34},{34,2},{3,35},{35,3},{4,36},{36... | collective-permute-start | bytes 1179656 | tf_op jit(solution)/shard_map/ppermute | solution.py:618
  77.8 17.9 %all-to-all-start.2 = ((bf16[32,24,256]{2,1,0:T(8,128)(2,1)}), bf16[32,24,256]{2,1,0:T(8,128)(2,1)S(1)}, u32[]{:S(2)}, u32[]{:S(2)}) async-start(bf16[32,24,256]{2,1,0:T(8,128)(2,1)} %broadcast_in_dim.7), calls=%async_computation.2 | async-start | bytes 786432 | tf_op jit(solution)/shard_map/all_to_all | solution.py:614
  95.7 8.5 %collective-permute-start.5 = (bf16[768,256]{1,0:T(8,128)(2,1)S(1)}, bf16[768,256]{1,0:T(8,128)(2,1)S(1)}, u32[]{:S(2)}, u32[]{:S(2)}) collective-permute-start(bf16[768,256]{1,0:T(8,128)(2,1)S(1)} %bitcast.8), channel_id=1, source_target_pairs={{0,32},{32,0},{1,33},{33,1},{2,34},{34,2},{3,35},{35,3},{4,36},{36... | collective-permute-start | bytes 1179656 | tf_op jit(solution)/shard_map/ppermute | solution.py:618

commit v6 on v4

--- a/solution.py
+++ b/solution.py
@@ -47,10 +47,10 @@
 
 ROW_CT = HR * C
 ROW_OFF = ROW_CT + 3 * PC
-ROW_END = ROW_OFF + 32
-COL_CT = ER * HC
+ROW_END = ROW_OFF + 16
+COL_CT = ER * 6 + 8
 COL_OFF = COL_CT + 64
-COL_END = COL_OFF + OR
+COL_END = COL_OFF + OR // 2
 
 
 def on_chip(*arrays):
@@ -97,7 +97,7 @@
     wide[:, 0:C] = off_buf[...]
     for out, off_at in ((up_ref, 0), (down_ref, R - 8)):
         high, middle, low = in_parts(wide[off_at : off_at + 8, :])
-        packed = jnp.concatenate([high, middle, low, jnp.zeros_like(low)], 0)
+        packed = jnp.concatenate([high + rolled(middle, C, 1), low], 0)
         out[ROW_OFF:ROW_END, :] = jnp.concatenate([packed, jnp.zeros_like(packed)], 1).astype(BF)
     for copy in copies[1:]:
         copy.wait()
@@ -124,7 +124,8 @@
 
 def row_offsets(ref):
     parts = ref[ROW_OFF:ROW_END, 0:128].astype(F32)
-    return parts[0:8] + parts[8:16] + parts[16:24]
+    whole = parts[0:8] + rolled(parts[0:8], C, 1) + parts[8:16]
+    return jnp.where(lax.broadcasted_iota(jnp.int32, (8, 128), 1) < C, whole, 0.0)
 
 
 def col_pack_kernel(*refs):
@@ -133,7 +134,8 @@
     wide[0:8, :] = row_offsets(above_ref)
     wide[8 + R : OR, :] = row_offsets(below_ref)
     lane = lax.broadcasted_iota(jnp.int32, (OR, 128), 1)
-    near = lax.broadcasted_iota(jnp.int32, (8, F), 0) < 4
+    row = lax.broadcasted_iota(jnp.int32, (8, F), 0)
+    near = row < 4
     for out, px_ref, ct_ref, px_at, ct_at, half in (
         (left_ref, pxl_ref, ctl_ref, 0, 0, slice(0, 8)),
         (right_ref, pxr_ref, ctr_ref, C - 16, PC - 16, slice(8, 16)),
@@ -144,11 +146,20 @@
                 return ref[base + k * width + at : base + k * width + at + 16, :].astype(F32)[half]
             return ref[k].astype(F32)[half]
 
-        for first, n, ref in ((0, HR, above_ref), (HR, R, px_ref), (HR + R, HR, below_ref)):
-            for r in range(0, n, 2):
-                tiles = [line(ref, k, 0, C, px_at) for k in (r, r + 1)]
-                at = (first + r) * HC
-                out[at : at + 16, :] = jnp.concatenate(tiles, 0).astype(BF)
+        lines = []
+        for n, ref in ((HR, above_ref), (R, px_ref), (HR, below_ref)):
+            for k in range(n):
+                one = line(ref, k, 0, C, px_at)
+                lines.append(one if out is left_ref else rolled(one, -2, 0))
+        tiles = []
+        for e in range(0, ER, 4):
+            one, two, three, four = lines[e : e + 4]
+            tiles.append(jnp.where(row < 6, one, rolled(two, 6, 0)))
+            tiles.append(jnp.where(row < 4, rolled(two, -2, 0), rolled(three, 4, 0)))
+            tiles.append(jnp.where(row < 2, rolled(three, -4, 0), rolled(four, 2, 0)))
+        tiles.append(jnp.zeros((8, F), F32))
+        for e in range(0, len(tiles), 2):
+            out[e * 8 : e * 8 + 16, :] = jnp.concatenate(tiles[e : e + 2], 0).astype(BF)
         lines = []
         for n, ref in ((3, above_ref), (PR, ct_ref), (3, below_ref)):
             lines += [line(ref, k, ROW_CT, PC, ct_at) for k in range(n)]
@@ -165,6 +176,7 @@
         part = wide[...] if out is left_ref else rolled(wide[...], HC - C, 1)
         high, middle, low = in_parts(jnp.where(lane < HC, part, 0.0))
         packed = high + rolled(middle, HC, 1) + rolled(low, 2 * HC, 1)
+        packed = packed[0 : OR // 2] + rolled(packed[OR // 2 :], 32, 1)
         out[COL_OFF:COL_END, :] = jnp.concatenate([packed, jnp.zeros_like(packed)], 1).astype(BF)
 
 
@@ -252,7 +264,7 @@
     (h_ref, hw_ref, pick_ref, phw_ref, psw_ref, pxe_ref, f1_ref, f2_ref, f1c_ref, f2c_ref, slope_ref, hid_ref,
      poolf_ref, p1f_ref, p2f_ref, ctf_ref, ptab_ref, pb_ref, p1b_ref, ctb_ref, topb_ref,
      midf_ref, midb_ref, pgf_ref, sp_ref, agc_ref, halves_ref, px_ref, ct_ref, w1_ref, w2_ref,
-     terms_ref, grad_ref, pxt_ref, f1t_ref, f2t_ref, sems, out_sems) = rest[5:]
+     terms_ref, grad_ref, pxt_ref, f1t_ref, f2t_ref, strip_ref, sems, out_sems) = rest[5:]
     copies = started(
         sems, [(px_hbm, px_ref), (ct_hbm, ct_ref), (w1_hbm, w1_ref), (w2_hbm, w2_ref)]
     )
@@ -269,6 +281,7 @@
 
     def col_offsets(ref):
         parts = ref[COL_OFF:COL_END, 0:128].astype(F32)
+        parts = jnp.concatenate([parts, rolled(parts, -32, 1)], 0)
         whole = parts + rolled(parts, -HC, 1) + rolled(parts, -2 * HC, 1)
         return jnp.where(lax.broadcasted_iota(jnp.int32, (OR, 128), 1) < HC, whole, 0.0)
 
@@ -354,12 +367,18 @@
 
     copies[0].wait()
     copies[1].wait()
+    for n, ref in enumerate((left_ref, right_ref)):
+        strip_ref[n, 0:8, :] = jnp.zeros((8, F), F32)
+        strip_ref[n, 8 : 8 + COL_CT, :] = ref[0:COL_CT, :].astype(F32)
     for at, n, ref in ((0, HR, above_ref), (HR, R, px_ref), (HR + R, HR, below_ref)):
         for r in range(0, n, 2):
-            side = slice((at + r) * HC, (at + r + 2) * HC)
-            left, right = left_ref[side, :].astype(F32), right_ref[side, :].astype(F32)
             middle = ref[r * C : (r + 2) * C, :].astype(F32)
-            lines = [left[0:8], middle[0:C], right[0:8], left[8:16], middle[C:], right[8:16]]
+            lines = []
+            for k in (0, 1):
+                e = 8 + (at + r + k) * 6
+                lines.append(strip_ref[0, e - 2 : e + 6, :])
+                lines.append(middle[k * C : (k + 1) * C])
+                lines.append(strip_ref[1, e : e + 8, :])
             row = (at + r) * EC
             pxe_ref[row : row + 2 * EC, :] = jnp.concatenate(lines, 0).astype(BF)
 
@@ -522,6 +541,7 @@
         ((F, R * C), BF),
         ((F, R * C), BF),
         ((F, R * C), BF),
+        ((2, 8 + COL_CT, F), F32),
     ]
     return pl.pallas_call(
         main_kernel,

time: 106 us -> 105 us (level)
  no operation moved by 1% of the time
where the time goes in v6:
time: 105 us
  blocking collectives  38.9 us (37%)
  starting transfers between devices  32 us (30%)
  waiting for transfers between devices  16.4 us (16%)
  Pallas kernels  15.5 us (15%)
    all_to_all x1, blocking collectives, sum_at_owner(): lax.all_to_all(value.reshape(lax.axis_size(axes), -1, F), axes, 0, 0, til...  24.2 us
    all_to_all x1, blocking collectives, sent_to_all(): return lax.all_to_all(copies, axes, 0, 0, tiled=True)  14.7 us
    ppermute x2, starting transfers between devices, swapped(): return lax.ppermute(value, 'grp_1', [(0, 1), (1, 0)])  9.07 us
    ppermute x2, starting transfers between devices, exchanged(): lax.ppermute(last, axis, forward)  8.58 us
    pallas_call x1, Pallas kernels, main_stage(): pl.pallas_call(main_kernel, out_shape=[pltpu.HBM((3, PR * QC, F), BF), pl...  8.29 us
    all_to_all x1, starting transfers between devices, sent_to_all(): return lax.all_to_all(copies, axes, 0, 0, tiled=True)  7.64 us
    ppermute x2, starting transfers between devices, exchanged(): lax.ppermute(first, axis, backward)  6.76 us
    ppermute x2, waiting for transfers between devices, exchanged(): lax.ppermute(first, axis, backward)  6.54 us
  transfers between devices with their start and end apart: 7, of which 6 were waited for; matrix products, arithmetic and copies ran while one was open for 0% of the time, Pallas kernels for 4%

profile of v6, /device:TPU:1, one launch (start us, length us, event | category | flops | bytes accessed | tf_op | source)
XLA Modules:
  0.0 104.7 jit_solution(4346233238040455794)
XLA Ops:
  0.6 0.0 copy-start.3
  0.6 0.0 copy-start
  0.7 0.0 copy-start.2
  0.7 0.0 copy-start.1
  0.7 1.4 %row_pack.1 = (bf16[496,256]{1,0:T(8,128)(2,1)S(1)}, bf16[496,256]{1,0:T(8,128)(2,1)S(1)}, bf16[16,16,256]{2,1,0:T(8,128)(2,1)S(1)}, bf16[16,16,256]{2,1,0:T(8,1...) custom-call(bf16[1024,256]{1,0:T(8,128)(2,1)} %bitcast.6, ...), custom_call_target="tpu_custom_call" | custom-call | tf_op jit(solution)/shard_map/row_pack/pallas_call | solution.py:107
  2.1 4.6 %collective-permute-start = (bf16[496,256]{1,0:T(8,128)(2,1)S(1)}, bf16[496,256]{1,0:T(8,128)(2,1)S(1)}, u32[]{:S(2)}, u32[]{:S(2)}) collective-permute-start(bf16[496,256]{1,0:T(8,128)(2,1)S(1)} %get-tuple-element.26), channel_id=1, source_target_pairs={{0,32},{32,64},{64,96},{96,128},{128,160},{160,192},{192,224},{224... | collective-permute-start | bytes 761864 | tf_op jit(solution)/shard_map/ppermute | solution.py:198
  6.7 5.5 %collective-permute-start.1 = (bf16[496,256]{1,0:T(8,128)(2,1)S(1)}, bf16[496,256]{1,0:T(8,128)(2,1)S(1)}, u32[]{:S(2)}, u32[]{:S(2)}) collective-permute-start(bf16[496,256]{1,0:T(8,128)(2,1)S(1)} %get-tuple-element.27), channel_id=1, source_target_pairs={{32,0},{64,32},{96,64},{128,96},{160,128},{192,160},{224,192},{256... | collective-permute-start | bytes 761864 | tf_op jit(solution)/shard_map/ppermute | solution.py:198
  12.2 0.0 collective-permute-done.refs_5_.above_ref
  12.2 2.1 %collective-permute-done.1.refs_6_.below_ref = bf16[496,256]{1,0:T(8,128)(2,1)S(1)} collective-permute-done((bf16[496,256]{1,0:T(8,128)(2,1)S(1)}, bf16[496,256]{1,0:T(8,128)(2,1)S(1)}, u32[]{:S(2)}, u32[]{:S(2)}) %collective-permute-start.1) | collective-permute-done | bytes 253984 | tf_op jit(solution)/shard_map/ppermute | solution.py:198
  14.3 0.3 col_pack.1
  14.6 4.0 %collective-permute-start.2 = (bf16[256,256]{1,0:T(8,128)(2,1)S(1)}, bf16[256,256]{1,0:T(8,128)(2,1)S(1)}, u32[]{:S(2)}, u32[]{:S(2)}) collective-permute-start(bf16[256,256]{1,0:T(8,128)(2,1)S(1)} %get-tuple-element.32), channel_id=1, source_target_pairs={{0,1},{1,2},{2,3},{3,4},{4,5},{5,6},{6,7},{7,8},{8,9},{9,10},{10,1... | collective-permute-start | bytes 393224 | tf_op jit(solution)/shard_map/ppermute | solution.py:198
  18.6 1.3 %collective-permute-start.3 = (bf16[256,256]{1,0:T(8,128)(2,1)S(1)}, bf16[256,256]{1,0:T(8,128)(2,1)S(1)}, u32[]{:S(2)}, u32[]{:S(2)}) collective-permute-start(bf16[256,256]{1,0:T(8,128)(2,1)S(1)} %get-tuple-element.33), channel_id=1, source_target_pairs={{1,0},{2,1},{3,2},{4,3},{5,4},{6,5},{7,6},{8,7},{9,8},{10,9},{11,1... | collective-permute-start | bytes 393224 | tf_op jit(solution)/shard_map/ppermute | solution.py:198
  19.9 0.6 collective-permute-done.2.left_ref
  20.5 4.4 %collective-permute-done.3.right_ref = bf16[256,256]{1,0:T(8,128)(2,1)S(1)} collective-permute-done((bf16[256,256]{1,0:T(8,128)(2,1)S(1)}, bf16[256,256]{1,0:T(8,128)(2,1)S(1)}, u32[]{:S(2)}, u32[]{:S(2)}) %collective-permute-start.3) | collective-permute-done | bytes 131104 | tf_op jit(solution)/shard_map/ppermute | solution.py:198
  24.9 0.0 copy-done.3
  24.9 0.0 copy-done
  24.9 0.0 copy-done.2
  24.9 0.0 copy-done.1
  24.9 8.3 %main.1 = (bf16[3,320,256]{2,1,0:T(8,128)(2,1)}, bf16[768,256]{1,0:T(8,128)(2,1)S(1)}, bf16[768,256]{1,0:T(8,128)(2,1)S(1)}, bf16[4160,256]{1,0:T(8,128)(2,1)S(1)}, bf16[1600,256]{1,0:T(8,128)(2,1)}) custom-call(bf16[1024,256]{1,0:T(8,128)(2,1)S(1)} %bitcast.7, bf16[256,256]{1,0:T(8,128)(2,1)S(1)} %bitcast.11, bf16[3,256,256]{2,1,0:T(8,128)(2,1)S(1)} %copy-done.1, ...), custom_call_target="tpu_custom_call" | custom-call | tf_op jit(solution)/shard_map/main/pallas_call | solution.py:546
  33.2 1.9 %collective-permute-start.4 = (bf16[768,256]{1,0:T(8,128)(2,1)S(1)}, bf16[768,256]{1,0:T(8,128)(2,1)S(1)}, u32[]{:S(2)}, u32[]{:S(2)}) collective-permute-start(bf16[768,256]{1,0:T(8,128)(2,1)S(1)} %get-tuple-element.35), channel_id=1, source_target_pairs={{0,32},{32,0},{1,33},{33,1},{2,34},{34,2},{3,35},{35,3},{4,36},{36... | collective-permute-start | bytes 1179656 | tf_op jit(solution)/shard_map/ppermute | solution.py:616
  35.2 1.7 %collective-permute-done.4 = bf16[768,256]{1,0:T(8,128)(2,1)S(1)} collective-permute-done((bf16[768,256]{1,0:T(8,128)(2,1)S(1)}, bf16[768,256]{1,0:T(8,128)(2,1)S(1)}, u32[]{:S(2)}, u32[]{:S(2)}) %collective-permute-start.4) | collective-permute-done | bytes 393248 | tf_op jit(solution)/shard_map/ppermute | solution.py:616
  36.9 0.1 add_convert_fusion
  37.0 24.2 %all_to_all.15 = bf16[32,24,256]{2,1,0:T(8,128)(2,1)S(1)} all-to-all(bf16[32,24,256]{2,1,0:T(8,128)(2,1)S(1)} %bitcast.12), channel_id=1, replica_groups=mesh['grp_0'=8,'grp_1'=2,'dev_0'=4,'dev_1'=8] {'dev_0','dev_1'}, dimensions={0} | all-to-all | bytes 786432 | tf_op jit(solution)/shard_map/all_to_all | solution.py:606
  61.2 0.1 reduce_sum.24
  61.3 14.7 %all_to_all.16 = bf16[8,24,256]{2,1,0:T(8,128)(2,1)S(1)} all-to-all(bf16[8,24,256]{2,1,0:T(8,128)(2,1)S(1)} %broadcast_in_dim.6), channel_id=1, replica_groups=mesh['grp_0'=8,'grp_1'=2,'dev_0'=4,'dev_1'=8] {'grp_0'}, dimensions={0} | all-to-all | bytes 196608 | tf_op jit(solution)/shard_map/all_to_all | solution.py:612
  76.0 0.8 broadcast_in_dim.7
  76.8 7.6 %all-to-all-start.2 = ((bf16[32,24,256]{2,1,0:T(8,128)(2,1)}), bf16[32,24,256]{2,1,0:T(8,128)(2,1)S(1)}, u32[]{:S(2)}, u32[]{:S(2)}) async-start(bf16[32,24,256]{2,1,0:T(8,128)(2,1)} %broadcast_in_dim.7), calls=%async_computation.2 | async-start | bytes 786432 | tf_op jit(solution)/shard_map/all_to_all | solution.py:612
  84.4 4.0 %tail.1 = (bf16[1024,256]{1,0:T(8,128)(2,1)}, bf16[256,256]{1,0:T(8,128)(2,1)}) custom-call(bf16[3,320,256]{2,1,0:T(8,128)(2,1)} %get-tuple-element.36.terms_ref, bf16[4160,256]{1,0:T(8,128)(2,1)S(1)} %get-tuple-element.37.table_ref, bf16[1600,256]{1,0:T(8,128)(2,1)} %get-tuple-element.38.grad_ref, bf16[3,256,256]{2,1,0:T(8,128)(2,1)S(1)} %copy-done.1, ...), custom_call_target="tpu_custom_call" | custom-call | tf_op jit(solution)/shard_map/tail/pallas_call | solution.py:589
  88.5 6.2 %all-to-all-done.2 = bf16[32,24,256]{2,1,0:T(8,128)(2,1)S(1)} async-done(((bf16[32,24,256]{2,1,0:T(8,128)(2,1)}), bf16[32,24,256]{2,1,0:T(8,128)(2,1)S(1)}, u32[]{:S(2)}, u32[]{:S(2)}) %all-to-all-start.2) | async-done | bytes 393248 | tf_op jit(solution)/shard_map/all_to_all | solution.py:612
  94.7 7.2 %collective-permute-start.5 = (bf16[768,256]{1,0:T(8,128)(2,1)S(1)}, bf16[768,256]{1,0:T(8,128)(2,1)S(1)}, u32[]{:S(2)}, u32[]{:S(2)}) collective-permute-start(bf16[768,256]{1,0:T(8,128)(2,1)S(1)} %bitcast.8), channel_id=1, source_target_pairs={{0,32},{32,0},{1,33},{33,1},{2,34},{34,2},{3,35},{35,3},{4,36},{36... | collective-permute-start | bytes 1179656 | tf_op jit(solution)/shard_map/ppermute | solution.py:616
  101.8 1.3 %collective-permute-done.5.other_ref = bf16[768,256]{1,0:T(8,128)(2,1)S(1)} collective-permute-done((bf16[768,256]{1,0:T(8,128)(2,1)S(1)}, bf16[768,256]{1,0:T(8,128)(2,1)S(1)}, u32[]{:S(2)}, u32[]{:S(2)}) %collective-permute-start.5) | collective-permute-done | bytes 393248 | tf_op jit(solution)/shard_map/ppermute | solution.py:616
  103.2 1.5 %clip.1 = (f32[3,256,256]{2,1,0:T(8,128)}, f32[3,256,256]{2,1,0:T(8,128)}) custom-call(bf16[768,256]{1,0:T(8,128)(2,1)S(1)} %bitcast.9, bf16[768,256]{1,0:T(8,128)(2,1)S(1)} %collective-permute-done.5.other_ref), custom_call_target="tpu_custom_call" | custom-call | tf_op jit(solution)/shard_map/clip/pallas_call | solution.py:644
  (2 shorter events, 0.0 us)
Async XLA Ops:
  0.6 24.3 %copy-start.3 = (bf16[8,32,256]{2,1,0:T(8,128)(2,1)S(1)}, bf16[8,32,256]{2,1,0:T(8,128)(2,1)}, u32[]{:S(2)}) copy-start(bf16[8,32,256]{2,1,0:T(8,128)(2,1)} %ct_rows.1) | copy-start | bytes 393220
  0.6 24.3 %copy-start = (bf16[16,64,256]{2,1,0:T(8,128)(2,1)S(1)}, bf16[16,64,256]{2,1,0:T(8,128)(2,1)}, u32[]{:S(2)}) copy-start(bf16[16,64,256]{2,1,0:T(8,128)(2,1)} %px_rows.1) | copy-start | bytes 1572868
  0.7 24.3 %copy-start.2 = (bf16[3,256,256]{2,1,0:T(8,128)(2,1)S(1)}, bf16[3,256,256]{2,1,0:T(8,128)(2,1)}, u32[]{:S(2)}) copy-start(bf16[3,256,256]{2,1,0:T(8,128)(2,1)} %w2_ref.1) | copy-start | bytes 1179652
  0.7 24.3 %copy-start.1 = (bf16[3,256,256]{2,1,0:T(8,128)(2,1)S(1)}, bf16[3,256,256]{2,1,0:T(8,128)(2,1)}, u32[]{:S(2)}) copy-start(bf16[3,256,256]{2,1,0:T(8,128)(2,1)} %w_ref.1) | copy-start | bytes 1179652
  2.1 10.1 %collective-permute-start = (bf16[496,256]{1,0:T(8,128)(2,1)S(1)}, bf16[496,256]{1,0:T(8,128)(2,1)S(1)}, u32[]{:S(2)}, u32[]{:S(2)}) collective-permute-start(bf16[496,256]{1,0:T(8,128)(2,1)S(1)} %get-tuple-element.26), channel_id=1, source_target_pairs={{0,32},{32,64},{64,96},{96,128},{128,160},{160,192},{192,224},{224... | collective-permute-start | bytes 761864 | tf_op jit(solution)/shard_map/ppermute | solution.py:198
  6.7 7.6 %collective-permute-start.1 = (bf16[496,256]{1,0:T(8,128)(2,1)S(1)}, bf16[496,256]{1,0:T(8,128)(2,1)S(1)}, u32[]{:S(2)}, u32[]{:S(2)}) collective-permute-start(bf16[496,256]{1,0:T(8,128)(2,1)S(1)} %get-tuple-element.27), channel_id=1, source_target_pairs={{32,0},{64,32},{96,64},{128,96},{160,128},{192,160},{224,192},{256... | collective-permute-start | bytes 761864 | tf_op jit(solution)/shard_map/ppermute | solution.py:198
  14.6 5.9 %collective-permute-start.2 = (bf16[256,256]{1,0:T(8,128)(2,1)S(1)}, bf16[256,256]{1,0:T(8,128)(2,1)S(1)}, u32[]{:S(2)}, u32[]{:S(2)}) collective-permute-start(bf16[256,256]{1,0:T(8,128)(2,1)S(1)} %get-tuple-element.32), channel_id=1, source_target_pairs={{0,1},{1,2},{2,3},{3,4},{4,5},{5,6},{6,7},{7,8},{8,9},{9,10},{10,1... | collective-permute-start | bytes 393224 | tf_op jit(solution)/shard_map/ppermute | solution.py:198
  18.6 6.3 %collective-permute-start.3 = (bf16[256,256]{1,0:T(8,128)(2,1)S(1)}, bf16[256,256]{1,0:T(8,128)(2,1)S(1)}, u32[]{:S(2)}, u32[]{:S(2)}) collective-permute-start(bf16[256,256]{1,0:T(8,128)(2,1)S(1)} %get-tuple-element.33), channel_id=1, source_target_pairs={{1,0},{2,1},{3,2},{4,3},{5,4},{6,5},{7,6},{8,7},{9,8},{10,9},{11,1... | collective-permute-start | bytes 393224 | tf_op jit(solution)/shard_map/ppermute | solution.py:198
  33.2 3.6 %collective-permute-start.4 = (bf16[768,256]{1,0:T(8,128)(2,1)S(1)}, bf16[768,256]{1,0:T(8,128)(2,1)S(1)}, u32[]{:S(2)}, u32[]{:S(2)}) collective-permute-start(bf16[768,256]{1,0:T(8,128)(2,1)S(1)} %get-tuple-element.35), channel_id=1, source_target_pairs={{0,32},{32,0},{1,33},{33,1},{2,34},{34,2},{3,35},{35,3},{4,36},{36... | collective-permute-start | bytes 1179656 | tf_op jit(solution)/shard_map/ppermute | solution.py:616
  76.8 17.9 %all-to-all-start.2 = ((bf16[32,24,256]{2,1,0:T(8,128)(2,1)}), bf16[32,24,256]{2,1,0:T(8,128)(2,1)S(1)}, u32[]{:S(2)}, u32[]{:S(2)}) async-start(bf16[32,24,256]{2,1,0:T(8,128)(2,1)} %broadcast_in_dim.7), calls=%async_computation.2 | async-start | bytes 786432 | tf_op jit(solution)/shard_map/all_to_all | solution.py:612
  94.7 8.5 %collective-permute-start.5 = (bf16[768,256]{1,0:T(8,128)(2,1)S(1)}, bf16[768,256]{1,0:T(8,128)(2,1)S(1)}, u32[]{:S(2)}, u32[]{:S(2)}) collective-permute-start(bf16[768,256]{1,0:T(8,128)(2,1)S(1)} %bitcast.8), channel_id=1, source_target_pairs={{0,32},{32,0},{1,33},{33,1},{2,34},{34,2},{3,35},{35,3},{4,36},{36... | collective-permute-start | bytes 1179656 | tf_op jit(solution)/shard_map/ppermute | solution.py:616
